TPU v7x, 32 devices: a whole 2x2x4 slice. The times are simulated.
32 devices in a mesh: parts: 1, sens: 32 (over z, y, x, core).
Axes of the slice: x: 2, y: 2, z: 4, core: 2. Of those that a mesh axis runs over, the one named last changes fastest.
Arguments:
- data: bfloat16 [5120, 2048], P(('parts', 'sens'))
- templates: bfloat16 [1024, 16, 256], P('sens')
- cover: int32 [1024, 16], P('sens'), may hold values from 0 to 31, all different within a row; in each aligned block of 32 rows (0 to 31, 32 to 63, ...) at most 20 rows name the same one
- channel: int32 [1024, 16], P('sens'), may hold values from 0 to 63
Outputs:
- stacked: float32 [1024, 4864], P(('parts', 'sens'))
Inputs may be any that keep to these rules, and one draw needn't show every extreme that they name: `cover`: each row names 16 different sensor groups. Within the 32 rows of one device no group is named by more than 20 rows, a bound that some of them reach.
All inputs are finite; a program needn't handle non-finite values.
Results may differ from a plain program's by a relative error of at most 0.0003.
Values may be sent and summed in bfloat16 or wider, within the bound.
No kernel may reach another device: no remote copies, remote signals or barrier semaphores. Data moves between devices by JAX's collectives and lax.ppermute only.
A program may use at most 128 MiB of HBM per device.

v0:
```python
import math

import jax
import jax.numpy as jnp
from jax import lax
from jax.experimental import pallas as pl
from jax.experimental.pallas import tpu as pltpu
from jax.sharding import PartitionSpec as P

EPSILON = 1e-05
LANES = 128
HALF = 64
ROWS = 16
GROUP = 8


def prepare_tables(main_ref, halo_ref, slab, fa, fb, sem, r_ref, g_ref, block, length):
    total = block + length
    strips = main_ref.shape[1] // LANES
    row_count = total // LANES
    lag_rows = block // LANES
    zero_tile = jnp.zeros((LANES, LANES), jnp.float32)
    zero_half = jnp.zeros((HALF, LANES), jnp.float32)

    def copies(strip, slot):
        cols = pl.ds(pl.multiple_of(strip * LANES, LANES), LANES)
        return (
            pltpu.make_async_copy(main_ref.at[:, cols], slab.at[slot, pl.ds(0, block)], sem.at[slot, 0]),
            pltpu.make_async_copy(
                halo_ref.at[:, cols], slab.at[slot, pl.ds(block, length)], sem.at[slot, 1]
            ),
        )

    def windowed(source, target, offsets, count):
        for start in range(0, count, HALF):
            value = source[start : start + HALF, :]
            for offset in offsets:
                value = value + source[start + offset : start + offset + HALF, :]
            target[start : start + HALF, :] = value

    for copy in copies(0, 0):
        copy.start()

    def step(strip, carry):
        slot = lax.rem(strip, 2)

        @pl.when(strip + 1 < strips)
        def _():
            for copy in copies(strip + 1, 1 - slot):
                copy.start()

        for copy in copies(strip, slot):
            copy.wait()
        base = pl.multiple_of(strip * LANES * ROWS, LANES * ROWS)

        def rows(index):
            return pl.ds(base + index, LANES, stride=ROWS)

        for q in range(row_count):
            tile = slab[slot, LANES * q : LANES * (q + 1), :].astype(jnp.float32)
            fa[LANES * q : LANES * (q + 1), :] = tile * tile * 0.5
            r_ref[rows(q), :] = tile.T
        for q in range(row_count, ROWS):
            r_ref[rows(q), :] = zero_tile
        windowed(fa, fb, (1, 2, 3), total)
        windowed(fb, fa, (4,), total)
        windowed(fa, fb, (8, 16, 24), total)
        windowed(fb, fa, (32, 64, 96), total - LANES)
        for start in range(0, block, LANES):
            energy_half = fa[start : start + LANES, :] + fa[start + LANES : start + 2 * LANES, :]
            fb[start : start + LANES, :] = lax.rsqrt(energy_half * (2.0 / length) + EPSILON)

        def half_block(index):
            if 0 <= index < 2 * lag_rows:
                return fb[HALF * index : HALF * (index + 1), :]
            return zero_half

        for parity in range(2):
            for q in range(lag_rows + 1 - parity):
                pair = (half_block(2 * q + parity), half_block(2 * q + parity - 1))
                g_ref[parity, rows(1 + q), :] = jnp.concatenate(pair, axis=0).T
        return carry

    lax.fori_loop(0, strips, step, 0)


def stack_templates(sensor, scale, x_ref, r_ref, g_ref, o_ref, sc, chan_count, lag_rows):
    shift = lax.broadcasted_iota(jnp.int32, (HALF, LANES), 0) + 1
    lane = lax.broadcasted_iota(jnp.int32, (HALF, LANES), 1)
    upper = (lane < HALF) & (lane >= shift)
    zero = jnp.zeros((HALF, LANES), jnp.float32)
    zero_narrow = jnp.zeros((HALF, LANES), jnp.bfloat16)
    low = lax.broadcasted_iota(jnp.int32, (ROWS, LANES), 1) < HALF
    low_out = lax.broadcasted_iota(jnp.int32, (lag_rows, LANES), 1) < HALF

    def one(k, carry):
        first = [jnp.zeros((ROWS, LANES), jnp.float32) for _ in range(2)]
        second = [jnp.zeros((ROWS, LANES), jnp.float32) for _ in range(2)]
        for c in range(chan_count):
            item = k * chan_count + c
            factor = scale[item]
            base = pl.multiple_of(sensor[item] * ROWS, ROWS)
            here = r_ref[pl.ds(base, ROWS), :]
            later = r_ref[pl.ds(base + 2, ROWS), :]
            even = jnp.where(low, here, pltpu.roll(later, HALF, 1))
            odd = jnp.where(low, pltpu.roll(here, HALF, 1), later)
            windows = jnp.concatenate([even, odd], axis=0).astype(jnp.bfloat16)
            lead = jnp.broadcast_to(x_ref[k, 2 * c : 2 * c + 1, :], (HALF, LANES))
            tail = jnp.broadcast_to(x_ref[k, 2 * c + 1 : 2 * c + 2, :], (HALF, LANES))
            lead = pltpu.roll(lead, 1, 1, stride=1, stride_axis=0)
            tail = pltpu.roll(tail, 1, 1, stride=1, stride_axis=0)
            t01 = jnp.where(upper, zero, lead).astype(jnp.bfloat16)
            t23 = jnp.where(upper, lead, tail).astype(jnp.bfloat16)
            t4 = jnp.where(upper, tail, zero).astype(jnp.bfloat16)
            taps = jnp.concatenate(
                [
                    jnp.concatenate([t01, t23], axis=1),
                    jnp.concatenate([t4, zero_narrow], axis=1),
                ],
                axis=0,
            )
            corr = lax.dot_general(
                windows, taps, (((1,), (0,)), ((), ())), preferred_element_type=jnp.float32
            )
            for p in range(2):
                part = corr[ROWS * p : ROWS * (p + 1)]
                first[p] = first[p] + part[:, :LANES] * g_ref[p, pl.ds(base + 1, ROWS), :] * factor
                second[p] = second[p] + part[:, LANES:] * g_ref[p, pl.ds(base, ROWS), :] * factor
        for p in range(2):
            sc[p, 0] = first[p]
            sc[p, 1] = second[p]
        w0 = sc[0, 0, 0:lag_rows] + sc[0, 1, 1 : 1 + lag_rows]
        w0_next = sc[0, 0, 1 : 1 + lag_rows] + sc[0, 1, 2 : 2 + lag_rows]
        w1 = sc[1, 0, 0:lag_rows] + sc[1, 1, 1 : 1 + lag_rows]
        o_ref[pl.ds(k * lag_rows, lag_rows), :] = jnp.where(low_out, w0, w0_next) + pltpu.roll(
            w1, HALF, 1
        )
        return carry

    lax.fori_loop(0, o_ref.shape[0] // lag_rows, one, 0, unroll=4)


def matched_stacks(sensor, scale, taps, main, halo):
    block, sensor_count = main.shape
    length = halo.shape[0]
    count, double, _ = taps.shape
    lag_rows = block // LANES
    total = block + length

    def kernel(sensor, scale, x_ref, main_ref, halo_ref, o_ref, r_ref, g_ref, slab, fa, fb, sc, sem):
        prepare_tables(main_ref, halo_ref, slab, fa, fb, sem, r_ref, g_ref, block, length)
        stack_templates(sensor, scale, x_ref, r_ref, g_ref, o_ref, sc, double // 2, lag_rows)

    single = pl.Buffered(1)
    return pl.pallas_call(
        kernel,
        grid_spec=pltpu.PrefetchScalarGridSpec(
            num_scalar_prefetch=2,
            grid=(1,),
            in_specs=[
                pl.BlockSpec(taps.shape, lambda i, *_: (0, 0, 0), pipeline_mode=single),
                pl.BlockSpec(memory_space=pl.ANY),
                pl.BlockSpec(memory_space=pl.ANY),
            ],
            out_specs=pl.BlockSpec((count * lag_rows, LANES), lambda i, *_: (0, 0), pipeline_mode=single),
            scratch_shapes=[
                pltpu.VMEM((sensor_count * ROWS + 8, LANES), jnp.float32),
                pltpu.VMEM((2, sensor_count * ROWS + 8, LANES), jnp.float32),
                pltpu.VMEM((2, total, LANES), jnp.bfloat16),
                pltpu.VMEM((total + LANES, LANES), jnp.float32),
                pltpu.VMEM((total + LANES, LANES), jnp.float32),
                pltpu.VMEM((2, 2, ROWS, LANES), jnp.float32),
                pltpu.SemaphoreType.DMA((2, 2)),
            ],
        ),
        out_shape=jax.ShapeDtypeStruct((count * lag_rows, LANES), jnp.float32),
        compiler_params=pltpu.CompilerParams(vmem_limit_bytes=62 * 2**20),
    )(sensor, scale, taps, main, halo)


def body(data, templates, cover, channel):
    devices = lax.axis_size("sens")
    layers = devices // GROUP
    per_dev, chan_count, length = templates.shape
    share, sensor_count = data.shape
    sensors_per_group = sensor_count // devices
    block = share * GROUP
    lag_rows = block // LANES
    lag_count = share * devices - length
    in_layer = [[layer * GROUP + j for j in range(GROUP)] for layer in range(layers)]
    across = [[layer * GROUP + j for layer in range(layers)] for j in range(GROUP)]

    main = lax.all_gather(data, "sens", axis_index_groups=in_layer, tiled=True)
    halo = lax.ppermute(
        main[:length], "sens", [(i + GROUP, i) for i in range(devices - GROUP)]
    )
    sensor_own = cover * sensors_per_group + channel
    sensor = lax.all_gather(sensor_own, "sens", axis_index_groups=across, tiled=True)
    weights = lax.all_gather(templates, "sens", axis_index_groups=across, tiled=True)
    count = weights.shape[0]
    wide = weights.astype(jnp.float32)
    power = jnp.sum(wide * wide, axis=2)
    scale = (math.sqrt(length / chan_count) / length) * lax.rsqrt(power / length + EPSILON)
    taps = wide.reshape(count, 2 * chan_count, LANES)[:, :, ::-1]
    stacks = matched_stacks(sensor.reshape(-1), scale.reshape(-1), taps, main, halo)
    spread = lax.all_to_all(
        stacks, "sens", split_axis=0, concat_axis=0, axis_index_groups=across, tiled=True
    )
    spread = spread.reshape(layers, per_dev, lag_rows * LANES)
    return spread.transpose(1, 0, 2).reshape(per_dev, layers * block)[:, :lag_count]


def solution(mesh):
    placed = (P(("parts", "sens"), None), P("sens", None, None), P("sens", None), P("sens", None))
    return jax.shard_map(
        body, mesh=mesh, in_specs=placed, out_specs=P(("parts", "sens"), None), check_vma=False
    )
```

profile of v0, /device:TPU:0, one launch (start us, length us, event | category | flops | bytes accessed | tf_op | source)
XLA Modules:
  0.0 210.0 jit_solution(1671016657352692207)
XLA Ops:
  6.5 0.0 copy-start.1
  6.5 0.0 copy-start.2
  6.5 0.0 all-gather.6.cloned.1.call-start
  6.5 0.7 all-gather.6.cloned.1.call-update
  7.3 0.0 all-gather.4.cloned.1.call-start
  7.3 0.7 all-gather.4.cloned.1.call-update
  8.0 45.1 %all-gather.6.cloned.1.call-done.main_ref = bf16[1280,2048]{1,0:T(8,128)(2,1)} async-done(((bf16[160,2048]{1,0:T(8,128)(2,1)}), bf16[1280,2048]{1,0:T(8,128)(2,1)}) %all-gather.6.cloned.1.call-update) | async-done | bytes 5242896 | tf_op jit(solution)/shard_map/all_gather | solution.py:193
  53.1 2.3 %slice.8 = bf16[256,2048]{1,0:T(8,128)(2,1)} slice(bf16[1280,2048]{1,0:T(8,128)(2,1)} %all-gather.6.cloned.1.call-done.main_ref), slice={[0:256], [0:2048]} | slice | bytes 2097152 | tf_op jit(solution)/shard_map/slice | solution.py:195
  55.4 1.3 collective-permute-start
  56.7 0.0 copy-done.1
  56.7 0.0 copy-done.2
  56.8 52.1 %all-gather = s32[4,32,16]{1,2,0:T(8,128)S(1)} all-gather(s32[1,32,16]{1,2,0:T(8,128)S(1)} %add_bitcast_fusion), channel_id=1, replica_groups={{0,8,16,24},{1,9,17,25},{2,10,18,26},{3,11,19,27},{4,12,20,28},{5,13,21..., dimensions={0}, use_global_device_ids=true | all-gather | bytes 10240 | tf_op jit(solution)/shard_map/all_gather | solution.py:198
  108.8 0.1 copy.13
  108.9 0.7 reshape.24.sensor
  109.6 0.0 all-gather.4.cloned.1.call-done
  109.6 1.6 multiply_reduce_fusion
  111.2 0.1 copy.14
  111.2 0.1 copy.15
  111.4 0.7 mul.24.scale
  112.1 1.4 reshape.25
  113.4 2.3 %rev.3.x_ref = f32[128,32,128]{2,1,0:T(8,128)} reverse(f32[128,32,128]{2,1,0:T(8,128)S(1)} %reshape.25), dimensions={2} | reverse | bytes 4194304 | tf_op jit(solution)/shard_map/rev | solution.py:204
  115.8 0.0 collective-permute-done.halo_ref
  115.8 0.0 copy-start
  115.8 1.0 copy-done
  116.8 66.4 %shard_map.46 = f32[1280,128]{1,0:T(8,128)} custom-call(s32[2048]{0:T(1024)} %reshape.24.sensor, f32[2048]{0:T(1024)} %mul.24.scale, f32[128,32,128]{2,1,0:T(8,128)} %rev.3.x_ref, bf16[1280,2048]{1,0:T(8,128)(2,1)} %all-gather.6.cloned.1.call-done.main_ref, bf16[256,2048]{1,0:T(8,128)(2,1)} %copy-done), custom_call_target="tpu_custom_call" | custom-call | tf_op jit(solution)/shard_map/pallas_call | solution.py:155
  183.2 18.4 %all_to_all.9 = f32[4,320,128]{2,1,0:T(8,128)S(1)} all-to-all(f32[4,320,128]{2,1,0:T(8,128)} %bitcast.6), channel_id=1, replica_groups={{0,8,16,24},{1,9,17,25},{2,10,18,26},{3,11,19,27},{4,12,20,28},{5,13,21..., dimensions={0} | all-to-all | bytes 1310720 | tf_op jit(solution)/shard_map/all_to_all | solution.py:206
  201.6 0.1 reshape.26
  201.7 0.4 copy.16
  202.1 0.1 copy.17
  202.3 0.9 slice.9
  (2 shorter events, 0.0 us)
Async XLA Ops:
  6.5 50.2 %copy-start.1 = (s32[32,16]{0,1:T(8,128)S(1)}, s32[32,16]{0,1:T(8,128)}, u32[]{:S(2)}) copy-start(s32[32,16]{0,1:T(8,128)} %param.7) | copy-start | bytes 6148
  6.5 50.2 %copy-start.2 = (s32[32,16]{0,1:T(8,128)S(1)}, s32[32,16]{0,1:T(8,128)}, u32[]{:S(2)}) copy-start(s32[32,16]{0,1:T(8,128)} %param.6) | copy-start | bytes 6148
  6.5 46.6 %all-gather.6.cloned.1.call-start = ((), (), s32[]{:S(2)}) async-start(), calls=%async_computation.2 | async-start | bytes 5898240 | tf_op jit(solution)/shard_map/all_gather | solution.py:193
  7.3 102.3 %all-gather.4.cloned.1.call-start = ((), (), s32[]{:S(2)}) async-start(), calls=%async_computation.1 | async-start | bytes 1310720 | tf_op jit(solution)/shard_map/all_gather | solution.py:199
  55.4 60.3 %collective-permute-start = (bf16[256,2048]{1,0:T(8,128)(2,1)}, bf16[256,2048]{1,0:T(8,128)(2,1)S(1)}, u32[]{:S(2)}, u32[]{:S(2)}) collective-permute-start(bf16[256,2048]{1,0:T(8,128)(2,1)} %slice.8), channel_id=1, source_target_pairs={{8,0},{9,1},{10,2},{11,3},{12,4},{13,5},{14,6},{15,7},{16,8},{17,9... | collective-permute-start | bytes 3145736 | tf_op jit(solution)/shard_map/ppermute | solution.py:194
  115.8 1.0 copy-start
Sparse Core Ops, SparseCore 0:
  9.2 43.8 all-gather.5
  54.7 39.0 all-gather.3
where the time goes:
time: 210 us
  blocking collectives  70.5 us (34%)
  Pallas kernels  66.4 us (32%)
  waiting for transfers between devices  46.5 us (22%)
  between operations  13.5 us (6%)
  local copies, waits for them, and re-layouts  10.2 us (5%)
    pallas_call x1, Pallas kernels, matched_stacks(): pl.pallas_call(kernel, grid_spec=pltpu.PrefetchScalarGridSpec(num_scalar_...  66.4 us
    all_gather x1, blocking collectives, body(): lax.all_gather(sensor_own, 'sens', axis_index_groups=across, tiled=True)  52.1 us
    all_gather x1, waiting for transfers between devices, body(): main = lax.all_gather(data, 'sens', axis_index_groups=in_layer, tiled=True)  45.1 us
    all_to_all x1, blocking collectives, body(): lax.all_to_all(stacks, 'sens', split_axis=0, concat_axis=0, axis_index_gr...  18.4 us
  transfers between devices with their start and end apart: 3, of which 1 were waited for; matrix products, arithmetic and copies ran while one was open for 4% of the time, Pallas kernels for 0%

commit v1 on v0

--- a/solution.py
+++ b/solution.py
@@ -14,9 +14,9 @@
 GROUP = 8
 
 
-def prepare_tables(main_ref, halo_ref, slab, fa, fb, sem, r_ref, g_ref, block, length):
+def prepare_tables(place, pieces, slab, fa, fb, sem, r_ref, g_ref, block, length):
     total = block + length
-    strips = main_ref.shape[1] // LANES
+    strips = pieces[0].shape[1] // LANES
     row_count = total // LANES
     lag_rows = block // LANES
     zero_tile = jnp.zeros((LANES, LANES), jnp.float32)
@@ -24,12 +24,13 @@
 
     def copies(strip, slot):
         cols = pl.ds(pl.multiple_of(strip * LANES, LANES), LANES)
-        return (
-            pltpu.make_async_copy(main_ref.at[:, cols], slab.at[slot, pl.ds(0, block)], sem.at[slot, 0]),
-            pltpu.make_async_copy(
-                halo_ref.at[:, cols], slab.at[slot, pl.ds(block, length)], sem.at[slot, 1]
-            ),
-        )
+        made = []
+        for i, piece in enumerate(pieces):
+            rows = pl.ds(pl.multiple_of(place[i], 16), piece.shape[0])
+            made.append(
+                pltpu.make_async_copy(piece.at[:, cols], slab.at[slot, rows], sem.at[slot, i])
+            )
+        return made
 
     def windowed(source, target, offsets, count):
         for start in range(0, count, HALF):
@@ -140,42 +141,42 @@
     lax.fori_loop(0, o_ref.shape[0] // lag_rows, one, 0, unroll=4)
 
 
-def matched_stacks(sensor, scale, taps, main, halo):
-    block, sensor_count = main.shape
-    length = halo.shape[0]
+def matched_stacks(sensor, scale, place, taps, pieces, block, length):
+    sensor_count = pieces[0].shape[1]
     count, double, _ = taps.shape
     lag_rows = block // LANES
     total = block + length
-
-    def kernel(sensor, scale, x_ref, main_ref, halo_ref, o_ref, r_ref, g_ref, slab, fa, fb, sc, sem):
-        prepare_tables(main_ref, halo_ref, slab, fa, fb, sem, r_ref, g_ref, block, length)
+    held = block + 2 * pieces[0].shape[0]
+    piece_count = len(pieces)
+
+    def kernel(sensor, scale, place, x_ref, *refs):
+        ins = refs[:piece_count]
+        o_ref, r_ref, g_ref, slab, fa, fb, sc, sem = refs[piece_count:]
+        prepare_tables(place, ins, slab, fa, fb, sem, r_ref, g_ref, block, length)
         stack_templates(sensor, scale, x_ref, r_ref, g_ref, o_ref, sc, double // 2, lag_rows)
 
     single = pl.Buffered(1)
     return pl.pallas_call(
         kernel,
         grid_spec=pltpu.PrefetchScalarGridSpec(
-            num_scalar_prefetch=2,
+            num_scalar_prefetch=3,
             grid=(1,),
-            in_specs=[
-                pl.BlockSpec(taps.shape, lambda i, *_: (0, 0, 0), pipeline_mode=single),
-                pl.BlockSpec(memory_space=pl.ANY),
-                pl.BlockSpec(memory_space=pl.ANY),
-            ],
+            in_specs=[pl.BlockSpec(taps.shape, lambda i, *_: (0, 0, 0), pipeline_mode=single)]
+            + [pl.BlockSpec(memory_space=pl.ANY)] * piece_count,
             out_specs=pl.BlockSpec((count * lag_rows, LANES), lambda i, *_: (0, 0), pipeline_mode=single),
             scratch_shapes=[
                 pltpu.VMEM((sensor_count * ROWS + 8, LANES), jnp.float32),
                 pltpu.VMEM((2, sensor_count * ROWS + 8, LANES), jnp.float32),
-                pltpu.VMEM((2, total, LANES), jnp.bfloat16),
+                pltpu.VMEM((2, held, LANES), jnp.bfloat16),
                 pltpu.VMEM((total + LANES, LANES), jnp.float32),
                 pltpu.VMEM((total + LANES, LANES), jnp.float32),
                 pltpu.VMEM((2, 2, ROWS, LANES), jnp.float32),
-                pltpu.SemaphoreType.DMA((2, 2)),
+                pltpu.SemaphoreType.DMA((2, piece_count)),
             ],
         ),
         out_shape=jax.ShapeDtypeStruct((count * lag_rows, LANES), jnp.float32),
         compiler_params=pltpu.CompilerParams(vmem_limit_bytes=62 * 2**20),
-    )(sensor, scale, taps, main, halo)
+    )(sensor, scale, place, taps, *pieces)
 
 
 def body(data, templates, cover, channel):
@@ -187,27 +188,78 @@
     block = share * GROUP
     lag_rows = block // LANES
     lag_count = share * devices - length
-    in_layer = [[layer * GROUP + j for j in range(GROUP)] for layer in range(layers)]
-    across = [[layer * GROUP + j for layer in range(layers)] for j in range(GROUP)]
-
-    main = lax.all_gather(data, "sens", axis_index_groups=in_layer, tiled=True)
-    halo = lax.ppermute(
-        main[:length], "sens", [(i + GROUP, i) for i in range(devices - GROUP)]
-    )
-    sensor_own = cover * sensors_per_group + channel
-    sensor = lax.all_gather(sensor_own, "sens", axis_index_groups=across, tiled=True)
-    weights = lax.all_gather(templates, "sens", axis_index_groups=across, tiled=True)
-    count = weights.shape[0]
-    wide = weights.astype(jnp.float32)
-    power = jnp.sum(wide * wide, axis=2)
+    half = share // 2
+    me = lax.axis_index("sens")
+    layer, inner = me // GROUP, me % GROUP
+
+    def flip(value, bits):
+        return lax.ppermute(value, "sens", [(i, i ^ bits) for i in range(devices)])
+
+    item_rows = per_dev * 2 * chan_count
+    id_rows = per_dev * chan_count // LANES
+    reversed_halves = templates.reshape(item_rows, LANES)[:, ::-1]
+    pad_rows = -(item_rows + 2 * id_rows) % 16
+    packet = jnp.concatenate(
+        [
+            reversed_halves,
+            cover.reshape(id_rows, LANES).astype(jnp.bfloat16),
+            channel.reshape(id_rows, LANES).astype(jnp.bfloat16),
+            jnp.zeros((pad_rows, LANES), jnp.bfloat16),
+        ],
+        axis=0,
+    )
+
+    near = flip(data, 2)
+    side = flip(data, 4)
+    packets = [flip(packet, GROUP * q) for q in reversed(range(1, layers))]
+    twin = flip(data, 1)
+    far_low = flip(near[:half], 4)
+    far_high = flip(side[half:], 2)
+    near_twin = flip(near, 1)
+    side_twin = flip(side, 1)
+    far_low_twin = flip(far_low, 1)
+    far_high_twin = flip(far_high, 1)
+    far = jnp.concatenate([far_low, far_high], axis=0)
+    chip = inner // 2
+    lead = jnp.where(
+        chip == 0, data, jnp.where(chip == 1, near, jnp.where(chip == 2, side, far))
+    )
+    held = lax.optimization_barrier(
+        (lead, *packets, twin, near_twin, side_twin, far_low_twin, far_high_twin)
+    )
+    lead, packets = held[0], [packet] + list(held[1:layers][::-1])
+    twin, near_twin, side_twin, far_low_twin, far_high_twin = held[layers:]
+    halo = lax.ppermute(lead, "sens", [(i + GROUP, i) for i in range(devices - GROUP)])
+    halo_twin = flip(halo, 1)
+    pieces = [
+        data, near, side, twin, near_twin, side_twin,
+        far_low, far_high, far_low_twin, far_high_twin, halo, halo_twin,
+    ]
+    core = inner % 2
+    starts = [share * (inner ^ r) for r in (0, 2, 4, 1, 3, 5)]
+    starts += [share * (inner ^ 6), share * (inner ^ 6) + half]
+    starts += [share * (inner ^ 7), share * (inner ^ 7) + half]
+    starts += [block + share * core, block + share * (1 - core)]
+    place = jnp.stack(starts).astype(jnp.int32)
+
+    gathered = jnp.stack(packets)
+    count = layers * per_dev
+    wide = gathered[:, :item_rows].astype(jnp.float32).reshape(count, 2 * chan_count, LANES)
+    ids = gathered[:, item_rows : item_rows + 2 * id_rows].astype(jnp.int32)
+    sensor = (ids[:, :id_rows] * sensors_per_group + ids[:, id_rows:]).reshape(-1)
+    power = jnp.sum((wide * wide).reshape(count, chan_count, length), axis=2)
     scale = (math.sqrt(length / chan_count) / length) * lax.rsqrt(power / length + EPSILON)
-    taps = wide.reshape(count, 2 * chan_count, LANES)[:, :, ::-1]
-    stacks = matched_stacks(sensor.reshape(-1), scale.reshape(-1), taps, main, halo)
-    spread = lax.all_to_all(
-        stacks, "sens", split_axis=0, concat_axis=0, axis_index_groups=across, tiled=True
-    )
-    spread = spread.reshape(layers, per_dev, lag_rows * LANES)
-    return spread.transpose(1, 0, 2).reshape(per_dev, layers * block)[:, :lag_count]
+
+    stacks = matched_stacks(sensor, scale.reshape(-1), place, wide, pieces, block, length)
+    parts = stacks.reshape(layers, per_dev * lag_rows, LANES)
+    received = [parts[0]] + [flip(parts[q], GROUP * q) for q in range(1, layers)]
+    ordered = []
+    for slot in range(layers):
+        value = received[slot]
+        for mine in range(1, layers):
+            value = jnp.where(layer == mine, received[slot ^ mine], value)
+        ordered.append(value.reshape(per_dev, block))
+    return jnp.concatenate(ordered, axis=1)[:, :lag_count]
 
 
 def solution(mesh):

time: 210 us -> 149 us (0.71)
  blocking collectives: 70.5 us -> 0 us
  starting transfers between devices: 1.32 us -> 18.8 us
  between operations: 13.5 us -> 0.17 us
  other arithmetic: 1.59 us -> 9.45 us
  waiting for transfers between devices: 46.5 us -> 42.4 us
    all_gather x1 -> x0, blocking collectives: 52.1 us -> none  [body(): lax.all_gather(sensor_own, 'sens', axis_index_groups=across, tiled=True)]
    all_gather x2 -> x0, waiting for transfers between devices: 45.1 us -> none  [the longest x1 45.1 us: body(): main = lax.all_gather(data, 'sens', axis_index_groups=in_layer, tiled=True)]
    ppermute x1 -> x17, waiting for transfers between devices: 0.01 us -> 42.4 us  [the longest x16 29.2 us: flip(): return lax.ppermute(value, 'sens', [(i, i ^ bits) for i in range(devices)])]
    all_to_all x1 -> x0, blocking collectives: 18.4 us -> none  [body(): lax.all_to_all(stacks, 'sens', split_axis=0, concat_axis=0, axis_index_gr...]
    ppermute x1 -> x17, starting transfers between devices: 1.28 us -> 18.8 us  [the longest x16 17.6 us: flip(): return lax.ppermute(value, 'sens', [(i, i ^ bits) for i in range(devices)])]
    select_n x0 -> x2, other arithmetic: none -> 3.23 us  [the longest x1 2.24 us: body(): jnp.where(chip == 0, data, jnp.where(chip == 1, near, jnp.where(chip == 2...]
    convert_element_type x0 -> x4, other arithmetic: none -> 2.92 us  [the longest x1 1.51 us: body(): gathered[:, :item_rows].astype(jnp.float32)]
  transfers between devices with their start and end apart: 3 -> 17, of which waited for: 1 -> 6; matrix products, arithmetic and copies ran while one was open for 4% -> 10% of each run, Pallas kernels for 0% -> 0%
where the time goes in v1:
time: 149 us; the launch traced here: 148 us
  Pallas kernels  67.2 us (45%)
  waiting for transfers between devices  42.4 us (28%)
  starting transfers between devices  18.8 us (13%)
  local copies, waits for them, and re-layouts  10 us (7%)
  other arithmetic  9.45 us (6%)
    pallas_call x1, Pallas kernels, matched_stacks(): pl.pallas_call(kernel, grid_spec=pltpu.PrefetchScalarGridSpec(num_scalar_...  67.2 us
    ppermute x16, waiting for transfers between devices, flip(): return lax.ppermute(value, 'sens', [(i, i ^ bits) for i in range(devices)])  29.2 us
    ppermute x16, starting transfers between devices, flip(): return lax.ppermute(value, 'sens', [(i, i ^ bits) for i in range(devices)])  17.6 us
    ppermute x1, waiting for transfers between devices, body(): lax.ppermute(lead, 'sens', [(i + GROUP, i) for i in range(devices - GROUP)])  13.3 us
  transfers between devices with their start and end apart: 17, of which 6 were waited for; matrix products, arithmetic and copies ran while one was open for 10% of the time, Pallas kernels for 0%

profile of v1, /device:TPU:0, one launch (start us, length us, event | category | flops | bytes accessed | tf_op | source)
XLA Modules:
  0.0 148.1 jit_solution(10377039274600807366)
XLA Ops:
  0.0 2.9 %collective-permute-start = (bf16[160,2048]{1,0:T(8,128)(2,1)}, bf16[160,2048]{1,0:T(8,128)(2,1)S(1)}, u32[]{:S(2)}, u32[]{:S(2)}) collective-permute-start(bf16[160,2048]{1,0:T(8,128)(2,1)} %refs_0_.1), channel_id=1, source_target_pairs={{0,2},{1,3},{2,0},{3,1},{4,6},{5,7},{6,4},{7,5},{8,10},{9,11},{10,... | collective-permute-start | bytes 1966088 | tf_op jit(solution)/shard_map/ppermute | solution.py:196
  2.9 1.5 %collective-permute-start.1 = (bf16[160,2048]{1,0:T(8,128)(2,1)}, bf16[160,2048]{1,0:T(8,128)(2,1)S(1)}, u32[]{:S(2)}, u32[]{:S(2)}) collective-permute-start(bf16[160,2048]{1,0:T(8,128)(2,1)} %refs_0_.1), channel_id=1, source_target_pairs={{0,4},{1,5},{2,6},{3,7},{4,0},{5,1},{6,2},{7,3},{8,12},{9,13},{10,... | collective-permute-start | bytes 1966088 | tf_op jit(solution)/shard_map/ppermute | solution.py:196
  4.5 1.0 reshape.46
  5.5 0.8 rev.3
  6.3 0.7 convert_element_type.18
  7.2 0.7 convert_element_type.20
  8.2 3.6 %collective-permute-start.4 = (bf16[1040,128]{1,0:T(8,128)(2,1)S(1)}, bf16[1040,128]{1,0:T(8,128)(2,1)S(1)}, u32[]{:S(2)}, u32[]{:S(2)}) collective-permute-start(bf16[1040,128]{1,0:T(8,128)(2,1)S(1)} %concatenate.9), channel_id=1, source_target_pairs={{0,24},{1,25},{2,26},{3,27},{4,28},{5,29},{6,30},{7,31},{8,16},{9,... | collective-permute-start | bytes 798728 | tf_op jit(solution)/shard_map/ppermute | solution.py:196
  11.8 0.8 collective-permute-start.6
  12.6 5.3 %collective-permute-done.refs_1_ = bf16[160,2048]{1,0:T(8,128)(2,1)S(1)} collective-permute-done((bf16[160,2048]{1,0:T(8,128)(2,1)}, bf16[160,2048]{1,0:T(8,128)(2,1)S(1)}, u32[]{:S(2)}, u32[]{:S(2)}) %collective-permute-start) | collective-permute-done | bytes 655392 | tf_op jit(solution)/shard_map/ppermute | solution.py:196
  18.0 0.8 slice.48
  18.8 1.7 %collective-permute-start.2 = (bf16[80,2048]{1,0:T(8,128)(2,1)}, bf16[80,2048]{1,0:T(8,128)(2,1)S(1)}, u32[]{:S(2)}, u32[]{:S(2)}) collective-permute-start(bf16[80,2048]{1,0:T(8,128)(2,1)} %slice.48), channel_id=1, source_target_pairs={{0,4},{1,5},{2,6},{3,7},{4,0},{5,1},{6,2},{7,3},{8,12},{9,13},{10,... | collective-permute-start | bytes 983048 | tf_op jit(solution)/shard_map/ppermute | solution.py:196
  20.5 0.8 slice.49
  21.3 1.5 %collective-permute-start.3 = (bf16[80,2048]{1,0:T(8,128)(2,1)}, bf16[80,2048]{1,0:T(8,128)(2,1)}, u32[]{:S(2)}, u32[]{:S(2)}) collective-permute-start(bf16[80,2048]{1,0:T(8,128)(2,1)} %slice.49), channel_id=1, source_target_pairs={{0,2},{1,3},{2,0},{3,1},{4,6},{5,7},{6,4},{7,5},{8,10},{9,11},{10,... | collective-permute-start | bytes 983048 | tf_op jit(solution)/shard_map/ppermute | solution.py:196
  22.8 11.2 %collective-permute-done.5 = bf16[1040,128]{1,0:T(8,128)(2,1)S(1)} collective-permute-done((bf16[1040,128]{1,0:T(8,128)(2,1)S(1)}, bf16[1040,128]{1,0:T(8,128)(2,1)S(1)}, u32[]{:S(2)}, u32[]{:S(2)}) %collective-permute-start.5) | collective-permute-done | bytes 266272 | tf_op jit(solution)/shard_map/ppermute | solution.py:196
  35.0 2.2 %fusion.2 = bf16[160,2048]{1,0:T(8,128)(2,1)} fusion(bf16[160,2048]{1,0:T(8,128)(2,1)S(1)} %copy-done.2, bf16[160,2048]{1,0:T(8,128)(2,1)S(1)} %collective-permute-done.refs_1_, bf16[160,2048]{1,0:T(8,128)(2,1)S(1)} %collective-permute-done.1.refs_2_, bf16[80,2048]{1,0:T(8,128)(2,1)} %collective-permute-done.3.refs_7_, ...), kind=kLoop, calls=%fused_computation.6 | loop fusion | flops 2293760 | bytes 3276803 | tf_op jit(solution)/shard_map/jit(_where)/select_n | solution.py:224
  37.2 0.8 collective-permute-done.9.refs_5_
  38.1 0.8 copy-done.6
  38.8 0.8 copy-done.7
  39.6 1.3 collective-permute-start.12
  41.5 1.5 fusion.3
  43.0 1.9 %mul.58 = f32[128,16,256]{2,1,0:T(8,128)S(1)} reshape(f32[4,1024,128]{2,1,0:T(8,128)} %fusion.3) | data formatting | bytes 4194304 | tf_op jit(solution)/shard_map/mul | solution.py:250
  45.3 13.3 %collective-permute-done.12.refs_10_ = bf16[160,2048]{1,0:T(8,128)(2,1)} collective-permute-done((bf16[160,2048]{1,0:T(8,128)(2,1)}, bf16[160,2048]{1,0:T(8,128)(2,1)}, u32[]{:S(2)}, u32[]{:S(2)}) %collective-permute-start.12) | collective-permute-done | bytes 655392 | tf_op jit(solution)/shard_map/ppermute | solution.py:232
  58.7 0.7 mul.61.scale
  59.3 1.5 %fusion = f32[4,1024,128]{2,1,0:T(8,128)} fusion(bf16[1,1040,128]{2,1,0:T(8,128)(2,1)S(1)} %bitcast.24, bf16[1,1040,128]{2,1,0:T(8,128)(2,1)S(1)} %bitcast.27, bf16[1,1040,128]{2,1,0:T(8,128)(2,1)S(1)} %bitcast.30, bf16[1,1040,128]{2,1,0:T(8,128)(2,1)S(1)} %bitcast.21), kind=kLoop, calls=%fused_computation.1 | loop fusion | flops 4194304 | bytes 3162112 | tf_op jit(solution)/shard_map/convert_element_type | solution.py:247
  61.5 67.2 %shard_map.46 = f32[1280,128]{1,0:T(8,128)} custom-call(s32[2048]{0:T(1024)} %bitcast.31, f32[2048]{0:T(1024)} %mul.61.scale, s32[12]{0:T(128)} %stack.71.place, f32[128,32,128]{2,1,0:T(8,128)} %bitcast.18, bf16[160,2048]{1,0:T(8,128)(2,1)} %refs_0_.1, bf16[160,2048]{1,0:T(8,128)(2,1)} %copy-done, bf16[160,2048]{1,0:T(8,128)(2,1)} %copy-done.1, ...), custom_call_target="tpu_custom_call" | custom-call | tf_op jit(solution)/shard_map/pallas_call | solution.py:159
  128.7 1.1 fusion.4
  129.9 1.1 collective-permute-start.15
  131.0 3.3 %collective-permute-start.16 = (f32[320,128]{1,0:T(8,128)S(1)}, f32[320,128]{1,0:T(8,128)S(1)}, u32[]{:S(2)}, u32[]{:S(2)}) collective-permute-start(f32[320,128]{1,0:T(8,128)S(1)} %get-tuple-element.28), channel_id=1, source_target_pairs={{0,8},{1,9},{2,10},{3,11},{4,12},{5,13},{6,14},{7,15},{8,0},{9,1},... | collective-permute-start | bytes 491528 | tf_op jit(solution)/shard_map/ppermute | solution.py:196
  134.2 4.6 %collective-permute-done.14 = f32[320,128]{1,0:T(8,128)S(1)} collective-permute-done((f32[320,128]{1,0:T(8,128)S(1)}, f32[320,128]{1,0:T(8,128)S(1)}, u32[]{:S(2)}, u32[]{:S(2)}) %collective-permute-start.14) | collective-permute-done | bytes 163872 | tf_op jit(solution)/shard_map/ppermute | solution.py:196
  138.8 7.3 %collective-permute-done.15 = f32[320,128]{1,0:T(8,128)S(1)} collective-permute-done((f32[320,128]{1,0:T(8,128)S(1)}, f32[320,128]{1,0:T(8,128)S(1)}, u32[]{:S(2)}, u32[]{:S(2)}) %collective-permute-start.15) | collective-permute-done | bytes 163872 | tf_op jit(solution)/shard_map/ppermute | solution.py:196
  146.1 1.0 select_select_fusion.3
  147.3 0.9 pad_maximum_fusion.3
  (50 shorter events, 3.5 us)
Async XLA Ops:
  0.0 22.8 %copy-start.2 = (bf16[160,2048]{1,0:T(8,128)(2,1)S(1)}, bf16[160,2048]{1,0:T(8,128)(2,1)}, u32[]{:S(2)}) copy-start(bf16[160,2048]{1,0:T(8,128)(2,1)} %refs_0_.1) | copy-start | bytes 1966084
  0.0 17.9 %collective-permute-start = (bf16[160,2048]{1,0:T(8,128)(2,1)}, bf16[160,2048]{1,0:T(8,128)(2,1)S(1)}, u32[]{:S(2)}, u32[]{:S(2)}) collective-permute-start(bf16[160,2048]{1,0:T(8,128)(2,1)} %refs_0_.1), channel_id=1, source_target_pairs={{0,2},{1,3},{2,0},{3,1},{4,6},{5,7},{6,4},{7,5},{8,10},{9,11},{10,... | collective-permute-start | bytes 1966088 | tf_op jit(solution)/shard_map/ppermute | solution.py:196
  2.9 17.5 %collective-permute-start.1 = (bf16[160,2048]{1,0:T(8,128)(2,1)}, bf16[160,2048]{1,0:T(8,128)(2,1)S(1)}, u32[]{:S(2)}, u32[]{:S(2)}) collective-permute-start(bf16[160,2048]{1,0:T(8,128)(2,1)} %refs_0_.1), channel_id=1, source_target_pairs={{0,4},{1,5},{2,6},{3,7},{4,0},{5,1},{6,2},{7,3},{8,12},{9,13},{10,... | collective-permute-start | bytes 1966088 | tf_op jit(solution)/shard_map/ppermute | solution.py:196
  8.2 14.6 %collective-permute-start.4 = (bf16[1040,128]{1,0:T(8,128)(2,1)S(1)}, bf16[1040,128]{1,0:T(8,128)(2,1)S(1)}, u32[]{:S(2)}, u32[]{:S(2)}) collective-permute-start(bf16[1040,128]{1,0:T(8,128)(2,1)S(1)} %concatenate.9), channel_id=1, source_target_pairs={{0,24},{1,25},{2,26},{3,27},{4,28},{5,29},{6,30},{7,31},{8,16},{9,... | collective-permute-start | bytes 798728 | tf_op jit(solution)/shard_map/ppermute | solution.py:196
  11.8 22.1 %collective-permute-start.5 = (bf16[1040,128]{1,0:T(8,128)(2,1)S(1)}, bf16[1040,128]{1,0:T(8,128)(2,1)S(1)}, u32[]{:S(2)}, u32[]{:S(2)}) collective-permute-start(bf16[1040,128]{1,0:T(8,128)(2,1)S(1)} %concatenate.9), channel_id=1, source_target_pairs={{0,16},{1,17},{2,18},{3,19},{4,20},{5,21},{6,22},{7,23},{8,24},{9,... | collective-permute-start | bytes 798728 | tf_op jit(solution)/shard_map/ppermute | solution.py:196
  11.8 22.1 %collective-permute-start.6 = (bf16[1040,128]{1,0:T(8,128)(2,1)S(1)}, bf16[1040,128]{1,0:T(8,128)(2,1)S(1)}, u32[]{:S(2)}, u32[]{:S(2)}) collective-permute-start(bf16[1040,128]{1,0:T(8,128)(2,1)S(1)} %concatenate.9), channel_id=1, source_target_pairs={{0,8},{1,9},{2,10},{3,11},{4,12},{5,13},{6,14},{7,15},{8,0},{9,1},... | collective-permute-start | bytes 798728 | tf_op jit(solution)/shard_map/ppermute | solution.py:196
  18.0 19.3 %copy-start = (bf16[160,2048]{1,0:T(8,128)(2,1)}, bf16[160,2048]{1,0:T(8,128)(2,1)S(1)}, u32[]{:S(2)}) copy-start(bf16[160,2048]{1,0:T(8,128)(2,1)S(1)} %collective-permute-done.refs_1_) | copy-start | bytes 1966084
  18.8 15.7 %collective-permute-start.2 = (bf16[80,2048]{1,0:T(8,128)(2,1)}, bf16[80,2048]{1,0:T(8,128)(2,1)S(1)}, u32[]{:S(2)}, u32[]{:S(2)}) collective-permute-start(bf16[80,2048]{1,0:T(8,128)(2,1)} %slice.48), channel_id=1, source_target_pairs={{0,4},{1,5},{2,6},{3,7},{4,0},{5,1},{6,2},{7,3},{8,12},{9,13},{10,... | collective-permute-start | bytes 983048 | tf_op jit(solution)/shard_map/ppermute | solution.py:196
  20.5 21.0 %copy-start.1 = (bf16[160,2048]{1,0:T(8,128)(2,1)}, bf16[160,2048]{1,0:T(8,128)(2,1)S(1)}, u32[]{:S(2)}) copy-start(bf16[160,2048]{1,0:T(8,128)(2,1)S(1)} %collective-permute-done.1.refs_2_) | copy-start | bytes 1966084
  21.3 13.3 %collective-permute-start.3 = (bf16[80,2048]{1,0:T(8,128)(2,1)}, bf16[80,2048]{1,0:T(8,128)(2,1)}, u32[]{:S(2)}, u32[]{:S(2)}) collective-permute-start(bf16[80,2048]{1,0:T(8,128)(2,1)} %slice.49), channel_id=1, source_target_pairs={{0,2},{1,3},{2,0},{3,1},{4,6},{5,7},{6,4},{7,5},{8,10},{9,11},{10,... | collective-permute-start | bytes 983048 | tf_op jit(solution)/shard_map/ppermute | solution.py:196
  22.8 14.4 %collective-permute-start.7 = (bf16[160,2048]{1,0:T(8,128)(2,1)S(1)}, bf16[160,2048]{1,0:T(8,128)(2,1)}, u32[]{:S(2)}, u32[]{:S(2)}) collective-permute-start(bf16[160,2048]{1,0:T(8,128)(2,1)S(1)} %copy-done.2), channel_id=1, source_target_pairs={{0,1},{1,0},{2,3},{3,2},{4,5},{5,4},{6,7},{7,6},{8,9},{9,8},{10,11... | collective-permute-start | bytes 1966088 | tf_op jit(solution)/shard_map/ppermute | solution.py:196
  33.9 3.3 %collective-permute-start.8 = (bf16[160,2048]{1,0:T(8,128)(2,1)S(1)}, bf16[160,2048]{1,0:T(8,128)(2,1)}, u32[]{:S(2)}, u32[]{:S(2)}) collective-permute-start(bf16[160,2048]{1,0:T(8,128)(2,1)S(1)} %collective-permute-done.refs_1_), channel_id=1, source_target_pairs={{0,1},{1,0},{2,3},{3,2},{4,5},{5,4},{6,7},{7,6},{8,9},{9,8},{10,11... | collective-permute-start | bytes 1966088 | tf_op jit(solution)/shard_map/ppermute | solution.py:196
  34.0 7.5 %copy-start.3 = (bf16[1040,128]{1,0:T(8,128)(2,1)}, bf16[1040,128]{1,0:T(8,128)(2,1)S(1)}, u32[]{:S(2)}) copy-start(bf16[1040,128]{1,0:T(8,128)(2,1)S(1)} %collective-permute-done.6) | copy-start | bytes 798724
  34.0 4.1 %collective-permute-start.9 = (bf16[160,2048]{1,0:T(8,128)(2,1)S(1)}, bf16[160,2048]{1,0:T(8,128)(2,1)}, u32[]{:S(2)}, u32[]{:S(2)}) collective-permute-start(bf16[160,2048]{1,0:T(8,128)(2,1)S(1)} %collective-permute-done.1.refs_2_), channel_id=1, source_target_pairs={{0,1},{1,0},{2,3},{3,2},{4,5},{5,4},{6,7},{7,6},{8,9},{9,8},{10,11... | collective-permute-start | bytes 1966088 | tf_op jit(solution)/shard_map/ppermute | solution.py:196
  34.5 7.0 %copy-start.5 = (bf16[80,2048]{1,0:T(8,128)(2,1)}, bf16[80,2048]{1,0:T(8,128)(2,1)S(1)}, u32[]{:S(2)}) copy-start(bf16[80,2048]{1,0:T(8,128)(2,1)S(1)} %collective-permute-done.2.refs_6_) | copy-start | bytes 983044
  34.5 3.6 %collective-permute-start.10 = (bf16[80,2048]{1,0:T(8,128)(2,1)S(1)}, bf16[80,2048]{1,0:T(8,128)(2,1)S(1)}, u32[]{:S(2)}, u32[]{:S(2)}) collective-permute-start(bf16[80,2048]{1,0:T(8,128)(2,1)S(1)} %collective-permute-done.2.refs_6_), channel_id=1, source_target_pairs={{0,1},{1,0},{2,3},{3,2},{4,5},{5,4},{6,7},{7,6},{8,9},{9,8},{10,11... | collective-permute-start | bytes 983048 | tf_op jit(solution)/shard_map/ppermute | solution.py:196
  34.6 4.2 %collective-permute-start.11 = (bf16[80,2048]{1,0:T(8,128)(2,1)}, bf16[80,2048]{1,0:T(8,128)(2,1)S(1)}, u32[]{:S(2)}, u32[]{:S(2)}) collective-permute-start(bf16[80,2048]{1,0:T(8,128)(2,1)} %collective-permute-done.3.refs_7_), channel_id=1, source_target_pairs={{0,1},{1,0},{2,3},{3,2},{4,5},{5,4},{6,7},{7,6},{8,9},{9,8},{10,11... | collective-permute-start | bytes 983048 | tf_op jit(solution)/shard_map/ppermute | solution.py:196
  38.1 0.8 copy-start.6
  38.8 0.8 copy-start.7
  39.6 19.0 %collective-permute-start.12 = (bf16[160,2048]{1,0:T(8,128)(2,1)}, bf16[160,2048]{1,0:T(8,128)(2,1)}, u32[]{:S(2)}, u32[]{:S(2)}) collective-permute-start(bf16[160,2048]{1,0:T(8,128)(2,1)} %fusion.2), channel_id=1, source_target_pairs={{8,0},{9,1},{10,2},{11,3},{12,4},{13,5},{14,6},{15,7},{16,8},{17,9... | collective-permute-start | bytes 1966088 | tf_op jit(solution)/shard_map/ppermute | solution.py:232
  44.9 14.5 %copy-start.4 = (bf16[1040,128]{1,0:T(8,128)(2,1)S(1)}, bf16[1040,128]{1,0:T(8,128)(2,1)}, u32[]{:S(2)}) copy-start(bf16[1040,128]{1,0:T(8,128)(2,1)} %copy-done.3) | copy-start | bytes 798724
  58.5 2.9 %collective-permute-start.13 = (bf16[160,2048]{1,0:T(8,128)(2,1)}, bf16[160,2048]{1,0:T(8,128)(2,1)}, u32[]{:S(2)}, u32[]{:S(2)}) collective-permute-start(bf16[160,2048]{1,0:T(8,128)(2,1)} %collective-permute-done.12.refs_10_), channel_id=1, source_target_pairs={{0,1},{1,0},{2,3},{3,2},{4,5},{5,4},{6,7},{7,6},{8,9},{9,8},{10,11... | collective-permute-start | bytes 1966088 | tf_op jit(solution)/shard_map/ppermute | solution.py:196
  129.8 9.0 %collective-permute-start.14 = (f32[320,128]{1,0:T(8,128)S(1)}, f32[320,128]{1,0:T(8,128)S(1)}, u32[]{:S(2)}, u32[]{:S(2)}) collective-permute-start(f32[320,128]{1,0:T(8,128)S(1)} %get-tuple-element.27), channel_id=1, source_target_pairs={{0,24},{1,25},{2,26},{3,27},{4,28},{5,29},{6,30},{7,31},{8,16},{9,... | collective-permute-start | bytes 491528 | tf_op jit(solution)/shard_map/ppermute | solution.py:196
  129.9 16.2 %collective-permute-start.15 = (f32[320,128]{1,0:T(8,128)S(1)}, f32[320,128]{1,0:T(8,128)S(1)}, u32[]{:S(2)}, u32[]{:S(2)}) collective-permute-start(f32[320,128]{1,0:T(8,128)S(1)} %get-tuple-element.29), channel_id=1, source_target_pairs={{0,16},{1,17},{2,18},{3,19},{4,20},{5,21},{6,22},{7,23},{8,24},{9,... | collective-permute-start | bytes 491528 | tf_op jit(solution)/shard_map/ppermute | solution.py:196
  131.0 15.1 %collective-permute-start.16 = (f32[320,128]{1,0:T(8,128)S(1)}, f32[320,128]{1,0:T(8,128)S(1)}, u32[]{:S(2)}, u32[]{:S(2)}) collective-permute-start(f32[320,128]{1,0:T(8,128)S(1)} %get-tuple-element.28), channel_id=1, source_target_pairs={{0,8},{1,9},{2,10},{3,11},{4,12},{5,13},{6,14},{7,15},{8,0},{9,1},... | collective-permute-start | bytes 491528 | tf_op jit(solution)/shard_map/ppermute | solution.py:196

commit v2 on v1

--- a/solution.py
+++ b/solution.py
@@ -12,14 +12,16 @@
 HALF = 64
 ROWS = 16
 GROUP = 8
-
-
-def prepare_tables(place, pieces, slab, fa, fb, sem, r_ref, g_ref, block, length):
+SLOTS = 4
+STAGE_ROWS = 33
+
+
+def prepare_tables(place, pieces, slab, stage, fa, fb, sem, w_ref, g_ref, block, length):
     total = block + length
     strips = pieces[0].shape[1] // LANES
-    row_count = total // LANES
     lag_rows = block // LANES
-    zero_tile = jnp.zeros((LANES, LANES), jnp.float32)
+    norm_rows = lag_rows + 3
+    double = 2 * ROWS
     zero_half = jnp.zeros((HALF, LANES), jnp.float32)
 
     def copies(strip, slot):
@@ -39,30 +41,40 @@
                 value = value + source[start + offset : start + offset + HALF, :]
             target[start : start + HALF, :] = value
 
-    for copy in copies(0, 0):
-        copy.start()
+    for ahead in range(SLOTS - 1):
+        for copy in copies(ahead, ahead):
+            copy.start()
+    for start in range(0, LANES * STAGE_ROWS, LANES):
+        stage[start : start + LANES, :] = jnp.zeros((LANES, LANES), jnp.float32)
 
     def step(strip, carry):
-        slot = lax.rem(strip, 2)
-
-        @pl.when(strip + 1 < strips)
+        slot = lax.rem(strip, SLOTS)
+
+        @pl.when(strip + SLOTS - 1 < strips)
         def _():
-            for copy in copies(strip + 1, 1 - slot):
+            for copy in copies(strip + SLOTS - 1, lax.rem(strip + SLOTS - 1, SLOTS)):
                 copy.start()
 
         for copy in copies(strip, slot):
             copy.wait()
-        base = pl.multiple_of(strip * LANES * ROWS, LANES * ROWS)
-
-        def rows(index):
-            return pl.ds(base + index, LANES, stride=ROWS)
-
-        for q in range(row_count):
-            tile = slab[slot, LANES * q : LANES * (q + 1), :].astype(jnp.float32)
-            fa[LANES * q : LANES * (q + 1), :] = tile * tile * 0.5
-            r_ref[rows(q), :] = tile.T
-        for q in range(row_count, ROWS):
-            r_ref[rows(q), :] = zero_tile
+
+        def samples(index):
+            if HALF * (index + 1) <= total:
+                return slab[slot, HALF * index : HALF * (index + 1), :].astype(jnp.float32)
+            return zero_half
+
+        for index in range(total // HALF):
+            value = samples(index)
+            fa[HALF * index : HALF * (index + 1), :] = value * value * 0.5
+        for parity in range(2):
+            for q in range(total // LANES):
+                index = 2 * q + parity
+                tile = jnp.concatenate([samples(index), samples(index + length // HALF)], axis=0)
+                stage[pl.ds(ROWS * parity + q, LANES, stride=STAGE_ROWS), :] = tile.T
+        base = pl.multiple_of(strip * LANES * double, LANES * double)
+        for item in range(LANES):
+            rows = stage[STAGE_ROWS * item : STAGE_ROWS * item + double, :]
+            w_ref[pl.ds(base + double * item, double), :] = rows.astype(jnp.bfloat16)
         windowed(fa, fb, (1, 2, 3), total)
         windowed(fb, fa, (4,), total)
         windowed(fa, fb, (8, 16, 24), total)
@@ -76,36 +88,34 @@
                 return fb[HALF * index : HALF * (index + 1), :]
             return zero_half
 
+        base = strip * (LANES * norm_rows)
         for parity in range(2):
             for q in range(lag_rows + 1 - parity):
                 pair = (half_block(2 * q + parity), half_block(2 * q + parity - 1))
-                g_ref[parity, rows(1 + q), :] = jnp.concatenate(pair, axis=0).T
+                rows = pl.ds(base + 1 + q, LANES, stride=norm_rows)
+                g_ref[parity, rows, :] = jnp.concatenate(pair, axis=0).T
         return carry
 
     lax.fori_loop(0, strips, step, 0)
 
 
-def stack_templates(sensor, scale, x_ref, r_ref, g_ref, o_ref, sc, chan_count, lag_rows):
+def stack_templates(sensor, scale, x_ref, w_ref, g_ref, o_ref, sc, first_k, count, chan_count, lag_rows):
     shift = lax.broadcasted_iota(jnp.int32, (HALF, LANES), 0) + 1
     lane = lax.broadcasted_iota(jnp.int32, (HALF, LANES), 1)
     upper = (lane < HALF) & (lane >= shift)
     zero = jnp.zeros((HALF, LANES), jnp.float32)
     zero_narrow = jnp.zeros((HALF, LANES), jnp.bfloat16)
-    low = lax.broadcasted_iota(jnp.int32, (ROWS, LANES), 1) < HALF
     low_out = lax.broadcasted_iota(jnp.int32, (lag_rows, LANES), 1) < HALF
 
-    def one(k, carry):
+    def one(step, carry):
+        k = first_k + step
         first = [jnp.zeros((ROWS, LANES), jnp.float32) for _ in range(2)]
         second = [jnp.zeros((ROWS, LANES), jnp.float32) for _ in range(2)]
         for c in range(chan_count):
             item = k * chan_count + c
             factor = scale[item]
-            base = pl.multiple_of(sensor[item] * ROWS, ROWS)
-            here = r_ref[pl.ds(base, ROWS), :]
-            later = r_ref[pl.ds(base + 2, ROWS), :]
-            even = jnp.where(low, here, pltpu.roll(later, HALF, 1))
-            odd = jnp.where(low, pltpu.roll(here, HALF, 1), later)
-            windows = jnp.concatenate([even, odd], axis=0).astype(jnp.bfloat16)
+            base = sensor[item] * (lag_rows + 3)
+            windows = w_ref[pl.ds(pl.multiple_of(sensor[item] * 2 * ROWS, 2 * ROWS), 2 * ROWS), :]
             lead = jnp.broadcast_to(x_ref[k, 2 * c : 2 * c + 1, :], (HALF, LANES))
             tail = jnp.broadcast_to(x_ref[k, 2 * c + 1 : 2 * c + 2, :], (HALF, LANES))
             lead = pltpu.roll(lead, 1, 1, stride=1, stride_axis=0)
@@ -138,40 +148,60 @@
         )
         return carry
 
-    lax.fori_loop(0, o_ref.shape[0] // lag_rows, one, 0, unroll=4)
-
-
-def matched_stacks(sensor, scale, place, taps, pieces, block, length):
+    lax.fori_loop(0, count, one, 0, unroll=4)
+
+
+def matched_stacks(sensor, scale, place, taps, pieces, block, length, layers):
     sensor_count = pieces[0].shape[1]
     count, double, _ = taps.shape
     lag_rows = block // LANES
     total = block + length
     held = block + 2 * pieces[0].shape[0]
     piece_count = len(pieces)
-
-    def kernel(sensor, scale, place, x_ref, *refs):
+    part = count // layers
+
+    def kernel(sensor, scale, place, x_hbm, *refs):
         ins = refs[:piece_count]
-        o_ref, r_ref, g_ref, slab, fa, fb, sc, sem = refs[piece_count:]
-        prepare_tables(place, ins, slab, fa, fb, sem, r_ref, g_ref, block, length)
-        stack_templates(sensor, scale, x_ref, r_ref, g_ref, o_ref, sc, double // 2, lag_rows)
-
-    single = pl.Buffered(1)
+        out, x_ref, o_ref, w_ref, g_ref, slab, stage, fa, fb, sc, sem, side_sem = refs[piece_count:]
+        load = pltpu.make_async_copy(x_hbm, x_ref, side_sem.at[layers])
+        load.start()
+        prepare_tables(place, ins, slab, stage, fa, fb, sem, w_ref, g_ref, block, length)
+        load.wait()
+
+        def stores(q):
+            rows = pl.ds(pl.multiple_of(q * part * lag_rows, 8), part * lag_rows)
+            return pltpu.make_async_copy(o_ref.at[rows], out.at[rows], side_sem.at[q])
+
+        def chunk(q, carry):
+            stack_templates(
+                sensor, scale, x_ref, w_ref, g_ref, o_ref, sc, q * part, part, double // 2, lag_rows
+            )
+            stores(q).start()
+            return carry
+
+        lax.fori_loop(0, layers, chunk, 0)
+        for q in range(layers):
+            stores(q).wait()
+
     return pl.pallas_call(
         kernel,
         grid_spec=pltpu.PrefetchScalarGridSpec(
             num_scalar_prefetch=3,
             grid=(1,),
-            in_specs=[pl.BlockSpec(taps.shape, lambda i, *_: (0, 0, 0), pipeline_mode=single)]
-            + [pl.BlockSpec(memory_space=pl.ANY)] * piece_count,
-            out_specs=pl.BlockSpec((count * lag_rows, LANES), lambda i, *_: (0, 0), pipeline_mode=single),
+            in_specs=[pl.BlockSpec(memory_space=pl.ANY)] * (1 + piece_count),
+            out_specs=pl.BlockSpec(memory_space=pl.ANY),
             scratch_shapes=[
-                pltpu.VMEM((sensor_count * ROWS + 8, LANES), jnp.float32),
-                pltpu.VMEM((2, sensor_count * ROWS + 8, LANES), jnp.float32),
-                pltpu.VMEM((2, held, LANES), jnp.bfloat16),
+                pltpu.VMEM(taps.shape, jnp.float32),
+                pltpu.VMEM((count * lag_rows, LANES), jnp.float32),
+                pltpu.VMEM((sensor_count * 2 * ROWS, LANES), jnp.bfloat16),
+                pltpu.VMEM((2, sensor_count * (lag_rows + 3) + 8, LANES), jnp.float32),
+                pltpu.VMEM((SLOTS, held, LANES), jnp.bfloat16),
+                pltpu.VMEM((STAGE_ROWS * LANES, LANES), jnp.float32),
                 pltpu.VMEM((total + LANES, LANES), jnp.float32),
                 pltpu.VMEM((total + LANES, LANES), jnp.float32),
                 pltpu.VMEM((2, 2, ROWS, LANES), jnp.float32),
-                pltpu.SemaphoreType.DMA((2, piece_count)),
+                pltpu.SemaphoreType.DMA((SLOTS, piece_count)),
+                pltpu.SemaphoreType.DMA((layers + 1,)),
             ],
         ),
         out_shape=jax.ShapeDtypeStruct((count * lag_rows, LANES), jnp.float32),
@@ -250,7 +280,7 @@
     power = jnp.sum((wide * wide).reshape(count, chan_count, length), axis=2)
     scale = (math.sqrt(length / chan_count) / length) * lax.rsqrt(power / length + EPSILON)
 
-    stacks = matched_stacks(sensor, scale.reshape(-1), place, wide, pieces, block, length)
+    stacks = matched_stacks(sensor, scale.reshape(-1), place, wide, pieces, block, length, layers)
     parts = stacks.reshape(layers, per_dev * lag_rows, LANES)
     received = [parts[0]] + [flip(parts[q], GROUP * q) for q in range(1, layers)]
     ordered = []

time: 149 us -> 134 us (0.90)
  Pallas kernels: 67.2 us -> 52.2 us
    pallas_call x1, Pallas kernels: 67.2 us -> 52.2 us  [matched_stacks(): pl.pallas_call(kernel, grid_spec=pltpu.PrefetchScalarGridSpec(num_scalar_...]
  transfers between devices with their start and end apart: 17 -> 17, of which waited for: 6 -> 6; matrix products, arithmetic and copies ran while one was open for 10% -> 11% of each run, Pallas kernels for 0% -> 0%
where the time goes in v2:
time: 134 us; the launch traced here: 133 us
  Pallas kernels  52.2 us (39%)
  waiting for transfers between devices  42.5 us (32%)
  starting transfers between devices  18.8 us (14%)
  local copies, waits for them, and re-layouts  10 us (7%)
  other arithmetic  9.45 us (7%)
    pallas_call x1, Pallas kernels, matched_stacks(): pl.pallas_call(kernel, grid_spec=pltpu.PrefetchScalarGridSpec(num_scalar_...  52.2 us
    ppermute x16, waiting for transfers between devices, flip(): return lax.ppermute(value, 'sens', [(i, i ^ bits) for i in range(devices)])  29.2 us
    ppermute x16, starting transfers between devices, flip(): return lax.ppermute(value, 'sens', [(i, i ^ bits) for i in range(devices)])  17.6 us
    ppermute x1, waiting for transfers between devices, body(): lax.ppermute(lead, 'sens', [(i + GROUP, i) for i in range(devices - GROUP)])  13.3 us
  transfers between devices with their start and end apart: 17, of which 6 were waited for; matrix products, arithmetic and copies ran while one was open for 11% of the time, Pallas kernels for 0%

profile of v2, /device:TPU:0, one launch (start us, length us, event | category | flops | bytes accessed | tf_op | source)
XLA Modules:
  0.0 133.1 jit_solution(7022114352331286751)
XLA Ops:
  0.0 2.9 %collective-permute-start = (bf16[160,2048]{1,0:T(8,128)(2,1)}, bf16[160,2048]{1,0:T(8,128)(2,1)S(1)}, u32[]{:S(2)}, u32[]{:S(2)}) collective-permute-start(bf16[160,2048]{1,0:T(8,128)(2,1)} %refs_0_.1), channel_id=1, source_target_pairs={{0,2},{1,3},{2,0},{3,1},{4,6},{5,7},{6,4},{7,5},{8,10},{9,11},{10,... | collective-permute-start | bytes 1966088 | tf_op jit(solution)/shard_map/ppermute | solution.py:226
  2.9 1.5 %collective-permute-start.1 = (bf16[160,2048]{1,0:T(8,128)(2,1)}, bf16[160,2048]{1,0:T(8,128)(2,1)S(1)}, u32[]{:S(2)}, u32[]{:S(2)}) collective-permute-start(bf16[160,2048]{1,0:T(8,128)(2,1)} %refs_0_.1), channel_id=1, source_target_pairs={{0,4},{1,5},{2,6},{3,7},{4,0},{5,1},{6,2},{7,3},{8,12},{9,13},{10,... | collective-permute-start | bytes 1966088 | tf_op jit(solution)/shard_map/ppermute | solution.py:226
  4.5 1.0 reshape.46
  5.5 0.8 rev.3
  6.3 0.7 convert_element_type.18
  7.2 0.7 convert_element_type.20
  8.2 3.6 %collective-permute-start.4 = (bf16[1040,128]{1,0:T(8,128)(2,1)S(1)}, bf16[1040,128]{1,0:T(8,128)(2,1)S(1)}, u32[]{:S(2)}, u32[]{:S(2)}) collective-permute-start(bf16[1040,128]{1,0:T(8,128)(2,1)S(1)} %concatenate.9), channel_id=1, source_target_pairs={{0,24},{1,25},{2,26},{3,27},{4,28},{5,29},{6,30},{7,31},{8,16},{9,... | collective-permute-start | bytes 798728 | tf_op jit(solution)/shard_map/ppermute | solution.py:226
  11.8 0.8 collective-permute-start.6
  12.6 5.3 %collective-permute-done.refs_1_ = bf16[160,2048]{1,0:T(8,128)(2,1)S(1)} collective-permute-done((bf16[160,2048]{1,0:T(8,128)(2,1)}, bf16[160,2048]{1,0:T(8,128)(2,1)S(1)}, u32[]{:S(2)}, u32[]{:S(2)}) %collective-permute-start) | collective-permute-done | bytes 655392 | tf_op jit(solution)/shard_map/ppermute | solution.py:226
  18.0 0.8 slice.48
  18.8 1.7 %collective-permute-start.2 = (bf16[80,2048]{1,0:T(8,128)(2,1)}, bf16[80,2048]{1,0:T(8,128)(2,1)S(1)}, u32[]{:S(2)}, u32[]{:S(2)}) collective-permute-start(bf16[80,2048]{1,0:T(8,128)(2,1)} %slice.48), channel_id=1, source_target_pairs={{0,4},{1,5},{2,6},{3,7},{4,0},{5,1},{6,2},{7,3},{8,12},{9,13},{10,... | collective-permute-start | bytes 983048 | tf_op jit(solution)/shard_map/ppermute | solution.py:226
  20.5 0.8 slice.49
  21.3 1.5 %collective-permute-start.3 = (bf16[80,2048]{1,0:T(8,128)(2,1)}, bf16[80,2048]{1,0:T(8,128)(2,1)}, u32[]{:S(2)}, u32[]{:S(2)}) collective-permute-start(bf16[80,2048]{1,0:T(8,128)(2,1)} %slice.49), channel_id=1, source_target_pairs={{0,2},{1,3},{2,0},{3,1},{4,6},{5,7},{6,4},{7,5},{8,10},{9,11},{10,... | collective-permute-start | bytes 983048 | tf_op jit(solution)/shard_map/ppermute | solution.py:226
  22.8 11.2 %collective-permute-done.5 = bf16[1040,128]{1,0:T(8,128)(2,1)S(1)} collective-permute-done((bf16[1040,128]{1,0:T(8,128)(2,1)S(1)}, bf16[1040,128]{1,0:T(8,128)(2,1)S(1)}, u32[]{:S(2)}, u32[]{:S(2)}) %collective-permute-start.5) | collective-permute-done | bytes 266272 | tf_op jit(solution)/shard_map/ppermute | solution.py:226
  35.0 2.2 %fusion.2 = bf16[160,2048]{1,0:T(8,128)(2,1)} fusion(bf16[160,2048]{1,0:T(8,128)(2,1)S(1)} %copy-done.2, bf16[160,2048]{1,0:T(8,128)(2,1)S(1)} %collective-permute-done.refs_1_, bf16[160,2048]{1,0:T(8,128)(2,1)S(1)} %collective-permute-done.1.refs_2_, bf16[80,2048]{1,0:T(8,128)(2,1)} %collective-permute-done.3.refs_7_, ...), kind=kLoop, calls=%fused_computation.6 | loop fusion | flops 2293760 | bytes 3276803 | tf_op jit(solution)/shard_map/jit(_where)/select_n | solution.py:254
  37.2 0.8 collective-permute-done.9.refs_5_
  38.1 0.8 copy-done.6
  38.8 0.8 copy-done.7
  39.6 1.3 collective-permute-start.12
  41.5 1.5 %fusion.3 = f32[4,1024,128]{2,1,0:T(8,128)} fusion(bf16[1,1040,128]{2,1,0:T(8,128)(2,1)S(1)} %bitcast.22, bf16[1,1040,128]{2,1,0:T(8,128)(2,1)S(1)} %bitcast.25, bf16[1,1040,128]{2,1,0:T(8,128)(2,1)S(1)} %bitcast.28, bf16[1,1040,128]{2,1,0:T(8,128)(2,1)S(1)} %bitcast.19), kind=kLoop, calls=%fused_computation.18 | loop fusion | flops 4718592 | bytes 3162112 | tf_op jit(solution)/shard_map/mul | solution.py:280
  43.0 1.9 %mul.58 = f32[128,16,256]{2,1,0:T(8,128)S(1)} reshape(f32[4,1024,128]{2,1,0:T(8,128)} %fusion.3) | data formatting | bytes 4194304 | tf_op jit(solution)/shard_map/mul | solution.py:280
  45.3 13.3 %collective-permute-done.12.refs_10_ = bf16[160,2048]{1,0:T(8,128)(2,1)} collective-permute-done((bf16[160,2048]{1,0:T(8,128)(2,1)}, bf16[160,2048]{1,0:T(8,128)(2,1)}, u32[]{:S(2)}, u32[]{:S(2)}) %collective-permute-start.12) | collective-permute-done | bytes 655392 | tf_op jit(solution)/shard_map/ppermute | solution.py:262
  58.7 0.7 mul.61.scale
  59.3 1.5 %fusion = f32[4,1024,128]{2,1,0:T(8,128)} fusion(bf16[1,1040,128]{2,1,0:T(8,128)(2,1)S(1)} %bitcast.24, bf16[1,1040,128]{2,1,0:T(8,128)(2,1)S(1)} %bitcast.27, bf16[1,1040,128]{2,1,0:T(8,128)(2,1)S(1)} %bitcast.30, bf16[1,1040,128]{2,1,0:T(8,128)(2,1)S(1)} %bitcast.21), kind=kLoop, calls=%fused_computation.1 | loop fusion | flops 4194304 | bytes 3162112 | tf_op jit(solution)/shard_map/convert_element_type | solution.py:277
  61.5 52.2 %shard_map.46 = f32[1280,128]{1,0:T(8,128)} custom-call(s32[2048]{0:T(1024)} %bitcast.31, f32[2048]{0:T(1024)} %mul.61.scale, s32[12]{0:T(128)} %stack.71.place, f32[128,32,128]{2,1,0:T(8,128)} %bitcast.18, bf16[160,2048]{1,0:T(8,128)(2,1)} %refs_0_.1, bf16[160,2048]{1,0:T(8,128)(2,1)} %copy-done, bf16[160,2048]{1,0:T(8,128)(2,1)} %copy-done.1, ...), custom_call_target="tpu_custom_call" | custom-call | tf_op jit(solution)/shard_map/pallas_call | solution.py:186
  113.6 1.1 fusion.4
  114.8 1.1 collective-permute-start.15
  115.9 3.3 %collective-permute-start.16 = (f32[320,128]{1,0:T(8,128)S(1)}, f32[320,128]{1,0:T(8,128)S(1)}, u32[]{:S(2)}, u32[]{:S(2)}) collective-permute-start(f32[320,128]{1,0:T(8,128)S(1)} %get-tuple-element.28), channel_id=1, source_target_pairs={{0,8},{1,9},{2,10},{3,11},{4,12},{5,13},{6,14},{7,15},{8,0},{9,1},... | collective-permute-start | bytes 491528 | tf_op jit(solution)/shard_map/ppermute | solution.py:226
  119.2 4.5 %collective-permute-done.14 = f32[320,128]{1,0:T(8,128)S(1)} collective-permute-done((f32[320,128]{1,0:T(8,128)S(1)}, f32[320,128]{1,0:T(8,128)S(1)}, u32[]{:S(2)}, u32[]{:S(2)}) %collective-permute-start.14) | collective-permute-done | bytes 163872 | tf_op jit(solution)/shard_map/ppermute | solution.py:226
  123.8 7.3 %collective-permute-done.15 = f32[320,128]{1,0:T(8,128)S(1)} collective-permute-done((f32[320,128]{1,0:T(8,128)S(1)}, f32[320,128]{1,0:T(8,128)S(1)}, u32[]{:S(2)}, u32[]{:S(2)}) %collective-permute-start.15) | collective-permute-done | bytes 163872 | tf_op jit(solution)/shard_map/ppermute | solution.py:226
  131.1 1.0 select_select_fusion.3
  132.2 0.9 pad_maximum_fusion.3
  (50 shorter events, 3.5 us)
Async XLA Ops:
  0.0 22.8 %copy-start.2 = (bf16[160,2048]{1,0:T(8,128)(2,1)S(1)}, bf16[160,2048]{1,0:T(8,128)(2,1)}, u32[]{:S(2)}) copy-start(bf16[160,2048]{1,0:T(8,128)(2,1)} %refs_0_.1) | copy-start | bytes 1966084
  0.0 17.9 %collective-permute-start = (bf16[160,2048]{1,0:T(8,128)(2,1)}, bf16[160,2048]{1,0:T(8,128)(2,1)S(1)}, u32[]{:S(2)}, u32[]{:S(2)}) collective-permute-start(bf16[160,2048]{1,0:T(8,128)(2,1)} %refs_0_.1), channel_id=1, source_target_pairs={{0,2},{1,3},{2,0},{3,1},{4,6},{5,7},{6,4},{7,5},{8,10},{9,11},{10,... | collective-permute-start | bytes 1966088 | tf_op jit(solution)/shard_map/ppermute | solution.py:226
  2.9 17.5 %collective-permute-start.1 = (bf16[160,2048]{1,0:T(8,128)(2,1)}, bf16[160,2048]{1,0:T(8,128)(2,1)S(1)}, u32[]{:S(2)}, u32[]{:S(2)}) collective-permute-start(bf16[160,2048]{1,0:T(8,128)(2,1)} %refs_0_.1), channel_id=1, source_target_pairs={{0,4},{1,5},{2,6},{3,7},{4,0},{5,1},{6,2},{7,3},{8,12},{9,13},{10,... | collective-permute-start | bytes 1966088 | tf_op jit(solution)/shard_map/ppermute | solution.py:226
  8.2 14.6 %collective-permute-start.4 = (bf16[1040,128]{1,0:T(8,128)(2,1)S(1)}, bf16[1040,128]{1,0:T(8,128)(2,1)S(1)}, u32[]{:S(2)}, u32[]{:S(2)}) collective-permute-start(bf16[1040,128]{1,0:T(8,128)(2,1)S(1)} %concatenate.9), channel_id=1, source_target_pairs={{0,24},{1,25},{2,26},{3,27},{4,28},{5,29},{6,30},{7,31},{8,16},{9,... | collective-permute-start | bytes 798728 | tf_op jit(solution)/shard_map/ppermute | solution.py:226
  11.8 22.1 %collective-permute-start.5 = (bf16[1040,128]{1,0:T(8,128)(2,1)S(1)}, bf16[1040,128]{1,0:T(8,128)(2,1)S(1)}, u32[]{:S(2)}, u32[]{:S(2)}) collective-permute-start(bf16[1040,128]{1,0:T(8,128)(2,1)S(1)} %concatenate.9), channel_id=1, source_target_pairs={{0,16},{1,17},{2,18},{3,19},{4,20},{5,21},{6,22},{7,23},{8,24},{9,... | collective-permute-start | bytes 798728 | tf_op jit(solution)/shard_map/ppermute | solution.py:226
  11.8 22.1 %collective-permute-start.6 = (bf16[1040,128]{1,0:T(8,128)(2,1)S(1)}, bf16[1040,128]{1,0:T(8,128)(2,1)S(1)}, u32[]{:S(2)}, u32[]{:S(2)}) collective-permute-start(bf16[1040,128]{1,0:T(8,128)(2,1)S(1)} %concatenate.9), channel_id=1, source_target_pairs={{0,8},{1,9},{2,10},{3,11},{4,12},{5,13},{6,14},{7,15},{8,0},{9,1},... | collective-permute-start | bytes 798728 | tf_op jit(solution)/shard_map/ppermute | solution.py:226
  18.0 19.3 %copy-start = (bf16[160,2048]{1,0:T(8,128)(2,1)}, bf16[160,2048]{1,0:T(8,128)(2,1)S(1)}, u32[]{:S(2)}) copy-start(bf16[160,2048]{1,0:T(8,128)(2,1)S(1)} %collective-permute-done.refs_1_) | copy-start | bytes 1966084
  18.8 15.7 %collective-permute-start.2 = (bf16[80,2048]{1,0:T(8,128)(2,1)}, bf16[80,2048]{1,0:T(8,128)(2,1)S(1)}, u32[]{:S(2)}, u32[]{:S(2)}) collective-permute-start(bf16[80,2048]{1,0:T(8,128)(2,1)} %slice.48), channel_id=1, source_target_pairs={{0,4},{1,5},{2,6},{3,7},{4,0},{5,1},{6,2},{7,3},{8,12},{9,13},{10,... | collective-permute-start | bytes 983048 | tf_op jit(solution)/shard_map/ppermute | solution.py:226
  20.5 21.0 %copy-start.1 = (bf16[160,2048]{1,0:T(8,128)(2,1)}, bf16[160,2048]{1,0:T(8,128)(2,1)S(1)}, u32[]{:S(2)}) copy-start(bf16[160,2048]{1,0:T(8,128)(2,1)S(1)} %collective-permute-done.1.refs_2_) | copy-start | bytes 1966084
  21.3 13.3 %collective-permute-start.3 = (bf16[80,2048]{1,0:T(8,128)(2,1)}, bf16[80,2048]{1,0:T(8,128)(2,1)}, u32[]{:S(2)}, u32[]{:S(2)}) collective-permute-start(bf16[80,2048]{1,0:T(8,128)(2,1)} %slice.49), channel_id=1, source_target_pairs={{0,2},{1,3},{2,0},{3,1},{4,6},{5,7},{6,4},{7,5},{8,10},{9,11},{10,... | collective-permute-start | bytes 983048 | tf_op jit(solution)/shard_map/ppermute | solution.py:226
  22.8 14.4 %collective-permute-start.7 = (bf16[160,2048]{1,0:T(8,128)(2,1)S(1)}, bf16[160,2048]{1,0:T(8,128)(2,1)}, u32[]{:S(2)}, u32[]{:S(2)}) collective-permute-start(bf16[160,2048]{1,0:T(8,128)(2,1)S(1)} %copy-done.2), channel_id=1, source_target_pairs={{0,1},{1,0},{2,3},{3,2},{4,5},{5,4},{6,7},{7,6},{8,9},{9,8},{10,11... | collective-permute-start | bytes 1966088 | tf_op jit(solution)/shard_map/ppermute | solution.py:226
  33.9 3.3 %collective-permute-start.8 = (bf16[160,2048]{1,0:T(8,128)(2,1)S(1)}, bf16[160,2048]{1,0:T(8,128)(2,1)}, u32[]{:S(2)}, u32[]{:S(2)}) collective-permute-start(bf16[160,2048]{1,0:T(8,128)(2,1)S(1)} %collective-permute-done.refs_1_), channel_id=1, source_target_pairs={{0,1},{1,0},{2,3},{3,2},{4,5},{5,4},{6,7},{7,6},{8,9},{9,8},{10,11... | collective-permute-start | bytes 1966088 | tf_op jit(solution)/shard_map/ppermute | solution.py:226
  34.0 7.5 %copy-start.3 = (bf16[1040,128]{1,0:T(8,128)(2,1)}, bf16[1040,128]{1,0:T(8,128)(2,1)S(1)}, u32[]{:S(2)}) copy-start(bf16[1040,128]{1,0:T(8,128)(2,1)S(1)} %collective-permute-done.6) | copy-start | bytes 798724
  34.0 4.1 %collective-permute-start.9 = (bf16[160,2048]{1,0:T(8,128)(2,1)S(1)}, bf16[160,2048]{1,0:T(8,128)(2,1)}, u32[]{:S(2)}, u32[]{:S(2)}) collective-permute-start(bf16[160,2048]{1,0:T(8,128)(2,1)S(1)} %collective-permute-done.1.refs_2_), channel_id=1, source_target_pairs={{0,1},{1,0},{2,3},{3,2},{4,5},{5,4},{6,7},{7,6},{8,9},{9,8},{10,11... | collective-permute-start | bytes 1966088 | tf_op jit(solution)/shard_map/ppermute | solution.py:226
  34.5 7.0 %copy-start.5 = (bf16[80,2048]{1,0:T(8,128)(2,1)}, bf16[80,2048]{1,0:T(8,128)(2,1)S(1)}, u32[]{:S(2)}) copy-start(bf16[80,2048]{1,0:T(8,128)(2,1)S(1)} %collective-permute-done.2.refs_6_) | copy-start | bytes 983044
  34.5 3.6 %collective-permute-start.10 = (bf16[80,2048]{1,0:T(8,128)(2,1)S(1)}, bf16[80,2048]{1,0:T(8,128)(2,1)S(1)}, u32[]{:S(2)}, u32[]{:S(2)}) collective-permute-start(bf16[80,2048]{1,0:T(8,128)(2,1)S(1)} %collective-permute-done.2.refs_6_), channel_id=1, source_target_pairs={{0,1},{1,0},{2,3},{3,2},{4,5},{5,4},{6,7},{7,6},{8,9},{9,8},{10,11... | collective-permute-start | bytes 983048 | tf_op jit(solution)/shard_map/ppermute | solution.py:226
  34.6 4.2 %collective-permute-start.11 = (bf16[80,2048]{1,0:T(8,128)(2,1)}, bf16[80,2048]{1,0:T(8,128)(2,1)S(1)}, u32[]{:S(2)}, u32[]{:S(2)}) collective-permute-start(bf16[80,2048]{1,0:T(8,128)(2,1)} %collective-permute-done.3.refs_7_), channel_id=1, source_target_pairs={{0,1},{1,0},{2,3},{3,2},{4,5},{5,4},{6,7},{7,6},{8,9},{9,8},{10,11... | collective-permute-start | bytes 983048 | tf_op jit(solution)/shard_map/ppermute | solution.py:226
  38.1 0.8 copy-start.6
  38.8 0.8 copy-start.7
  39.6 19.0 %collective-permute-start.12 = (bf16[160,2048]{1,0:T(8,128)(2,1)}, bf16[160,2048]{1,0:T(8,128)(2,1)}, u32[]{:S(2)}, u32[]{:S(2)}) collective-permute-start(bf16[160,2048]{1,0:T(8,128)(2,1)} %fusion.2), channel_id=1, source_target_pairs={{8,0},{9,1},{10,2},{11,3},{12,4},{13,5},{14,6},{15,7},{16,8},{17,9... | collective-permute-start | bytes 1966088 | tf_op jit(solution)/shard_map/ppermute | solution.py:262
  44.9 14.5 %copy-start.4 = (bf16[1040,128]{1,0:T(8,128)(2,1)S(1)}, bf16[1040,128]{1,0:T(8,128)(2,1)}, u32[]{:S(2)}) copy-start(bf16[1040,128]{1,0:T(8,128)(2,1)} %copy-done.3) | copy-start | bytes 798724
  58.5 2.9 %collective-permute-start.13 = (bf16[160,2048]{1,0:T(8,128)(2,1)}, bf16[160,2048]{1,0:T(8,128)(2,1)}, u32[]{:S(2)}, u32[]{:S(2)}) collective-permute-start(bf16[160,2048]{1,0:T(8,128)(2,1)} %collective-permute-done.12.refs_10_), channel_id=1, source_target_pairs={{0,1},{1,0},{2,3},{3,2},{4,5},{5,4},{6,7},{7,6},{8,9},{9,8},{10,11... | collective-permute-start | bytes 1966088 | tf_op jit(solution)/shard_map/ppermute | solution.py:226
  114.8 9.0 %collective-permute-start.14 = (f32[320,128]{1,0:T(8,128)S(1)}, f32[320,128]{1,0:T(8,128)S(1)}, u32[]{:S(2)}, u32[]{:S(2)}) collective-permute-start(f32[320,128]{1,0:T(8,128)S(1)} %get-tuple-element.27), channel_id=1, source_target_pairs={{0,24},{1,25},{2,26},{3,27},{4,28},{5,29},{6,30},{7,31},{8,16},{9,... | collective-permute-start | bytes 491528 | tf_op jit(solution)/shard_map/ppermute | solution.py:226
  114.8 16.3 %collective-permute-start.15 = (f32[320,128]{1,0:T(8,128)S(1)}, f32[320,128]{1,0:T(8,128)S(1)}, u32[]{:S(2)}, u32[]{:S(2)}) collective-permute-start(f32[320,128]{1,0:T(8,128)S(1)} %get-tuple-element.29), channel_id=1, source_target_pairs={{0,16},{1,17},{2,18},{3,19},{4,20},{5,21},{6,22},{7,23},{8,24},{9,... | collective-permute-start | bytes 491528 | tf_op jit(solution)/shard_map/ppermute | solution.py:226
  115.9 15.2 %collective-permute-start.16 = (f32[320,128]{1,0:T(8,128)S(1)}, f32[320,128]{1,0:T(8,128)S(1)}, u32[]{:S(2)}, u32[]{:S(2)}) collective-permute-start(f32[320,128]{1,0:T(8,128)S(1)} %get-tuple-element.28), channel_id=1, source_target_pairs={{0,8},{1,9},{2,10},{3,11},{4,12},{5,13},{6,14},{7,15},{8,0},{9,1},... | collective-permute-start | bytes 491528 | tf_op jit(solution)/shard_map/ppermute | solution.py:226

commit v3 on v1

v3 whole, which is shorter than its diff:
```python
import math

import jax
import jax.numpy as jnp
from jax import lax
from jax.experimental import pallas as pl
from jax.experimental.pallas import tpu as pltpu
from jax.sharding import PartitionSpec as P

EPSILON = 1e-05
LANES = 128
HALF = 64
ROWS = 16
GROUP = 8
SLOTS = 4
VMEM_LIMIT = 14 * 2**20
STAGE_ROWS = 33


def start_strip_copies(place, pieces, slab, sem, strip, slot):
    cols = pl.ds(pl.multiple_of(strip * LANES, LANES), LANES)
    made = []
    for i, piece in enumerate(pieces):
        rows = pl.ds(pl.multiple_of(place[i], 16), piece.shape[0])
        made.append(pltpu.make_async_copy(piece.at[:, cols], slab.at[slot, rows], sem.at[slot, i]))
    return made


def for_each_strip(place, pieces, slab, sem, work):
    strips = pieces[0].shape[1] // LANES
    for ahead in range(SLOTS - 1):
        for copy in start_strip_copies(place, pieces, slab, sem, ahead, ahead):
            copy.start()

    def step(strip, carry):
        slot = lax.rem(strip, SLOTS)
        coming = strip + SLOTS - 1

        @pl.when(coming < strips)
        def _():
            for copy in start_strip_copies(place, pieces, slab, sem, coming, lax.rem(coming, SLOTS)):
                copy.start()

        for copy in start_strip_copies(place, pieces, slab, sem, strip, slot):
            copy.wait()
        work(strip, slot)
        return carry

    lax.fori_loop(0, strips, step, 0)


def windowed(source, target, offsets, count):
    for start in range(0, count, HALF):
        value = source[start : start + HALF, :]
        for offset in offsets:
            value = value + source[start + offset : start + offset + HALF, :]
        target[start : start + HALF, :] = value


def table_part(strip, samples, stage, fa, fb, w_ref, g_ref, span, norms, rows, lag_rows, length):
    double = 2 * ROWS
    norm_rows = lag_rows + 3
    origin, limit = span
    first, last = rows
    for index in range(origin, limit):
        value = samples(index)
        at = HALF * (index - origin)
        fa[at : at + HALF, :] = value * value * 0.5
    for parity in range(2):
        for q in range(first, last):
            index = 2 * q + parity
            tile = jnp.concatenate([samples(index), samples(index + length // HALF)], axis=0)
            stage[pl.ds(ROWS * parity + q, LANES, stride=STAGE_ROWS), :] = tile.T
    base = pl.multiple_of(strip * LANES * double, LANES * double)
    top = min(ROWS, -(-last // 8) * 8)
    for item in range(LANES):
        for parity in range(2):
            low = ROWS * parity
            value = stage[STAGE_ROWS * item + low + first : STAGE_ROWS * item + low + top, :]
            target = pl.ds(base + double * item + low + first, top - first)
            w_ref[target, :] = value.astype(jnp.bfloat16)
    count = HALF * (limit - origin)
    windowed(fa, fb, (1, 2, 3), count)
    windowed(fb, fa, (4,), count)
    windowed(fa, fb, (8, 16, 24), count)
    windowed(fb, fa, (32, 64, 96), count - LANES)
    for index in range(*norms):
        at = HALF * (index - origin)
        energy_half = fa[at : at + HALF, :] + fa[at + LANES : at + LANES + HALF, :]
        fb[at : at + HALF, :] = lax.rsqrt(energy_half * (2.0 / length) + EPSILON)

    def norm_block(index):
        if norms[0] <= index < norms[1]:
            return fb[HALF * (index - origin) : HALF * (index - origin + 1), :]
        return jnp.zeros((HALF, LANES), jnp.float32)

    base = strip * (LANES * norm_rows)
    for parity in range(2):
        for q in range(first, min(last, lag_rows + 1 - parity)):
            pair = (norm_block(2 * q + parity), norm_block(2 * q + parity - 1))
            target = pl.ds(base + 1 + q, LANES, stride=norm_rows)
            g_ref[parity, target, :] = jnp.concatenate(pair, axis=0).T


def clear(stage):
    for start in range(0, LANES * STAGE_ROWS, LANES):
        stage[start : start + LANES, :] = jnp.zeros((LANES, LANES), jnp.float32)


def stack_templates(sensor, scale, x_ref, w_ref, g_ref, o_ref, sc, first, offset, chan_count, lag_rows):
    shift = lax.broadcasted_iota(jnp.int32, (HALF, LANES), 0) + 1
    lane = lax.broadcasted_iota(jnp.int32, (HALF, LANES), 1)
    upper = (lane < HALF) & (lane >= shift)
    zero = jnp.zeros((HALF, LANES), jnp.float32)
    zero_narrow = jnp.zeros((HALF, LANES), jnp.bfloat16)
    low_out = lax.broadcasted_iota(jnp.int32, (lag_rows, LANES), 1) < HALF

    def one(step, carry):
        k = offset + step
        leading = [jnp.zeros((ROWS, LANES), jnp.float32) for _ in range(2)]
        trailing = [jnp.zeros((ROWS, LANES), jnp.float32) for _ in range(2)]
        for c in range(chan_count):
            item = (first + step) * chan_count + c
            factor = scale[item]
            base = sensor[item] * (lag_rows + 3)
            windows = w_ref[pl.ds(pl.multiple_of(sensor[item] * 2 * ROWS, 2 * ROWS), 2 * ROWS), :]
            lead = jnp.broadcast_to(x_ref[k, 2 * c : 2 * c + 1, :], (HALF, LANES))
            tail = jnp.broadcast_to(x_ref[k, 2 * c + 1 : 2 * c + 2, :], (HALF, LANES))
            lead = pltpu.roll(lead, 1, 1, stride=1, stride_axis=0)
            tail = pltpu.roll(tail, 1, 1, stride=1, stride_axis=0)
            t01 = jnp.where(upper, zero, lead).astype(jnp.bfloat16)
            t23 = jnp.where(upper, lead, tail).astype(jnp.bfloat16)
            t4 = jnp.where(upper, tail, zero).astype(jnp.bfloat16)
            taps = jnp.concatenate(
                [
                    jnp.concatenate([t01, t23], axis=1),
                    jnp.concatenate([t4, zero_narrow], axis=1),
                ],
                axis=0,
            )
            corr = lax.dot_general(
                windows, taps, (((1,), (0,)), ((), ())), preferred_element_type=jnp.float32
            )
            for p in range(2):
                part = corr[ROWS * p : ROWS * (p + 1)]
                leading[p] = leading[p] + part[:, :LANES] * g_ref[p, pl.ds(base + 1, ROWS), :] * factor
                trailing[p] = trailing[p] + part[:, LANES:] * g_ref[p, pl.ds(base, ROWS), :] * factor
        for p in range(2):
            sc[p, 0] = leading[p]
            sc[p, 1] = trailing[p]
        w0 = sc[0, 0, 0:lag_rows] + sc[0, 1, 1 : 1 + lag_rows]
        w0_next = sc[0, 0, 1 : 1 + lag_rows] + sc[0, 1, 2 : 2 + lag_rows]
        w1 = sc[1, 0, 0:lag_rows] + sc[1, 1, 1 : 1 + lag_rows]
        o_ref[pl.ds(step * lag_rows, lag_rows), :] = jnp.where(low_out, w0, w0_next) + pltpu.roll(
            w1, HALF, 1
        )
        return carry

    lax.fori_loop(0, o_ref.shape[0] // lag_rows, one, 0, unroll=4)


def in_vmem(value):
    return pltpu.with_memory_space_constraint(value, pltpu.VMEM)


def cost(microseconds):
    return pl.CostEstimate(
        flops=int(microseconds * 1e9), bytes_accessed=int(microseconds * 1e6), transcendentals=0
    )


def early_tables(place, pieces, block, length):
    sensor_count = pieces[0].shape[1]
    strips = sensor_count // LANES
    lag_rows = block // LANES
    local = (block - length) // HALF
    kept = block - HALF * (local - 1)
    piece_count = len(pieces)

    def kernel(place, *refs):
        ins = refs[:piece_count]
        w_ref, g_ref, tail_ref, slab, stage, fa, fb, sem = refs[piece_count:]
        clear(stage)

        def work(strip, slot):
            def samples(index):
                return slab[slot, HALF * index : HALF * (index + 1), :].astype(jnp.float32)

            tail_ref[strip] = slab[slot, block - kept : block, :]
            table_part(
                strip, samples, stage, fa, fb, w_ref, g_ref,
                (0, block // HALF), (0, local), (0, local // 2), lag_rows, length,
            )

        for_each_strip(place, ins, slab, sem, work)

    whole = pl.BlockSpec(memory_space=pltpu.VMEM)
    return pl.pallas_call(
        kernel,
        grid_spec=pltpu.PrefetchScalarGridSpec(
            num_scalar_prefetch=1,
            grid=(),
            in_specs=[pl.BlockSpec(memory_space=pl.ANY)] * piece_count,
            out_specs=(whole, whole, whole),
            scratch_shapes=[
                pltpu.VMEM((SLOTS, block, LANES), jnp.bfloat16),
                pltpu.VMEM((STAGE_ROWS * LANES, LANES), jnp.float32),
                pltpu.VMEM((block + LANES, LANES), jnp.float32),
                pltpu.VMEM((block + LANES, LANES), jnp.float32),
                pltpu.SemaphoreType.DMA((SLOTS, piece_count)),
            ],
        ),
        out_shape=(
            pltpu.VMEM((sensor_count * 2 * ROWS, LANES), jnp.bfloat16),
            pltpu.VMEM((2, sensor_count * (lag_rows + 3) + 8, LANES), jnp.float32),
            pltpu.VMEM((strips, kept, LANES), jnp.bfloat16),
        ),
        compiler_params=pltpu.CompilerParams(vmem_limit_bytes=VMEM_LIMIT),
    )(place, *pieces)


def late_tables(place, pieces, early, block, length):
    lag_rows = block // LANES
    local = (block - length) // HALF
    total = (block + length) // HALF
    inside = block // HALF
    piece_count = len(pieces)

    def kernel(place, tail_ref, w_in, g_in, *refs):
        ins = refs[:piece_count]
        w_ref, g_ref, slab, stage, fa, fb, sem = refs[piece_count:]
        clear(stage)

        def work(strip, slot):
            def samples(index):
                if index < inside:
                    at = HALF * (index - local + 1)
                    return tail_ref[strip, at : at + HALF, :].astype(jnp.float32)
                if index < total:
                    at = HALF * (index - inside)
                    return slab[slot, at : at + HALF, :].astype(jnp.float32)
                return jnp.zeros((HALF, LANES), jnp.float32)

            table_part(
                strip, samples, stage, fa, fb, w_ref, g_ref,
                (local - 1, total), (local - 1, inside), (local // 2, total // 2), lag_rows, length,
            )

        for_each_strip(place, ins, slab, sem, work)

    whole = pl.BlockSpec(memory_space=pltpu.VMEM)
    span = HALF * (total - local + 1)
    return pl.pallas_call(
        kernel,
        grid_spec=pltpu.PrefetchScalarGridSpec(
            num_scalar_prefetch=1,
            grid=(),
            in_specs=[whole, whole, whole] + [pl.BlockSpec(memory_space=pl.ANY)] * piece_count,
            out_specs=(whole, whole),
            scratch_shapes=[
                pltpu.VMEM((SLOTS, 2 * pieces[0].shape[0], LANES), jnp.bfloat16),
                pltpu.VMEM((STAGE_ROWS * LANES, LANES), jnp.float32),
                pltpu.VMEM((span + LANES, LANES), jnp.float32),
                pltpu.VMEM((span + LANES, LANES), jnp.float32),
                pltpu.SemaphoreType.DMA((SLOTS, piece_count)),
            ],
        ),
        out_shape=(
            pltpu.VMEM(early[0].shape, early[0].dtype),
            pltpu.VMEM(early[1].shape, early[1].dtype),
        ),
        input_output_aliases={2: 0, 3: 1},
        compiler_params=pltpu.CompilerParams(vmem_limit_bytes=VMEM_LIMIT),
    )(place, in_vmem(early[2]), in_vmem(early[0]), in_vmem(early[1]), *pieces)


def matched_stacks(sensor, scale, taps, tables, per_dev, lag_rows):
    count, double, _ = taps.shape
    number = count // per_dev

    def kernel(sensor, scale, x_ref, w_ref, g_ref, *refs):
        for i in range(number):
            stack_templates(
                sensor, scale, x_ref, w_ref, g_ref, refs[i], refs[number],
                i * per_dev, i * per_dev, double // 2, lag_rows,
            )

    whole = pl.BlockSpec(memory_space=pltpu.VMEM)
    return pl.pallas_call(
        kernel,
        grid_spec=pltpu.PrefetchScalarGridSpec(
            num_scalar_prefetch=2,
            grid=(),
            in_specs=[whole, whole, whole],
            out_specs=[whole] * number,
            scratch_shapes=[pltpu.VMEM((2, 2, ROWS, LANES), jnp.float32)],
        ),
        out_shape=[jax.ShapeDtypeStruct((per_dev * lag_rows, LANES), jnp.float32)] * number,
        compiler_params=pltpu.CompilerParams(vmem_limit_bytes=VMEM_LIMIT),
        cost_estimate=cost(8 * number),
    )(sensor, scale, taps, in_vmem(tables[0]), in_vmem(tables[1]))


def body(data, templates, cover, channel):
    devices = lax.axis_size("sens")
    layers = devices // GROUP
    per_dev, chan_count, length = templates.shape
    share, sensor_count = data.shape
    sensors_per_group = sensor_count // devices
    block = share * GROUP
    lag_rows = block // LANES
    lag_count = share * devices - length
    half = share // 2
    me = lax.axis_index("sens")
    layer, inner = me // GROUP, me % GROUP

    def flip(value, bits):
        return lax.ppermute(value, "sens", [(i, i ^ bits) for i in range(devices)])

    item_rows = per_dev * 2 * chan_count
    id_rows = per_dev * chan_count // LANES
    reversed_halves = templates.reshape(item_rows, LANES)[:, ::-1]
    pad_rows = -(item_rows + 2 * id_rows) % 16
    packet = jnp.concatenate(
        [
            reversed_halves,
            cover.reshape(id_rows, LANES).astype(jnp.bfloat16),
            channel.reshape(id_rows, LANES).astype(jnp.bfloat16),
            jnp.zeros((pad_rows, LANES), jnp.bfloat16),
        ],
        axis=0,
    )

    near = flip(data, 2)
    side = flip(data, 4)
    packets = [flip(packet, GROUP * q) for q in reversed(range(1, layers))]
    twin = flip(data, 1)
    far_low = flip(near[:half], 4)
    far_high = flip(side[half:], 2)
    near_twin = flip(near, 1)
    side_twin = flip(side, 1)
    far_low_twin = flip(far_low, 1)
    far_high_twin = flip(far_high, 1)
    far = jnp.concatenate([far_low, far_high], axis=0)
    chip = inner // 2
    lead = jnp.where(
        chip == 0, data, jnp.where(chip == 1, near, jnp.where(chip == 2, side, far))
    )
    held = lax.optimization_barrier(
        (lead, *packets, twin, near_twin, side_twin, far_low_twin, far_high_twin)
    )
    lead, packets = held[0], [packet] + list(held[1:layers][::-1])
    twin, near_twin, side_twin, far_low_twin, far_high_twin = held[layers:]
    halo = lax.ppermute(lead, "sens", [(i + GROUP, i) for i in range(devices - GROUP)])
    halo_twin = flip(halo, 1)
    pieces = [
        data, near, side, twin, near_twin, side_twin,
        far_low, far_high, far_low_twin, far_high_twin,
    ]
    core = inner % 2
    starts = [share * (inner ^ r) for r in (0, 2, 4, 1, 3, 5)]
    starts += [share * (inner ^ 6), share * (inner ^ 6) + half]
    starts += [share * (inner ^ 7), share * (inner ^ 7) + half]
    place = jnp.stack(starts).astype(jnp.int32)
    halo_place = jnp.stack([share * core, share * (1 - core)]).astype(jnp.int32)
    early = early_tables(place, pieces, block, length)
    tables = late_tables(halo_place, [halo, halo_twin], early, block, length)
    gain = math.sqrt(length / chan_count) / length

    def stacks_of(relations):
        chosen = jnp.stack([packets[q] for q in relations])
        count = len(relations) * per_dev
        wide = chosen[:, :item_rows].astype(jnp.float32).reshape(count, 2 * chan_count, LANES)
        ids = chosen[:, item_rows : item_rows + 2 * id_rows].astype(jnp.int32)
        sensor = (ids[:, :id_rows] * sensors_per_group + ids[:, id_rows:]).reshape(-1)
        power = jnp.sum((wide * wide).reshape(count, chan_count, length), axis=2)
        scale = (gain * lax.rsqrt(power / length + EPSILON)).reshape(-1)
        return matched_stacks(sensor, scale, wide, tables, per_dev, lag_rows)

    far_parts = stacks_of(range(layers // 2, layers))
    received = [flip(far_parts[q - layers // 2], GROUP * q) for q in range(layers // 2, layers)]
    near_parts = [stacks_of([q])[0] for q in range(layers // 2)]
    received = [
        near_parts[q] if q == 0 else flip(near_parts[q], GROUP * q) for q in range(layers // 2)
    ] + received
    ordered = []
    for slot in range(layers):
        value = received[slot]
        for mine in range(1, layers):
            value = jnp.where(layer == mine, received[slot ^ mine], value)
        ordered.append(value.reshape(per_dev, block))
    return jnp.concatenate(ordered, axis=1)[:, :lag_count]


def solution(mesh):
    placed = (P(("parts", "sens"), None), P("sens", None, None), P("sens", None), P("sens", None))
    return jax.shard_map(
        body, mesh=mesh, in_specs=placed, out_specs=P(("parts", "sens"), None), check_vma=False
    )
```

time: 149 us -> 127 us (0.85)
  waiting for transfers between devices: 42.4 us -> 22.9 us
  other arithmetic: 9.45 us -> 14.8 us
  Pallas kernels: 67.2 us -> 62.9 us
  local copies, waits for them, and re-layouts: 10 us -> 7.39 us
    pallas_call x1 -> x3, Pallas kernels: 67.2 us -> 36.4 us  [matched_stacks(): pl.pallas_call(kernel, grid_spec=pltpu.PrefetchScalarGridSpec(num_scalar_...]
    pallas_call x0 -> x2, Pallas kernels: none -> 26.5 us  [the longest x1 17.1 us: early_tables(): pl.pallas_call(kernel, grid_spec=pltpu.PrefetchScalarGridSpec(num_scalar_...]
    ppermute x1, waiting for transfers between devices: 13.3 us -> 0.01 us  [body(): lax.ppermute(lead, 'sens', [(i + GROUP, i) for i in range(devices - GROUP)])]
    ppermute x16, waiting for transfers between devices: 29.2 us -> 22.9 us  [flip(): return lax.ppermute(value, 'sens', [(i, i ^ bits) for i in range(devices)])]
    convert_element_type x2 -> x6, other arithmetic: 1.51 us -> 6.09 us  [the longest x3 4.71 us: stacks_of(): chosen[:, :item_rows].astype(jnp.float32)]
  transfers between devices with their start and end apart: 17 -> 17, of which waited for: 6 -> 4; matrix products, arithmetic and copies ran while one was open for 10% -> 15% of each run, Pallas kernels for 0% -> 35%
where the time goes in v3:
time: 127 us; the launch traced here: 126 us
  Pallas kernels  62.9 us (50%)
  waiting for transfers between devices  22.9 us (18%)
  starting transfers between devices  18.3 us (14%)
  other arithmetic  14.8 us (12%)
  local copies, waits for them, and re-layouts  7.39 us (6%)
    pallas_call x3, Pallas kernels, matched_stacks(): pl.pallas_call(kernel, grid_spec=pltpu.PrefetchScalarGridSpec(num_scalar_...  36.4 us
    ppermute x16, waiting for transfers between devices, flip(): return lax.ppermute(value, 'sens', [(i, i ^ bits) for i in range(devices)])  22.9 us
    pallas_call x1, Pallas kernels, early_tables(): pl.pallas_call(kernel, grid_spec=pltpu.PrefetchScalarGridSpec(num_scalar_...  17.1 us
    ppermute x16, starting transfers between devices, flip(): return lax.ppermute(value, 'sens', [(i, i ^ bits) for i in range(devices)])  17 us
    pallas_call x1, Pallas kernels, late_tables(): pl.pallas_call(kernel, grid_spec=pltpu.PrefetchScalarGridSpec(num_scalar_...  9.34 us
    convert_element_type x3, other arithmetic, stacks_of(): chosen[:, :item_rows].astype(jnp.float32)  4.71 us
  transfers between devices with their start and end apart: 17, of which 4 were waited for; matrix products, arithmetic and copies ran while one was open for 15% of the time, Pallas kernels for 35%

profile of v3, /device:TPU:0, one launch (start us, length us, event | category | flops | bytes accessed | tf_op | source)
XLA Modules:
  0.0 126.5 jit_solution(5096331970548905743)
XLA Ops:
  0.0 2.9 %collective-permute-start = (bf16[160,2048]{1,0:T(8,128)(2,1)}, bf16[160,2048]{1,0:T(8,128)(2,1)S(1)}, u32[]{:S(2)}, u32[]{:S(2)}) collective-permute-start(bf16[160,2048]{1,0:T(8,128)(2,1)} %refs_0_.1), channel_id=1, source_target_pairs={{0,2},{1,3},{2,0},{3,1},{4,6},{5,7},{6,4},{7,5},{8,10},{9,11},{10,... | collective-permute-start | bytes 1966088 | tf_op jit(solution)/shard_map/ppermute | solution.py:318
  2.9 1.5 %collective-permute-start.1 = (bf16[160,2048]{1,0:T(8,128)(2,1)}, bf16[160,2048]{1,0:T(8,128)(2,1)S(1)}, u32[]{:S(2)}, u32[]{:S(2)}) collective-permute-start(bf16[160,2048]{1,0:T(8,128)(2,1)} %refs_0_.1), channel_id=1, source_target_pairs={{0,4},{1,5},{2,6},{3,7},{4,0},{5,1},{6,2},{7,3},{8,12},{9,13},{10,... | collective-permute-start | bytes 1966088 | tf_op jit(solution)/shard_map/ppermute | solution.py:318
  4.5 1.0 reshape.73
  5.5 0.8 rev.3
  6.3 0.7 convert_element_type.30
  7.2 0.7 convert_element_type.32
  8.2 3.6 %collective-permute-start.4 = (bf16[1040,128]{1,0:T(8,128)(2,1)S(1)}, bf16[1040,128]{1,0:T(8,128)(2,1)S(1)}, u32[]{:S(2)}, u32[]{:S(2)}) collective-permute-start(bf16[1040,128]{1,0:T(8,128)(2,1)S(1)} %concatenate.10), channel_id=1, source_target_pairs={{0,24},{1,25},{2,26},{3,27},{4,28},{5,29},{6,30},{7,31},{8,16},{9,... | collective-permute-start | bytes 798728 | tf_op jit(solution)/shard_map/ppermute | solution.py:318
  11.8 0.8 collective-permute-start.6
  13.0 0.8 slice_convert_fusion
  13.8 4.0 %collective-permute-done.refs_1_ = bf16[160,2048]{1,0:T(8,128)(2,1)S(1)} collective-permute-done((bf16[160,2048]{1,0:T(8,128)(2,1)}, bf16[160,2048]{1,0:T(8,128)(2,1)S(1)}, u32[]{:S(2)}, u32[]{:S(2)}) %collective-permute-start) | collective-permute-done | bytes 655392 | tf_op jit(solution)/shard_map/ppermute | solution.py:318
  17.9 1.4 %collective-permute-done.1.refs_2_ = bf16[160,2048]{1,0:T(8,128)(2,1)S(1)} collective-permute-done((bf16[160,2048]{1,0:T(8,128)(2,1)}, bf16[160,2048]{1,0:T(8,128)(2,1)S(1)}, u32[]{:S(2)}, u32[]{:S(2)}) %collective-permute-start.1) | collective-permute-done | bytes 655392 | tf_op jit(solution)/shard_map/ppermute | solution.py:318
  19.3 1.5 %collective-permute-start.2 = (bf16[80,2048]{1,0:T(8,128)(2,1)S(1)}, bf16[80,2048]{1,0:T(8,128)(2,1)S(1)}, u32[]{:S(2)}, u32[]{:S(2)}) collective-permute-start(bf16[80,2048]{1,0:T(8,128)(2,1)S(1)} %slice.60), channel_id=1, source_target_pairs={{0,4},{1,5},{2,6},{3,7},{4,0},{5,1},{6,2},{7,3},{8,12},{9,13},{10,... | collective-permute-start | bytes 983048 | tf_op jit(solution)/shard_map/ppermute | solution.py:318
  20.9 0.8 slice.61
  22.2 11.8 %collective-permute-done.5 = bf16[1040,128]{1,0:T(8,128)(2,1)S(1)} collective-permute-done((bf16[1040,128]{1,0:T(8,128)(2,1)S(1)}, bf16[1040,128]{1,0:T(8,128)(2,1)S(1)}, u32[]{:S(2)}, u32[]{:S(2)}) %collective-permute-start.5) | collective-permute-done | bytes 266272 | tf_op jit(solution)/shard_map/ppermute | solution.py:318
  35.0 0.7 mul.123.scale
  37.5 2.4 %fusion.1 = bf16[160,2048]{1,0:T(8,128)(2,1)} fusion(bf16[160,2048]{1,0:T(8,128)(2,1)} %refs_0_.1, bf16[160,2048]{1,0:T(8,128)(2,1)S(1)} %collective-permute-done.refs_1_, bf16[160,2048]{1,0:T(8,128)(2,1)S(1)} %collective-permute-done.1.refs_2_, bf16[80,2048]{1,0:T(8,128)(2,1)S(1)} %collective-permute-done.3.refs_7_, ...), kind=kLoop, calls=%fused_computation.2 | loop fusion | flops 2293760 | bytes 3276803 | tf_op jit(solution)/shard_map/jit(_where)/select_n | solution.py:346
  39.9 1.3 %collective-permute-start.12 = (bf16[160,2048]{1,0:T(8,128)(2,1)}, bf16[160,2048]{1,0:T(8,128)(2,1)}, u32[]{:S(2)}, u32[]{:S(2)}) collective-permute-start(bf16[160,2048]{1,0:T(8,128)(2,1)} %fusion.1), channel_id=1, source_target_pairs={{8,0},{9,1},{10,2},{11,3},{12,4},{13,5},{14,6},{15,7},{16,8},{17,9... | collective-permute-start | bytes 1966088 | tf_op jit(solution)/shard_map/ppermute | solution.py:354
  43.6 17.1 %shard_map.46 = (bf16[65536,128]{1,0:T(8,128)(2,1)S(1)}, f32[2,26632,128]{2,1,0:T(8,128)S(1)}, bf16[16,320,128]{2,1,0:T(8,128)(2,1)S(1)}) custom-call(s32[10]{0:T(128)} %stack.73.place, bf16[160,2048]{1,0:T(8,128)(2,1)} %refs_0_.1, bf16[160,2048]{1,0:T(8,128)(2,1)} %copy-done, bf16[160,2048]{1,0:T(8,128)(2,1)} %copy-done.1, ...), custom_call_target="tpu_custom_call" | custom-call | tf_op jit(solution)/shard_map/pallas_call | solution.py:198
  60.8 0.7 maximum_convert_fusion
  61.4 2.1 %fusion.2 = f32[2,1024,128]{2,1,0:T(8,128)} fusion(bf16[1,1040,128]{2,1,0:T(8,128)(2,1)} %bitcast.26, bf16[1,1040,128]{2,1,0:T(8,128)(2,1)} %bitcast.29), kind=kLoop, calls=%fused_computation.7 | loop fusion | flops 1048576 | bytes 1581056 | tf_op jit(solution)/shard_map/convert_element_type | solution.py:373
  63.5 0.7 slice_convert_fusion.3
  65.5 1.8 %slice_convert_fusion.1 = f32[1,1024,128]{2,1,0:T(8,128)} fusion(bf16[1,1040,128]{2,1,0:T(8,128)(2,1)} %bitcast.38), kind=kLoop, calls=%fused_computation.9 | loop fusion | flops 131072 | bytes 786432 | tf_op jit(solution)/shard_map/convert_element_type | solution.py:373
  67.3 0.9 copy-done.7
  68.2 9.3 %shard_map.47 = (bf16[65536,128]{1,0:T(8,128)(2,1)S(1)}, f32[2,26632,128]{2,1,0:T(8,128)S(1)}) custom-call(s32[2]{0:T(128)} %pad_add_fusion.place, bf16[16,320,128]{2,1,0:T(8,128)(2,1)S(1)} %get-tuple-element.28.tail_ref, bf16[65536,128]{1,0:T(8,128)(2,1)S(1)} %get-tuple-element.29.w_in, ...), custom_call_target="tpu_custom_call", output_to_operand_aliasing={{0}: (2, {}), {1}: (3, {})} | custom-call | tf_op jit(solution)/shard_map/pallas_call | solution.py:253
  77.5 9.7 %shard_map.49 = f32[320,128]{1,0:T(8,128)} custom-call(s32[512]{0:T(512)} %add_bitcast_fusion.1.sensor, f32[512]{0:T(512)} %mul.118.scale, f32[32,32,128]{2,1,0:T(8,128)} %bitcast.34, bf16[65536,128]{1,0:T(8,128)(2,1)S(1)} %get-tuple-element.32.w_ref, f32[2,26632,128]{2,1,0:T(8,128)S(1)} %get-tuple-element.33.g_ref), custom_call_target="tpu_custom_call" | custom-call | flops 8000000000 | bytes 8000000 | tf_op jit(solution)/shard_map/pallas_call | solution.py:289
  87.2 2.5 %collective-permute-start.16 = (f32[320,128]{1,0:T(8,128)}, f32[320,128]{1,0:T(8,128)S(1)}, u32[]{:S(2)}, u32[]{:S(2)}) collective-permute-start(f32[320,128]{1,0:T(8,128)} %shard_map.49), channel_id=1, source_target_pairs={{0,8},{1,9},{2,10},{3,11},{4,12},{5,13},{6,14},{7,15},{8,0},{9,1},... | collective-permute-start | bytes 491528 | tf_op jit(solution)/shard_map/ppermute | solution.py:318
  89.7 17.1 %shard_map.48 = (f32[320,128]{1,0:T(8,128)}, f32[320,128]{1,0:T(8,128)}) custom-call(s32[1024]{0:T(1024)} %bitcast.39, f32[1024]{0:T(1024)} %mul.103.scale, f32[64,32,128]{2,1,0:T(8,128)} %bitcast.35, bf16[65536,128]{1,0:T(8,128)(2,1)S(1)} %get-tuple-element.32.w_ref, f32[2,26632,128]{2,1,0:T(8,128)S(1)} %get-tuple-element.33.g_ref), custom_call_target="tpu_custom_call" | custom-call | flops 16000000000 | bytes 16000000 | tf_op jit(solution)/shard_map/pallas_call | solution.py:289
  106.8 1.8 %collective-permute-start.14 = (f32[320,128]{1,0:T(8,128)}, f32[320,128]{1,0:T(8,128)S(1)}, u32[]{:S(2)}, u32[]{:S(2)}) collective-permute-start(f32[320,128]{1,0:T(8,128)} %get-tuple-element.34), channel_id=1, source_target_pairs={{0,24},{1,25},{2,26},{3,27},{4,28},{5,29},{6,30},{7,31},{8,16},{9,... | collective-permute-start | bytes 491528 | tf_op jit(solution)/shard_map/ppermute | solution.py:318
  109.2 9.6 %shard_map.50 = f32[320,128]{1,0:T(8,128)} custom-call(s32[512]{0:T(512)} %add_bitcast_fusion.sensor, f32[512]{0:T(512)} %mul.123.scale, f32[32,32,128]{2,1,0:T(8,128)} %bitcast.33, bf16[65536,128]{1,0:T(8,128)(2,1)S(1)} %get-tuple-element.32.w_ref, f32[2,26632,128]{2,1,0:T(8,128)S(1)} %get-tuple-element.33.g_ref), custom_call_target="tpu_custom_call" | custom-call | flops 8000000000 | bytes 8000000 | tf_op jit(solution)/shard_map/pallas_call | solution.py:289
  118.9 5.6 %collective-permute-done.15 = f32[320,128]{1,0:T(8,128)S(1)} collective-permute-done((f32[320,128]{1,0:T(8,128)}, f32[320,128]{1,0:T(8,128)S(1)}, u32[]{:S(2)}, u32[]{:S(2)}) %collective-permute-start.15) | collective-permute-done | bytes 163872 | tf_op jit(solution)/shard_map/ppermute | solution.py:318
  124.5 1.0 select_select_fusion.3
  125.6 0.9 pad_maximum_fusion
  (72 shorter events, 8.6 us)
Async XLA Ops:
  0.0 17.9 %collective-permute-start = (bf16[160,2048]{1,0:T(8,128)(2,1)}, bf16[160,2048]{1,0:T(8,128)(2,1)S(1)}, u32[]{:S(2)}, u32[]{:S(2)}) collective-permute-start(bf16[160,2048]{1,0:T(8,128)(2,1)} %refs_0_.1), channel_id=1, source_target_pairs={{0,2},{1,3},{2,0},{3,1},{4,6},{5,7},{6,4},{7,5},{8,10},{9,11},{10,... | collective-permute-start | bytes 1966088 | tf_op jit(solution)/shard_map/ppermute | solution.py:318
  2.9 16.4 %collective-permute-start.1 = (bf16[160,2048]{1,0:T(8,128)(2,1)}, bf16[160,2048]{1,0:T(8,128)(2,1)S(1)}, u32[]{:S(2)}, u32[]{:S(2)}) collective-permute-start(bf16[160,2048]{1,0:T(8,128)(2,1)} %refs_0_.1), channel_id=1, source_target_pairs={{0,4},{1,5},{2,6},{3,7},{4,0},{5,1},{6,2},{7,3},{8,12},{9,13},{10,... | collective-permute-start | bytes 1966088 | tf_op jit(solution)/shard_map/ppermute | solution.py:318
  8.2 13.4 %collective-permute-start.4 = (bf16[1040,128]{1,0:T(8,128)(2,1)S(1)}, bf16[1040,128]{1,0:T(8,128)(2,1)S(1)}, u32[]{:S(2)}, u32[]{:S(2)}) collective-permute-start(bf16[1040,128]{1,0:T(8,128)(2,1)S(1)} %concatenate.10), channel_id=1, source_target_pairs={{0,24},{1,25},{2,26},{3,27},{4,28},{5,29},{6,30},{7,31},{8,16},{9,... | collective-permute-start | bytes 798728 | tf_op jit(solution)/shard_map/ppermute | solution.py:318
  11.8 22.1 %collective-permute-start.5 = (bf16[1040,128]{1,0:T(8,128)(2,1)S(1)}, bf16[1040,128]{1,0:T(8,128)(2,1)S(1)}, u32[]{:S(2)}, u32[]{:S(2)}) collective-permute-start(bf16[1040,128]{1,0:T(8,128)(2,1)S(1)} %concatenate.10), channel_id=1, source_target_pairs={{0,16},{1,17},{2,18},{3,19},{4,20},{5,21},{6,22},{7,23},{8,24},{9,... | collective-permute-start | bytes 798728 | tf_op jit(solution)/shard_map/ppermute | solution.py:318
  11.8 22.1 %collective-permute-start.6 = (bf16[1040,128]{1,0:T(8,128)(2,1)S(1)}, bf16[1040,128]{1,0:T(8,128)(2,1)S(1)}, u32[]{:S(2)}, u32[]{:S(2)}) collective-permute-start(bf16[1040,128]{1,0:T(8,128)(2,1)S(1)} %concatenate.10), channel_id=1, source_target_pairs={{0,8},{1,9},{2,10},{3,11},{4,12},{5,13},{6,14},{7,15},{8,0},{9,1},... | collective-permute-start | bytes 798728 | tf_op jit(solution)/shard_map/ppermute | solution.py:318
  17.9 25.7 %copy-start = (bf16[160,2048]{1,0:T(8,128)(2,1)}, bf16[160,2048]{1,0:T(8,128)(2,1)S(1)}, u32[]{:S(2)}) copy-start(bf16[160,2048]{1,0:T(8,128)(2,1)S(1)} %collective-permute-done.refs_1_) | copy-start | bytes 1966084
  17.9 22.0 %collective-permute-start.7 = (bf16[160,2048]{1,0:T(8,128)(2,1)}, bf16[160,2048]{1,0:T(8,128)(2,1)}, u32[]{:S(2)}, u32[]{:S(2)}) collective-permute-start(bf16[160,2048]{1,0:T(8,128)(2,1)} %refs_0_.1), channel_id=1, source_target_pairs={{0,1},{1,0},{2,3},{3,2},{4,5},{5,4},{6,7},{7,6},{8,9},{9,8},{10,11... | collective-permute-start | bytes 1966088 | tf_op jit(solution)/shard_map/ppermute | solution.py:318
  19.3 24.3 %copy-start.1 = (bf16[160,2048]{1,0:T(8,128)(2,1)}, bf16[160,2048]{1,0:T(8,128)(2,1)S(1)}, u32[]{:S(2)}) copy-start(bf16[160,2048]{1,0:T(8,128)(2,1)S(1)} %collective-permute-done.1.refs_2_) | copy-start | bytes 1966084
  19.3 17.7 %collective-permute-start.2 = (bf16[80,2048]{1,0:T(8,128)(2,1)S(1)}, bf16[80,2048]{1,0:T(8,128)(2,1)S(1)}, u32[]{:S(2)}, u32[]{:S(2)}) collective-permute-start(bf16[80,2048]{1,0:T(8,128)(2,1)S(1)} %slice.60), channel_id=1, source_target_pairs={{0,4},{1,5},{2,6},{3,7},{4,0},{5,1},{6,2},{7,3},{8,12},{9,13},{10,... | collective-permute-start | bytes 983048 | tf_op jit(solution)/shard_map/ppermute | solution.py:318
  21.6 20.7 %copy-start.2 = (bf16[1040,128]{1,0:T(8,128)(2,1)}, bf16[1040,128]{1,0:T(8,128)(2,1)S(1)}, u32[]{:S(2)}) copy-start(bf16[1040,128]{1,0:T(8,128)(2,1)S(1)} %collective-permute-done.4) | copy-start | bytes 798724
  21.6 15.5 %collective-permute-start.3 = (bf16[80,2048]{1,0:T(8,128)(2,1)}, bf16[80,2048]{1,0:T(8,128)(2,1)S(1)}, u32[]{:S(2)}, u32[]{:S(2)}) collective-permute-start(bf16[80,2048]{1,0:T(8,128)(2,1)} %slice.61), channel_id=1, source_target_pairs={{0,2},{1,3},{2,0},{3,1},{4,6},{5,7},{6,4},{7,5},{8,10},{9,11},{10,... | collective-permute-start | bytes 983048 | tf_op jit(solution)/shard_map/ppermute | solution.py:318
  33.9 8.4 %copy-start.3 = (bf16[1040,128]{1,0:T(8,128)(2,1)}, bf16[1040,128]{1,0:T(8,128)(2,1)S(1)}, u32[]{:S(2)}) copy-start(bf16[1040,128]{1,0:T(8,128)(2,1)S(1)} %collective-permute-done.5) | copy-start | bytes 798724
  33.9 6.0 %collective-permute-start.8 = (bf16[160,2048]{1,0:T(8,128)(2,1)S(1)}, bf16[160,2048]{1,0:T(8,128)(2,1)}, u32[]{:S(2)}, u32[]{:S(2)}) collective-permute-start(bf16[160,2048]{1,0:T(8,128)(2,1)S(1)} %collective-permute-done.refs_1_), channel_id=1, source_target_pairs={{0,1},{1,0},{2,3},{3,2},{4,5},{5,4},{6,7},{7,6},{8,9},{9,8},{10,11... | collective-permute-start | bytes 1966088 | tf_op jit(solution)/shard_map/ppermute | solution.py:318
  34.0 8.4 %copy-start.6 = (bf16[1040,128]{1,0:T(8,128)(2,1)}, bf16[1040,128]{1,0:T(8,128)(2,1)S(1)}, u32[]{:S(2)}) copy-start(bf16[1040,128]{1,0:T(8,128)(2,1)S(1)} %collective-permute-done.6) | copy-start | bytes 798724
  34.0 6.0 %collective-permute-start.9 = (bf16[160,2048]{1,0:T(8,128)(2,1)S(1)}, bf16[160,2048]{1,0:T(8,128)(2,1)}, u32[]{:S(2)}, u32[]{:S(2)}) collective-permute-start(bf16[160,2048]{1,0:T(8,128)(2,1)S(1)} %collective-permute-done.1.refs_2_), channel_id=1, source_target_pairs={{0,1},{1,0},{2,3},{3,2},{4,5},{5,4},{6,7},{7,6},{8,9},{9,8},{10,11... | collective-permute-start | bytes 1966088 | tf_op jit(solution)/shard_map/ppermute | solution.py:318
  37.0 4.2 %copy-start.4 = (bf16[80,2048]{1,0:T(8,128)(2,1)}, bf16[80,2048]{1,0:T(8,128)(2,1)S(1)}, u32[]{:S(2)}) copy-start(bf16[80,2048]{1,0:T(8,128)(2,1)S(1)} %collective-permute-done.2.refs_6_) | copy-start | bytes 983044
  37.0 2.9 %collective-permute-start.10 = (bf16[80,2048]{1,0:T(8,128)(2,1)S(1)}, bf16[80,2048]{1,0:T(8,128)(2,1)S(1)}, u32[]{:S(2)}, u32[]{:S(2)}) collective-permute-start(bf16[80,2048]{1,0:T(8,128)(2,1)S(1)} %collective-permute-done.2.refs_6_), channel_id=1, source_target_pairs={{0,1},{1,0},{2,3},{3,2},{4,5},{5,4},{6,7},{7,6},{8,9},{9,8},{10,11... | collective-permute-start | bytes 983048 | tf_op jit(solution)/shard_map/ppermute | solution.py:318
  37.1 4.1 %copy-start.5 = (bf16[80,2048]{1,0:T(8,128)(2,1)}, bf16[80,2048]{1,0:T(8,128)(2,1)S(1)}, u32[]{:S(2)}) copy-start(bf16[80,2048]{1,0:T(8,128)(2,1)S(1)} %collective-permute-done.3.refs_7_) | copy-start | bytes 983044
  37.1 2.8 %collective-permute-start.11 = (bf16[80,2048]{1,0:T(8,128)(2,1)S(1)}, bf16[80,2048]{1,0:T(8,128)(2,1)S(1)}, u32[]{:S(2)}, u32[]{:S(2)}) collective-permute-start(bf16[80,2048]{1,0:T(8,128)(2,1)S(1)} %collective-permute-done.3.refs_7_), channel_id=1, source_target_pairs={{0,1},{1,0},{2,3},{3,2},{4,5},{5,4},{6,7},{7,6},{8,9},{9,8},{10,11... | collective-permute-start | bytes 983048 | tf_op jit(solution)/shard_map/ppermute | solution.py:318
  39.9 1.4 %copy-start.8 = (bf16[80,2048]{1,0:T(8,128)(2,1)}, bf16[80,2048]{1,0:T(8,128)(2,1)S(1)}, u32[]{:S(2)}) copy-start(bf16[80,2048]{1,0:T(8,128)(2,1)S(1)} %collective-permute-done.10.refs_8_) | copy-start | bytes 983044
  39.9 1.4 %copy-start.9 = (bf16[80,2048]{1,0:T(8,128)(2,1)}, bf16[80,2048]{1,0:T(8,128)(2,1)S(1)}, u32[]{:S(2)}) copy-start(bf16[80,2048]{1,0:T(8,128)(2,1)S(1)} %collective-permute-done.11.refs_9_) | copy-start | bytes 983044
  39.9 24.3 %collective-permute-start.12 = (bf16[160,2048]{1,0:T(8,128)(2,1)}, bf16[160,2048]{1,0:T(8,128)(2,1)}, u32[]{:S(2)}, u32[]{:S(2)}) collective-permute-start(bf16[160,2048]{1,0:T(8,128)(2,1)} %fusion.1), channel_id=1, source_target_pairs={{8,0},{9,1},{10,2},{11,3},{12,4},{13,5},{14,6},{15,7},{16,8},{17,9... | collective-permute-start | bytes 1966088 | tf_op jit(solution)/shard_map/ppermute | solution.py:354
  64.2 3.1 %collective-permute-start.13 = (bf16[160,2048]{1,0:T(8,128)(2,1)}, bf16[160,2048]{1,0:T(8,128)(2,1)S(1)}, u32[]{:S(2)}, u32[]{:S(2)}) collective-permute-start(bf16[160,2048]{1,0:T(8,128)(2,1)} %collective-permute-done.12.refs_0_), channel_id=1, source_target_pairs={{0,1},{1,0},{2,3},{3,2},{4,5},{5,4},{6,7},{7,6},{8,9},{9,8},{10,11... | collective-permute-start | bytes 1966088 | tf_op jit(solution)/shard_map/ppermute | solution.py:318
  67.3 0.9 copy-start.7
  87.2 31.7 %collective-permute-start.16 = (f32[320,128]{1,0:T(8,128)}, f32[320,128]{1,0:T(8,128)S(1)}, u32[]{:S(2)}, u32[]{:S(2)}) collective-permute-start(f32[320,128]{1,0:T(8,128)} %shard_map.49), channel_id=1, source_target_pairs={{0,8},{1,9},{2,10},{3,11},{4,12},{5,13},{6,14},{7,15},{8,0},{9,1},... | collective-permute-start | bytes 491528 | tf_op jit(solution)/shard_map/ppermute | solution.py:318
  106.8 12.1 %collective-permute-start.14 = (f32[320,128]{1,0:T(8,128)}, f32[320,128]{1,0:T(8,128)S(1)}, u32[]{:S(2)}, u32[]{:S(2)}) collective-permute-start(f32[320,128]{1,0:T(8,128)} %get-tuple-element.34), channel_id=1, source_target_pairs={{0,24},{1,25},{2,26},{3,27},{4,28},{5,29},{6,30},{7,31},{8,16},{9,... | collective-permute-start | bytes 491528 | tf_op jit(solution)/shard_map/ppermute | solution.py:318
  108.7 15.8 %collective-permute-start.15 = (f32[320,128]{1,0:T(8,128)}, f32[320,128]{1,0:T(8,128)S(1)}, u32[]{:S(2)}, u32[]{:S(2)}) collective-permute-start(f32[320,128]{1,0:T(8,128)} %get-tuple-element.35), channel_id=1, source_target_pairs={{0,16},{1,17},{2,18},{3,19},{4,20},{5,21},{6,22},{7,23},{8,24},{9,... | collective-permute-start | bytes 491528 | tf_op jit(solution)/shard_map/ppermute | solution.py:318

commit v4 on v3

--- a/solution.py
+++ b/solution.py
@@ -333,8 +333,10 @@
 
     near = flip(data, 2)
     side = flip(data, 4)
-    packets = [flip(packet, GROUP * q) for q in reversed(range(1, layers))]
+    across = flip(packet, 2 * GROUP)
+    next_door = flip(packet, GROUP)
     twin = flip(data, 1)
+    near, side, across = lax.optimization_barrier((near, side, across))
     far_low = flip(near[:half], 4)
     far_high = flip(side[half:], 2)
     near_twin = flip(near, 1)
@@ -346,11 +348,13 @@
     lead = jnp.where(
         chip == 0, data, jnp.where(chip == 1, near, jnp.where(chip == 2, side, far))
     )
-    held = lax.optimization_barrier(
-        (lead, *packets, twin, near_twin, side_twin, far_low_twin, far_high_twin)
+    beyond = flip(across, GROUP)
+    lead, across, next_door, beyond, twin, near_twin, side_twin, far_low_twin, far_high_twin = (
+        lax.optimization_barrier(
+            (lead, across, next_door, beyond, twin, near_twin, side_twin, far_low_twin, far_high_twin)
+        )
     )
-    lead, packets = held[0], [packet] + list(held[1:layers][::-1])
-    twin, near_twin, side_twin, far_low_twin, far_high_twin = held[layers:]
+    packets = [packet, next_door, across, beyond]
     halo = lax.ppermute(lead, "sens", [(i + GROUP, i) for i in range(devices - GROUP)])
     halo_twin = flip(halo, 1)
     pieces = [

time: 127 us -> 123 us (0.969)
  waiting for transfers between devices: 22.9 us -> 20.1 us
    ppermute x16, waiting for transfers between devices: 22.9 us -> 20.1 us  [flip(): return lax.ppermute(value, 'sens', [(i, i ^ bits) for i in range(devices)])]
  transfers between devices with their start and end apart: 17 -> 17, of which waited for: 4 -> 4; matrix products, arithmetic and copies ran while one was open for 15% -> 15% of each run, Pallas kernels for 35% -> 36%
where the time goes in v4:
time: 123 us; the launch traced here: 122 us
  Pallas kernels  62.9 us (51%)
  waiting for transfers between devices  20.1 us (16%)
  starting transfers between devices  17.5 us (14%)
  other arithmetic  14.8 us (12%)
  local copies, waits for them, and re-layouts  6.65 us (5%)
    pallas_call x3, Pallas kernels, matched_stacks(): pl.pallas_call(kernel, grid_spec=pltpu.PrefetchScalarGridSpec(num_scalar_...  36.4 us
    ppermute x16, waiting for transfers between devices, flip(): return lax.ppermute(value, 'sens', [(i, i ^ bits) for i in range(devices)])  20.1 us
    pallas_call x1, Pallas kernels, early_tables(): pl.pallas_call(kernel, grid_spec=pltpu.PrefetchScalarGridSpec(num_scalar_...  17.1 us
    ppermute x16, starting transfers between devices, flip(): return lax.ppermute(value, 'sens', [(i, i ^ bits) for i in range(devices)])  16.2 us
    pallas_call x1, Pallas kernels, late_tables(): pl.pallas_call(kernel, grid_spec=pltpu.PrefetchScalarGridSpec(num_scalar_...  9.34 us
    convert_element_type x3, other arithmetic, stacks_of(): chosen[:, :item_rows].astype(jnp.float32)  4.71 us
  transfers between devices with their start and end apart: 17, of which 4 were waited for; matrix products, arithmetic and copies ran while one was open for 15% of the time, Pallas kernels for 36%

profile of v4, /device:TPU:0, one launch (start us, length us, event | category | flops | bytes accessed | tf_op | source)
XLA Modules:
  0.0 122.2 jit_solution(16674718968867570857)
XLA Ops:
  0.0 2.9 %collective-permute-start = (bf16[160,2048]{1,0:T(8,128)(2,1)}, bf16[160,2048]{1,0:T(8,128)(2,1)S(1)}, u32[]{:S(2)}, u32[]{:S(2)}) collective-permute-start(bf16[160,2048]{1,0:T(8,128)(2,1)} %refs_0_.1), channel_id=1, source_target_pairs={{0,2},{1,3},{2,0},{3,1},{4,6},{5,7},{6,4},{7,5},{8,10},{9,11},{10,... | collective-permute-start | bytes 1966088 | tf_op jit(solution)/shard_map/ppermute | solution.py:318
  2.9 1.5 %collective-permute-start.1 = (bf16[160,2048]{1,0:T(8,128)(2,1)}, bf16[160,2048]{1,0:T(8,128)(2,1)S(1)}, u32[]{:S(2)}, u32[]{:S(2)}) collective-permute-start(bf16[160,2048]{1,0:T(8,128)(2,1)} %refs_0_.1), channel_id=1, source_target_pairs={{0,4},{1,5},{2,6},{3,7},{4,0},{5,1},{6,2},{7,3},{8,12},{9,13},{10,... | collective-permute-start | bytes 1966088 | tf_op jit(solution)/shard_map/ppermute | solution.py:318
  4.5 1.0 reshape.73
  5.5 0.8 rev.3
  6.3 0.7 convert_element_type.30
  7.2 0.7 convert_element_type.32
  8.2 2.6 %collective-permute-start.2 = (bf16[1040,128]{1,0:T(8,128)(2,1)S(1)}, bf16[1040,128]{1,0:T(8,128)(2,1)S(1)}, u32[]{:S(2)}, u32[]{:S(2)}) collective-permute-start(bf16[1040,128]{1,0:T(8,128)(2,1)S(1)} %concatenate.9), channel_id=1, source_target_pairs={{0,16},{1,17},{2,18},{3,19},{4,20},{5,21},{6,22},{7,23},{8,24},{9,... | collective-permute-start | bytes 798728 | tf_op jit(solution)/shard_map/ppermute | solution.py:318
  10.8 1.6 %collective-permute-start.5 = (bf16[1040,128]{1,0:T(8,128)(2,1)S(1)}, bf16[1040,128]{1,0:T(8,128)(2,1)S(1)}, u32[]{:S(2)}, u32[]{:S(2)}) collective-permute-start(bf16[1040,128]{1,0:T(8,128)(2,1)S(1)} %concatenate.9), channel_id=1, source_target_pairs={{0,8},{1,9},{2,10},{3,11},{4,12},{5,13},{6,14},{7,15},{8,0},{9,1},... | collective-permute-start | bytes 798728 | tf_op jit(solution)/shard_map/ppermute | solution.py:318
  12.8 0.8 slice_convert_fusion
  13.6 8.9 %collective-permute-done.2 = bf16[1040,128]{1,0:T(8,128)(2,1)S(1)} collective-permute-done((bf16[1040,128]{1,0:T(8,128)(2,1)S(1)}, bf16[1040,128]{1,0:T(8,128)(2,1)S(1)}, u32[]{:S(2)}, u32[]{:S(2)}) %collective-permute-start.2) | collective-permute-done | bytes 266272 | tf_op jit(solution)/shard_map/ppermute | solution.py:318
  24.8 0.7 mul.123.scale
  25.5 0.7 stack.73.place
  27.4 5.5 %collective-permute-done.3.refs_6_ = bf16[80,2048]{1,0:T(8,128)(2,1)S(1)} collective-permute-done((bf16[80,2048]{1,0:T(8,128)(2,1)S(1)}, bf16[80,2048]{1,0:T(8,128)(2,1)S(1)}, u32[]{:S(2)}, u32[]{:S(2)}) %collective-permute-start.3) | collective-permute-done | bytes 327712 | tf_op jit(solution)/shard_map/ppermute | solution.py:318
  33.5 2.4 %fusion.1 = bf16[160,2048]{1,0:T(8,128)(2,1)} fusion(bf16[160,2048]{1,0:T(8,128)(2,1)} %refs_0_.1, bf16[160,2048]{1,0:T(8,128)(2,1)S(1)} %collective-permute-done.refs_1_, bf16[160,2048]{1,0:T(8,128)(2,1)S(1)} %collective-permute-done.1.refs_2_, bf16[80,2048]{1,0:T(8,128)(2,1)S(1)} %collective-permute-done.4.refs_7_, ...), kind=kLoop, calls=%fused_computation.2 | loop fusion | flops 2293760 | bytes 3276803 | tf_op jit(solution)/shard_map/jit(_where)/select_n | solution.py:348
  35.9 1.3 %collective-permute-start.12 = (bf16[160,2048]{1,0:T(8,128)(2,1)}, bf16[160,2048]{1,0:T(8,128)(2,1)}, u32[]{:S(2)}, u32[]{:S(2)}) collective-permute-start(bf16[160,2048]{1,0:T(8,128)(2,1)} %fusion.1), channel_id=1, source_target_pairs={{8,0},{9,1},{10,2},{11,3},{12,4},{13,5},{14,6},{15,7},{16,8},{17,9... | collective-permute-start | bytes 1966088 | tf_op jit(solution)/shard_map/ppermute | solution.py:358
  37.6 0.7 mul.118.scale
  38.9 0.7 mul.103.scale
  39.6 17.1 %shard_map.46 = (bf16[65536,128]{1,0:T(8,128)(2,1)S(1)}, f32[2,26632,128]{2,1,0:T(8,128)S(1)}, bf16[16,320,128]{2,1,0:T(8,128)(2,1)S(1)}) custom-call(s32[10]{0:T(128)} %stack.73.place, bf16[160,2048]{1,0:T(8,128)(2,1)} %refs_0_.1, bf16[160,2048]{1,0:T(8,128)(2,1)} %copy-done, bf16[160,2048]{1,0:T(8,128)(2,1)} %copy-done.1, ...), custom_call_target="tpu_custom_call" | custom-call | tf_op jit(solution)/shard_map/pallas_call | solution.py:198
  56.7 0.7 maximum_convert_fusion
  57.4 2.1 %fusion.2 = f32[2,1024,128]{2,1,0:T(8,128)} fusion(bf16[1,1040,128]{2,1,0:T(8,128)(2,1)} %bitcast.29, bf16[1,1040,128]{2,1,0:T(8,128)(2,1)} %bitcast.26), kind=kLoop, calls=%fused_computation.7 | loop fusion | flops 1048576 | bytes 1581056 | tf_op jit(solution)/shard_map/convert_element_type | solution.py:377
  59.5 0.7 slice_convert_fusion.3
  61.6 1.8 %slice_convert_fusion.1 = f32[1,1024,128]{2,1,0:T(8,128)} fusion(bf16[1,1040,128]{2,1,0:T(8,128)(2,1)} %bitcast.38), kind=kLoop, calls=%fused_computation.9 | loop fusion | flops 131072 | bytes 786432 | tf_op jit(solution)/shard_map/convert_element_type | solution.py:377
  63.4 0.9 copy-done.7
  64.2 9.3 %shard_map.47 = (bf16[65536,128]{1,0:T(8,128)(2,1)S(1)}, f32[2,26632,128]{2,1,0:T(8,128)S(1)}) custom-call(s32[2]{0:T(128)} %pad_add_fusion.place, bf16[16,320,128]{2,1,0:T(8,128)(2,1)S(1)} %get-tuple-element.34.tail_ref, bf16[65536,128]{1,0:T(8,128)(2,1)S(1)} %get-tuple-element.35.w_in, ...), custom_call_target="tpu_custom_call", output_to_operand_aliasing={{0}: (2, {}), {1}: (3, {})} | custom-call | tf_op jit(solution)/shard_map/pallas_call | solution.py:253
  73.6 9.7 %shard_map.49 = f32[320,128]{1,0:T(8,128)} custom-call(s32[512]{0:T(512)} %add_bitcast_fusion.1.sensor, f32[512]{0:T(512)} %mul.118.scale, f32[32,32,128]{2,1,0:T(8,128)} %bitcast.34, bf16[65536,128]{1,0:T(8,128)(2,1)S(1)} %get-tuple-element.38.w_ref, f32[2,26632,128]{2,1,0:T(8,128)S(1)} %get-tuple-element.39.g_ref), custom_call_target="tpu_custom_call" | custom-call | flops 8000000000 | bytes 8000000 | tf_op jit(solution)/shard_map/pallas_call | solution.py:289
  83.3 2.4 %collective-permute-start.16 = (f32[320,128]{1,0:T(8,128)}, f32[320,128]{1,0:T(8,128)S(1)}, u32[]{:S(2)}, u32[]{:S(2)}) collective-permute-start(f32[320,128]{1,0:T(8,128)} %shard_map.49), channel_id=1, source_target_pairs={{0,8},{1,9},{2,10},{3,11},{4,12},{5,13},{6,14},{7,15},{8,0},{9,1},... | collective-permute-start | bytes 491528 | tf_op jit(solution)/shard_map/ppermute | solution.py:318
  85.7 17.1 %shard_map.48 = (f32[320,128]{1,0:T(8,128)}, f32[320,128]{1,0:T(8,128)}) custom-call(s32[1024]{0:T(1024)} %bitcast.39, f32[1024]{0:T(1024)} %mul.103.scale, f32[64,32,128]{2,1,0:T(8,128)} %bitcast.35, bf16[65536,128]{1,0:T(8,128)(2,1)S(1)} %get-tuple-element.38.w_ref, f32[2,26632,128]{2,1,0:T(8,128)S(1)} %get-tuple-element.39.g_ref), custom_call_target="tpu_custom_call" | custom-call | flops 16000000000 | bytes 16000000 | tf_op jit(solution)/shard_map/pallas_call | solution.py:289
  102.8 1.8 %collective-permute-start.14 = (f32[320,128]{1,0:T(8,128)}, f32[320,128]{1,0:T(8,128)S(1)}, u32[]{:S(2)}, u32[]{:S(2)}) collective-permute-start(f32[320,128]{1,0:T(8,128)} %get-tuple-element.40), channel_id=1, source_target_pairs={{0,24},{1,25},{2,26},{3,27},{4,28},{5,29},{6,30},{7,31},{8,16},{9,... | collective-permute-start | bytes 491528 | tf_op jit(solution)/shard_map/ppermute | solution.py:318
  105.1 9.7 %shard_map.50 = f32[320,128]{1,0:T(8,128)} custom-call(s32[512]{0:T(512)} %add_bitcast_fusion.sensor, f32[512]{0:T(512)} %mul.123.scale, f32[32,32,128]{2,1,0:T(8,128)} %bitcast.33, bf16[65536,128]{1,0:T(8,128)(2,1)S(1)} %get-tuple-element.38.w_ref, f32[2,26632,128]{2,1,0:T(8,128)S(1)} %get-tuple-element.39.g_ref), custom_call_target="tpu_custom_call" | custom-call | flops 8000000000 | bytes 8000000 | tf_op jit(solution)/shard_map/pallas_call | solution.py:289
  114.8 5.4 %collective-permute-done.15 = f32[320,128]{1,0:T(8,128)S(1)} collective-permute-done((f32[320,128]{1,0:T(8,128)}, f32[320,128]{1,0:T(8,128)S(1)}, u32[]{:S(2)}, u32[]{:S(2)}) %collective-permute-start.15) | collective-permute-done | bytes 163872 | tf_op jit(solution)/shard_map/ppermute | solution.py:318
  120.2 1.0 select_select_fusion.3
  121.4 0.9 pad_maximum_fusion
  (72 shorter events, 8.0 us)
Async XLA Ops:
  0.0 22.5 %collective-permute-start = (bf16[160,2048]{1,0:T(8,128)(2,1)}, bf16[160,2048]{1,0:T(8,128)(2,1)S(1)}, u32[]{:S(2)}, u32[]{:S(2)}) collective-permute-start(bf16[160,2048]{1,0:T(8,128)(2,1)} %refs_0_.1), channel_id=1, source_target_pairs={{0,2},{1,3},{2,0},{3,1},{4,6},{5,7},{6,4},{7,5},{8,10},{9,11},{10,... | collective-permute-start | bytes 1966088 | tf_op jit(solution)/shard_map/ppermute | solution.py:318
  2.9 19.6 %collective-permute-start.1 = (bf16[160,2048]{1,0:T(8,128)(2,1)}, bf16[160,2048]{1,0:T(8,128)(2,1)S(1)}, u32[]{:S(2)}, u32[]{:S(2)}) collective-permute-start(bf16[160,2048]{1,0:T(8,128)(2,1)} %refs_0_.1), channel_id=1, source_target_pairs={{0,4},{1,5},{2,6},{3,7},{4,0},{5,1},{6,2},{7,3},{8,12},{9,13},{10,... | collective-permute-start | bytes 1966088 | tf_op jit(solution)/shard_map/ppermute | solution.py:318
  8.2 14.3 %collective-permute-start.2 = (bf16[1040,128]{1,0:T(8,128)(2,1)S(1)}, bf16[1040,128]{1,0:T(8,128)(2,1)S(1)}, u32[]{:S(2)}, u32[]{:S(2)}) collective-permute-start(bf16[1040,128]{1,0:T(8,128)(2,1)S(1)} %concatenate.9), channel_id=1, source_target_pairs={{0,16},{1,17},{2,18},{3,19},{4,20},{5,21},{6,22},{7,23},{8,24},{9,... | collective-permute-start | bytes 798728 | tf_op jit(solution)/shard_map/ppermute | solution.py:318
  10.8 12.9 %collective-permute-start.5 = (bf16[1040,128]{1,0:T(8,128)(2,1)S(1)}, bf16[1040,128]{1,0:T(8,128)(2,1)S(1)}, u32[]{:S(2)}, u32[]{:S(2)}) collective-permute-start(bf16[1040,128]{1,0:T(8,128)(2,1)S(1)} %concatenate.9), channel_id=1, source_target_pairs={{0,8},{1,9},{2,10},{3,11},{4,12},{5,13},{6,14},{7,15},{8,0},{9,1},... | collective-permute-start | bytes 798728 | tf_op jit(solution)/shard_map/ppermute | solution.py:318
  12.4 14.4 %collective-permute-start.7 = (bf16[160,2048]{1,0:T(8,128)(2,1)}, bf16[160,2048]{1,0:T(8,128)(2,1)}, u32[]{:S(2)}, u32[]{:S(2)}) collective-permute-start(bf16[160,2048]{1,0:T(8,128)(2,1)} %refs_0_.1), channel_id=1, source_target_pairs={{0,1},{1,0},{2,3},{3,2},{4,5},{5,4},{6,7},{7,6},{8,9},{9,8},{10,11... | collective-permute-start | bytes 1966088 | tf_op jit(solution)/shard_map/ppermute | solution.py:318
  22.5 15.7 %copy-start.2 = (bf16[1040,128]{1,0:T(8,128)(2,1)}, bf16[1040,128]{1,0:T(8,128)(2,1)S(1)}, u32[]{:S(2)}) copy-start(bf16[1040,128]{1,0:T(8,128)(2,1)S(1)} %collective-permute-done.2) | copy-start | bytes 798724
  22.5 17.0 %copy-start = (bf16[160,2048]{1,0:T(8,128)(2,1)}, bf16[160,2048]{1,0:T(8,128)(2,1)S(1)}, u32[]{:S(2)}) copy-start(bf16[160,2048]{1,0:T(8,128)(2,1)S(1)} %collective-permute-done.refs_1_) | copy-start | bytes 1966084
  22.5 17.0 %copy-start.1 = (bf16[160,2048]{1,0:T(8,128)(2,1)}, bf16[160,2048]{1,0:T(8,128)(2,1)S(1)}, u32[]{:S(2)}) copy-start(bf16[160,2048]{1,0:T(8,128)(2,1)S(1)} %collective-permute-done.1.refs_2_) | copy-start | bytes 1966084
  22.6 13.3 %collective-permute-start.8 = (bf16[160,2048]{1,0:T(8,128)(2,1)S(1)}, bf16[160,2048]{1,0:T(8,128)(2,1)}, u32[]{:S(2)}, u32[]{:S(2)}) collective-permute-start(bf16[160,2048]{1,0:T(8,128)(2,1)S(1)} %collective-permute-done.refs_1_), channel_id=1, source_target_pairs={{0,1},{1,0},{2,3},{3,2},{4,5},{5,4},{6,7},{7,6},{8,9},{9,8},{10,11... | collective-permute-start | bytes 1966088 | tf_op jit(solution)/shard_map/ppermute | solution.py:318
  22.7 13.2 %collective-permute-start.9 = (bf16[160,2048]{1,0:T(8,128)(2,1)S(1)}, bf16[160,2048]{1,0:T(8,128)(2,1)}, u32[]{:S(2)}, u32[]{:S(2)}) collective-permute-start(bf16[160,2048]{1,0:T(8,128)(2,1)S(1)} %collective-permute-done.1.refs_2_), channel_id=1, source_target_pairs={{0,1},{1,0},{2,3},{3,2},{4,5},{5,4},{6,7},{7,6},{8,9},{9,8},{10,11... | collective-permute-start | bytes 1966088 | tf_op jit(solution)/shard_map/ppermute | solution.py:318
  23.2 9.7 %collective-permute-start.3 = (bf16[80,2048]{1,0:T(8,128)(2,1)S(1)}, bf16[80,2048]{1,0:T(8,128)(2,1)S(1)}, u32[]{:S(2)}, u32[]{:S(2)}) collective-permute-start(bf16[80,2048]{1,0:T(8,128)(2,1)S(1)} %slice.45), channel_id=1, source_target_pairs={{0,4},{1,5},{2,6},{3,7},{4,0},{5,1},{6,2},{7,3},{8,12},{9,13},{10,... | collective-permute-start | bytes 983048 | tf_op jit(solution)/shard_map/ppermute | solution.py:318
  23.8 14.5 %copy-start.6 = (bf16[1040,128]{1,0:T(8,128)(2,1)}, bf16[1040,128]{1,0:T(8,128)(2,1)S(1)}, u32[]{:S(2)}) copy-start(bf16[1040,128]{1,0:T(8,128)(2,1)S(1)} %collective-permute-done.5) | copy-start | bytes 798724
  23.8 9.4 %collective-permute-start.4 = (bf16[80,2048]{1,0:T(8,128)(2,1)S(1)}, bf16[80,2048]{1,0:T(8,128)(2,1)S(1)}, u32[]{:S(2)}, u32[]{:S(2)}) collective-permute-start(bf16[80,2048]{1,0:T(8,128)(2,1)S(1)} %slice.46), channel_id=1, source_target_pairs={{0,2},{1,3},{2,0},{3,1},{4,6},{5,7},{6,4},{7,5},{8,10},{9,11},{10,... | collective-permute-start | bytes 983048 | tf_op jit(solution)/shard_map/ppermute | solution.py:318
  26.8 9.0 %collective-permute-start.6 = (bf16[1040,128]{1,0:T(8,128)(2,1)S(1)}, bf16[1040,128]{1,0:T(8,128)(2,1)S(1)}, u32[]{:S(2)}, u32[]{:S(2)}) collective-permute-start(bf16[1040,128]{1,0:T(8,128)(2,1)S(1)} %collective-permute-done.2), channel_id=1, source_target_pairs={{0,8},{1,9},{2,10},{3,11},{4,12},{5,13},{6,14},{7,15},{8,0},{9,1},... | collective-permute-start | bytes 798728 | tf_op jit(solution)/shard_map/ppermute | solution.py:318
  32.9 4.3 %copy-start.4 = (bf16[80,2048]{1,0:T(8,128)(2,1)}, bf16[80,2048]{1,0:T(8,128)(2,1)S(1)}, u32[]{:S(2)}) copy-start(bf16[80,2048]{1,0:T(8,128)(2,1)S(1)} %collective-permute-done.3.refs_6_) | copy-start | bytes 983044
  32.9 2.9 %collective-permute-start.10 = (bf16[80,2048]{1,0:T(8,128)(2,1)S(1)}, bf16[80,2048]{1,0:T(8,128)(2,1)S(1)}, u32[]{:S(2)}, u32[]{:S(2)}) collective-permute-start(bf16[80,2048]{1,0:T(8,128)(2,1)S(1)} %collective-permute-done.3.refs_6_), channel_id=1, source_target_pairs={{0,1},{1,0},{2,3},{3,2},{4,5},{5,4},{6,7},{7,6},{8,9},{9,8},{10,11... | collective-permute-start | bytes 983048 | tf_op jit(solution)/shard_map/ppermute | solution.py:318
  33.2 4.0 %copy-start.5 = (bf16[80,2048]{1,0:T(8,128)(2,1)}, bf16[80,2048]{1,0:T(8,128)(2,1)S(1)}, u32[]{:S(2)}) copy-start(bf16[80,2048]{1,0:T(8,128)(2,1)S(1)} %collective-permute-done.4.refs_7_) | copy-start | bytes 983044
  33.2 2.7 %collective-permute-start.11 = (bf16[80,2048]{1,0:T(8,128)(2,1)S(1)}, bf16[80,2048]{1,0:T(8,128)(2,1)S(1)}, u32[]{:S(2)}, u32[]{:S(2)}) collective-permute-start(bf16[80,2048]{1,0:T(8,128)(2,1)S(1)} %collective-permute-done.4.refs_7_), channel_id=1, source_target_pairs={{0,1},{1,0},{2,3},{3,2},{4,5},{5,4},{6,7},{7,6},{8,9},{9,8},{10,11... | collective-permute-start | bytes 983048 | tf_op jit(solution)/shard_map/ppermute | solution.py:318
  35.8 2.4 %copy-start.3 = (bf16[1040,128]{1,0:T(8,128)(2,1)}, bf16[1040,128]{1,0:T(8,128)(2,1)S(1)}, u32[]{:S(2)}) copy-start(bf16[1040,128]{1,0:T(8,128)(2,1)S(1)} %collective-permute-done.6) | copy-start | bytes 798724
  35.8 1.4 %copy-start.8 = (bf16[80,2048]{1,0:T(8,128)(2,1)}, bf16[80,2048]{1,0:T(8,128)(2,1)S(1)}, u32[]{:S(2)}) copy-start(bf16[80,2048]{1,0:T(8,128)(2,1)S(1)} %collective-permute-done.10.refs_8_) | copy-start | bytes 983044
  35.9 1.3 %copy-start.9 = (bf16[80,2048]{1,0:T(8,128)(2,1)}, bf16[80,2048]{1,0:T(8,128)(2,1)S(1)}, u32[]{:S(2)}) copy-start(bf16[80,2048]{1,0:T(8,128)(2,1)S(1)} %collective-permute-done.11.refs_9_) | copy-start | bytes 983044
  35.9 24.3 %collective-permute-start.12 = (bf16[160,2048]{1,0:T(8,128)(2,1)}, bf16[160,2048]{1,0:T(8,128)(2,1)}, u32[]{:S(2)}, u32[]{:S(2)}) collective-permute-start(bf16[160,2048]{1,0:T(8,128)(2,1)} %fusion.1), channel_id=1, source_target_pairs={{8,0},{9,1},{10,2},{11,3},{12,4},{13,5},{14,6},{15,7},{16,8},{17,9... | collective-permute-start | bytes 1966088 | tf_op jit(solution)/shard_map/ppermute | solution.py:358
  60.2 3.2 %collective-permute-start.13 = (bf16[160,2048]{1,0:T(8,128)(2,1)}, bf16[160,2048]{1,0:T(8,128)(2,1)S(1)}, u32[]{:S(2)}, u32[]{:S(2)}) collective-permute-start(bf16[160,2048]{1,0:T(8,128)(2,1)} %collective-permute-done.12.refs_0_), channel_id=1, source_target_pairs={{0,1},{1,0},{2,3},{3,2},{4,5},{5,4},{6,7},{7,6},{8,9},{9,8},{10,11... | collective-permute-start | bytes 1966088 | tf_op jit(solution)/shard_map/ppermute | solution.py:318
  63.4 0.9 copy-start.7
  83.3 31.5 %collective-permute-start.16 = (f32[320,128]{1,0:T(8,128)}, f32[320,128]{1,0:T(8,128)S(1)}, u32[]{:S(2)}, u32[]{:S(2)}) collective-permute-start(f32[320,128]{1,0:T(8,128)} %shard_map.49), channel_id=1, source_target_pairs={{0,8},{1,9},{2,10},{3,11},{4,12},{5,13},{6,14},{7,15},{8,0},{9,1},... | collective-permute-start | bytes 491528 | tf_op jit(solution)/shard_map/ppermute | solution.py:318
  102.8 12.0 %collective-permute-start.14 = (f32[320,128]{1,0:T(8,128)}, f32[320,128]{1,0:T(8,128)S(1)}, u32[]{:S(2)}, u32[]{:S(2)}) collective-permute-start(f32[320,128]{1,0:T(8,128)} %get-tuple-element.40), channel_id=1, source_target_pairs={{0,24},{1,25},{2,26},{3,27},{4,28},{5,29},{6,30},{7,31},{8,16},{9,... | collective-permute-start | bytes 491528 | tf_op jit(solution)/shard_map/ppermute | solution.py:318
  104.6 15.7 %collective-permute-start.15 = (f32[320,128]{1,0:T(8,128)}, f32[320,128]{1,0:T(8,128)S(1)}, u32[]{:S(2)}, u32[]{:S(2)}) collective-permute-start(f32[320,128]{1,0:T(8,128)} %get-tuple-element.41), channel_id=1, source_target_pairs={{0,16},{1,17},{2,18},{3,19},{4,20},{5,21},{6,22},{7,23},{8,24},{9,... | collective-permute-start | bytes 491528 | tf_op jit(solution)/shard_map/ppermute | solution.py:318

commit v5 on v4

--- a/solution.py
+++ b/solution.py
@@ -336,11 +336,11 @@
     across = flip(packet, 2 * GROUP)
     next_door = flip(packet, GROUP)
     twin = flip(data, 1)
-    near, side, across = lax.optimization_barrier((near, side, across))
+    near_held, side_held, across = lax.optimization_barrier((near, side, across))
     far_low = flip(near[:half], 4)
     far_high = flip(side[half:], 2)
-    near_twin = flip(near, 1)
-    side_twin = flip(side, 1)
+    near_twin = flip(near_held, 1)
+    side_twin = flip(side_held, 1)
     far_low_twin = flip(far_low, 1)
     far_high_twin = flip(far_high, 1)
     far = jnp.concatenate([far_low, far_high], axis=0)

time: 123 us -> 122 us (level)
  waiting for transfers between devices: 20.1 us -> 16 us
  starting transfers between devices: 17.5 us -> 20.6 us
    ppermute x16, waiting for transfers between devices: 20.1 us -> 16 us  [flip(): return lax.ppermute(value, 'sens', [(i, i ^ bits) for i in range(devices)])]
    ppermute x16, starting transfers between devices: 16.2 us -> 19.3 us  [flip(): return lax.ppermute(value, 'sens', [(i, i ^ bits) for i in range(devices)])]
  transfers between devices with their start and end apart: 17 -> 17, of which waited for: 4 -> 7; matrix products, arithmetic and copies ran while one was open for 15% -> 15% of each run, Pallas kernels for 36% -> 36%
where the time goes in v5:
time: 122 us; the launch traced here: 121 us
  Pallas kernels  62.9 us (52%)
  starting transfers between devices  20.6 us (17%)
  waiting for transfers between devices  16 us (13%)
  other arithmetic  14.9 us (12%)
  local copies, waits for them, and re-layouts  6.65 us (5%)
    pallas_call x3, Pallas kernels, matched_stacks(): pl.pallas_call(kernel, grid_spec=pltpu.PrefetchScalarGridSpec(num_scalar_...  36.4 us
    ppermute x16, starting transfers between devices, flip(): return lax.ppermute(value, 'sens', [(i, i ^ bits) for i in range(devices)])  19.3 us
    pallas_call x1, Pallas kernels, early_tables(): pl.pallas_call(kernel, grid_spec=pltpu.PrefetchScalarGridSpec(num_scalar_...  17.1 us
    ppermute x16, waiting for transfers between devices, flip(): return lax.ppermute(value, 'sens', [(i, i ^ bits) for i in range(devices)])  16 us
    pallas_call x1, Pallas kernels, late_tables(): pl.pallas_call(kernel, grid_spec=pltpu.PrefetchScalarGridSpec(num_scalar_...  9.34 us
    convert_element_type x3, other arithmetic, stacks_of(): chosen[:, :item_rows].astype(jnp.float32)  4.71 us
    select_n x1, other arithmetic, body(): jnp.where(chip == 0, data, jnp.where(chip == 1, near, jnp.where(chip == 2...  2.48 us
  transfers between devices with their start and end apart: 17, of which 7 were waited for; matrix products, arithmetic and copies ran while one was open for 15% of the time, Pallas kernels for 36%

profile of v5, /device:TPU:0, one launch (start us, length us, event | category | flops | bytes accessed | tf_op | source)
XLA Modules:
  0.0 121.3 jit_solution(2740061053199075412)
XLA Ops:
  0.0 2.9 %collective-permute-start = (bf16[160,2048]{1,0:T(8,128)(2,1)}, bf16[160,2048]{1,0:T(8,128)(2,1)S(1)}, u32[]{:S(2)}, u32[]{:S(2)}) collective-permute-start(bf16[160,2048]{1,0:T(8,128)(2,1)} %refs_0_.1), channel_id=1, source_target_pairs={{0,2},{1,3},{2,0},{3,1},{4,6},{5,7},{6,4},{7,5},{8,10},{9,11},{10,... | collective-permute-start | bytes 1966088 | tf_op jit(solution)/shard_map/ppermute | solution.py:318
  2.9 1.5 %collective-permute-start.1 = (bf16[160,2048]{1,0:T(8,128)(2,1)}, bf16[160,2048]{1,0:T(8,128)(2,1)S(1)}, u32[]{:S(2)}, u32[]{:S(2)}) collective-permute-start(bf16[160,2048]{1,0:T(8,128)(2,1)} %refs_0_.1), channel_id=1, source_target_pairs={{0,4},{1,5},{2,6},{3,7},{4,0},{5,1},{6,2},{7,3},{8,12},{9,13},{10,... | collective-permute-start | bytes 1966088 | tf_op jit(solution)/shard_map/ppermute | solution.py:318
  4.5 1.0 reshape.73
  5.5 0.8 rev.3
  6.3 0.7 convert_element_type.30
  7.2 0.7 convert_element_type.32
  8.2 2.6 %collective-permute-start.4 = (bf16[1040,128]{1,0:T(8,128)(2,1)S(1)}, bf16[1040,128]{1,0:T(8,128)(2,1)S(1)}, u32[]{:S(2)}, u32[]{:S(2)}) collective-permute-start(bf16[1040,128]{1,0:T(8,128)(2,1)S(1)} %concatenate.10), channel_id=1, source_target_pairs={{0,16},{1,17},{2,18},{3,19},{4,20},{5,21},{6,22},{7,23},{8,24},{9,... | collective-permute-start | bytes 798728 | tf_op jit(solution)/shard_map/ppermute | solution.py:318
  10.8 1.6 %collective-permute-start.5 = (bf16[1040,128]{1,0:T(8,128)(2,1)S(1)}, bf16[1040,128]{1,0:T(8,128)(2,1)S(1)}, u32[]{:S(2)}, u32[]{:S(2)}) collective-permute-start(bf16[1040,128]{1,0:T(8,128)(2,1)S(1)} %concatenate.10), channel_id=1, source_target_pairs={{0,8},{1,9},{2,10},{3,11},{4,12},{5,13},{6,14},{7,15},{8,0},{9,1},... | collective-permute-start | bytes 798728 | tf_op jit(solution)/shard_map/ppermute | solution.py:318
  12.8 0.8 slice_convert_fusion
  13.6 4.3 %collective-permute-done.refs_1_ = bf16[160,2048]{1,0:T(8,128)(2,1)S(1)} collective-permute-done((bf16[160,2048]{1,0:T(8,128)(2,1)}, bf16[160,2048]{1,0:T(8,128)(2,1)S(1)}, u32[]{:S(2)}, u32[]{:S(2)}) %collective-permute-start) | collective-permute-done | bytes 655392 | tf_op jit(solution)/shard_map/ppermute | solution.py:318
  17.9 1.8 %collective-permute-start.2 = (bf16[80,2048]{1,0:T(8,128)(2,1)S(1)}, bf16[80,2048]{1,0:T(8,128)(2,1)S(1)}, u32[]{:S(2)}, u32[]{:S(2)}) collective-permute-start(bf16[80,2048]{1,0:T(8,128)(2,1)S(1)} %slice.60), channel_id=1, source_target_pairs={{0,4},{1,5},{2,6},{3,7},{4,0},{5,1},{6,2},{7,3},{8,12},{9,13},{10,... | collective-permute-start | bytes 983048 | tf_op jit(solution)/shard_map/ppermute | solution.py:318
  19.8 1.6 %collective-permute-start.3 = (bf16[80,2048]{1,0:T(8,128)(2,1)S(1)}, bf16[80,2048]{1,0:T(8,128)(2,1)S(1)}, u32[]{:S(2)}, u32[]{:S(2)}) collective-permute-start(bf16[80,2048]{1,0:T(8,128)(2,1)S(1)} %slice.61), channel_id=1, source_target_pairs={{0,2},{1,3},{2,0},{3,1},{4,6},{5,7},{6,4},{7,5},{8,10},{9,11},{10,... | collective-permute-start | bytes 983048 | tf_op jit(solution)/shard_map/ppermute | solution.py:318
  21.3 1.2 collective-permute-done.4
  25.6 1.2 collective-permute-start.6
  27.0 1.2 collective-permute-done.3.refs_7_
  28.1 2.5 %fusion.1 = bf16[160,2048]{1,0:T(8,128)(2,1)} fusion(bf16[160,2048]{1,0:T(8,128)(2,1)} %refs_0_.1, bf16[160,2048]{1,0:T(8,128)(2,1)S(1)} %collective-permute-done.refs_1_, bf16[160,2048]{1,0:T(8,128)(2,1)S(1)} %collective-permute-done.1.refs_2_, bf16[80,2048]{1,0:T(8,128)(2,1)S(1)} %collective-permute-done.3.refs_7_, ...), kind=kLoop, calls=%fused_computation.2 | loop fusion | flops 2293760 | bytes 3276803 | tf_op jit(solution)/shard_map/jit(_where)/select_n | solution.py:348
  30.6 3.4 %collective-permute-done.6 = bf16[1040,128]{1,0:T(8,128)(2,1)S(1)} collective-permute-done((bf16[1040,128]{1,0:T(8,128)(2,1)S(1)}, bf16[1040,128]{1,0:T(8,128)(2,1)S(1)}, u32[]{:S(2)}, u32[]{:S(2)}) %collective-permute-start.6) | collective-permute-done | bytes 266272 | tf_op jit(solution)/shard_map/ppermute | solution.py:318
  34.1 1.3 %collective-permute-start.12 = (bf16[160,2048]{1,0:T(8,128)(2,1)}, bf16[160,2048]{1,0:T(8,128)(2,1)}, u32[]{:S(2)}, u32[]{:S(2)}) collective-permute-start(bf16[160,2048]{1,0:T(8,128)(2,1)} %fusion.1), channel_id=1, source_target_pairs={{8,0},{9,1},{10,2},{11,3},{12,4},{13,5},{14,6},{15,7},{16,8},{17,9... | collective-permute-start | bytes 1966088 | tf_op jit(solution)/shard_map/ppermute | solution.py:358
  37.8 17.1 %shard_map.46 = (bf16[65536,128]{1,0:T(8,128)(2,1)S(1)}, f32[2,26632,128]{2,1,0:T(8,128)S(1)}, bf16[16,320,128]{2,1,0:T(8,128)(2,1)S(1)}) custom-call(s32[10]{0:T(128)} %stack.73.place, bf16[160,2048]{1,0:T(8,128)(2,1)} %refs_0_.1, bf16[160,2048]{1,0:T(8,128)(2,1)} %copy-done, bf16[160,2048]{1,0:T(8,128)(2,1)} %copy-done.1, ...), custom_call_target="tpu_custom_call" | custom-call | tf_op jit(solution)/shard_map/pallas_call | solution.py:198
  55.0 0.7 maximum_convert_fusion
  55.6 2.1 %fusion.2 = f32[2,1024,128]{2,1,0:T(8,128)} fusion(bf16[1,1040,128]{2,1,0:T(8,128)(2,1)} %bitcast.29, bf16[1,1040,128]{2,1,0:T(8,128)(2,1)} %bitcast.26), kind=kLoop, calls=%fused_computation.7 | loop fusion | flops 1048576 | bytes 1581056 | tf_op jit(solution)/shard_map/convert_element_type | solution.py:377
  59.6 1.8 %slice_convert_fusion.1 = f32[1,1024,128]{2,1,0:T(8,128)} fusion(bf16[1,1040,128]{2,1,0:T(8,128)(2,1)} %bitcast.38), kind=kLoop, calls=%fused_computation.9 | loop fusion | flops 131072 | bytes 786432 | tf_op jit(solution)/shard_map/convert_element_type | solution.py:377
  61.4 0.9 copy-done.7
  62.3 9.3 %shard_map.47 = (bf16[65536,128]{1,0:T(8,128)(2,1)S(1)}, f32[2,26632,128]{2,1,0:T(8,128)S(1)}) custom-call(s32[2]{0:T(128)} %pad_add_fusion.place, bf16[16,320,128]{2,1,0:T(8,128)(2,1)S(1)} %get-tuple-element.34.tail_ref, bf16[65536,128]{1,0:T(8,128)(2,1)S(1)} %get-tuple-element.35.w_in, ...), custom_call_target="tpu_custom_call", output_to_operand_aliasing={{0}: (2, {}), {1}: (3, {})} | custom-call | tf_op jit(solution)/shard_map/pallas_call | solution.py:253
  71.6 9.7 %shard_map.49 = f32[320,128]{1,0:T(8,128)} custom-call(s32[512]{0:T(512)} %add_bitcast_fusion.1.sensor, f32[512]{0:T(512)} %mul.118.scale, f32[32,32,128]{2,1,0:T(8,128)} %bitcast.34, bf16[65536,128]{1,0:T(8,128)(2,1)S(1)} %get-tuple-element.38.w_ref, f32[2,26632,128]{2,1,0:T(8,128)S(1)} %get-tuple-element.39.g_ref), custom_call_target="tpu_custom_call" | custom-call | flops 8000000000 | bytes 8000000 | tf_op jit(solution)/shard_map/pallas_call | solution.py:289
  81.3 2.6 %collective-permute-start.16 = (f32[320,128]{1,0:T(8,128)}, f32[320,128]{1,0:T(8,128)S(1)}, u32[]{:S(2)}, u32[]{:S(2)}) collective-permute-start(f32[320,128]{1,0:T(8,128)} %shard_map.49), channel_id=1, source_target_pairs={{0,8},{1,9},{2,10},{3,11},{4,12},{5,13},{6,14},{7,15},{8,0},{9,1},... | collective-permute-start | bytes 491528 | tf_op jit(solution)/shard_map/ppermute | solution.py:318
  83.9 17.1 %shard_map.48 = (f32[320,128]{1,0:T(8,128)}, f32[320,128]{1,0:T(8,128)}) custom-call(s32[1024]{0:T(1024)} %bitcast.39, f32[1024]{0:T(1024)} %mul.103.scale, f32[64,32,128]{2,1,0:T(8,128)} %bitcast.35, bf16[65536,128]{1,0:T(8,128)(2,1)S(1)} %get-tuple-element.38.w_ref, f32[2,26632,128]{2,1,0:T(8,128)S(1)} %get-tuple-element.39.g_ref), custom_call_target="tpu_custom_call" | custom-call | flops 16000000000 | bytes 16000000 | tf_op jit(solution)/shard_map/pallas_call | solution.py:289
  101.0 2.4 %collective-permute-start.14 = (f32[320,128]{1,0:T(8,128)}, f32[320,128]{1,0:T(8,128)S(1)}, u32[]{:S(2)}, u32[]{:S(2)}) collective-permute-start(f32[320,128]{1,0:T(8,128)} %get-tuple-element.40), channel_id=1, source_target_pairs={{0,24},{1,25},{2,26},{3,27},{4,28},{5,29},{6,30},{7,31},{8,16},{9,... | collective-permute-start | bytes 491528 | tf_op jit(solution)/shard_map/ppermute | solution.py:318
  104.0 9.6 %shard_map.50 = f32[320,128]{1,0:T(8,128)} custom-call(s32[512]{0:T(512)} %add_bitcast_fusion.sensor, f32[512]{0:T(512)} %mul.123.scale, f32[32,32,128]{2,1,0:T(8,128)} %bitcast.33, bf16[65536,128]{1,0:T(8,128)(2,1)S(1)} %get-tuple-element.38.w_ref, f32[2,26632,128]{2,1,0:T(8,128)S(1)} %get-tuple-element.39.g_ref), custom_call_target="tpu_custom_call" | custom-call | flops 8000000000 | bytes 8000000 | tf_op jit(solution)/shard_map/pallas_call | solution.py:289
  113.6 5.7 %collective-permute-done.15 = f32[320,128]{1,0:T(8,128)S(1)} collective-permute-done((f32[320,128]{1,0:T(8,128)}, f32[320,128]{1,0:T(8,128)S(1)}, u32[]{:S(2)}, u32[]{:S(2)}) %collective-permute-start.15) | collective-permute-done | bytes 163872 | tf_op jit(solution)/shard_map/ppermute | solution.py:318
  119.3 1.0 select_select_fusion.3
  120.4 0.9 pad_maximum_fusion
  (72 shorter events, 9.0 us)
Async XLA Ops:
  0.0 17.9 %collective-permute-start = (bf16[160,2048]{1,0:T(8,128)(2,1)}, bf16[160,2048]{1,0:T(8,128)(2,1)S(1)}, u32[]{:S(2)}, u32[]{:S(2)}) collective-permute-start(bf16[160,2048]{1,0:T(8,128)(2,1)} %refs_0_.1), channel_id=1, source_target_pairs={{0,2},{1,3},{2,0},{3,1},{4,6},{5,7},{6,4},{7,5},{8,10},{9,11},{10,... | collective-permute-start | bytes 1966088 | tf_op jit(solution)/shard_map/ppermute | solution.py:318
  2.9 16.8 %collective-permute-start.1 = (bf16[160,2048]{1,0:T(8,128)(2,1)}, bf16[160,2048]{1,0:T(8,128)(2,1)S(1)}, u32[]{:S(2)}, u32[]{:S(2)}) collective-permute-start(bf16[160,2048]{1,0:T(8,128)(2,1)} %refs_0_.1), channel_id=1, source_target_pairs={{0,4},{1,5},{2,6},{3,7},{4,0},{5,1},{6,2},{7,3},{8,12},{9,13},{10,... | collective-permute-start | bytes 1966088 | tf_op jit(solution)/shard_map/ppermute | solution.py:318
  8.2 14.3 %collective-permute-start.4 = (bf16[1040,128]{1,0:T(8,128)(2,1)S(1)}, bf16[1040,128]{1,0:T(8,128)(2,1)S(1)}, u32[]{:S(2)}, u32[]{:S(2)}) collective-permute-start(bf16[1040,128]{1,0:T(8,128)(2,1)S(1)} %concatenate.10), channel_id=1, source_target_pairs={{0,16},{1,17},{2,18},{3,19},{4,20},{5,21},{6,22},{7,23},{8,24},{9,... | collective-permute-start | bytes 798728 | tf_op jit(solution)/shard_map/ppermute | solution.py:318
  10.8 11.9 %collective-permute-start.5 = (bf16[1040,128]{1,0:T(8,128)(2,1)S(1)}, bf16[1040,128]{1,0:T(8,128)(2,1)S(1)}, u32[]{:S(2)}, u32[]{:S(2)}) collective-permute-start(bf16[1040,128]{1,0:T(8,128)(2,1)S(1)} %concatenate.10), channel_id=1, source_target_pairs={{0,8},{1,9},{2,10},{3,11},{4,12},{5,13},{6,14},{7,15},{8,0},{9,1},... | collective-permute-start | bytes 798728 | tf_op jit(solution)/shard_map/ppermute | solution.py:318
  12.4 13.2 %collective-permute-start.7 = (bf16[160,2048]{1,0:T(8,128)(2,1)}, bf16[160,2048]{1,0:T(8,128)(2,1)}, u32[]{:S(2)}, u32[]{:S(2)}) collective-permute-start(bf16[160,2048]{1,0:T(8,128)(2,1)} %refs_0_.1), channel_id=1, source_target_pairs={{0,1},{1,0},{2,3},{3,2},{4,5},{5,4},{6,7},{7,6},{8,9},{9,8},{10,11... | collective-permute-start | bytes 1966088 | tf_op jit(solution)/shard_map/ppermute | solution.py:318
  17.9 19.9 %copy-start = (bf16[160,2048]{1,0:T(8,128)(2,1)}, bf16[160,2048]{1,0:T(8,128)(2,1)S(1)}, u32[]{:S(2)}) copy-start(bf16[160,2048]{1,0:T(8,128)(2,1)S(1)} %collective-permute-done.refs_1_) | copy-start | bytes 1966084
  17.9 9.0 %collective-permute-start.2 = (bf16[80,2048]{1,0:T(8,128)(2,1)S(1)}, bf16[80,2048]{1,0:T(8,128)(2,1)S(1)}, u32[]{:S(2)}, u32[]{:S(2)}) collective-permute-start(bf16[80,2048]{1,0:T(8,128)(2,1)S(1)} %slice.60), channel_id=1, source_target_pairs={{0,4},{1,5},{2,6},{3,7},{4,0},{5,1},{6,2},{7,3},{8,12},{9,13},{10,... | collective-permute-start | bytes 983048 | tf_op jit(solution)/shard_map/ppermute | solution.py:318
  19.7 18.1 %copy-start.1 = (bf16[160,2048]{1,0:T(8,128)(2,1)}, bf16[160,2048]{1,0:T(8,128)(2,1)S(1)}, u32[]{:S(2)}) copy-start(bf16[160,2048]{1,0:T(8,128)(2,1)S(1)} %collective-permute-done.1.refs_2_) | copy-start | bytes 1966084
  19.8 8.4 %collective-permute-start.3 = (bf16[80,2048]{1,0:T(8,128)(2,1)S(1)}, bf16[80,2048]{1,0:T(8,128)(2,1)S(1)}, u32[]{:S(2)}, u32[]{:S(2)}) collective-permute-start(bf16[80,2048]{1,0:T(8,128)(2,1)S(1)} %slice.61), channel_id=1, source_target_pairs={{0,2},{1,3},{2,0},{3,1},{4,6},{5,7},{6,4},{7,5},{8,10},{9,11},{10,... | collective-permute-start | bytes 983048 | tf_op jit(solution)/shard_map/ppermute | solution.py:318
  22.5 14.0 %copy-start.2 = (bf16[1040,128]{1,0:T(8,128)(2,1)}, bf16[1040,128]{1,0:T(8,128)(2,1)S(1)}, u32[]{:S(2)}) copy-start(bf16[1040,128]{1,0:T(8,128)(2,1)S(1)} %collective-permute-done.4) | copy-start | bytes 798724
  22.5 11.6 %collective-permute-start.8 = (bf16[160,2048]{1,0:T(8,128)(2,1)S(1)}, bf16[160,2048]{1,0:T(8,128)(2,1)}, u32[]{:S(2)}, u32[]{:S(2)}) collective-permute-start(bf16[160,2048]{1,0:T(8,128)(2,1)S(1)} %collective-permute-done.refs_1_), channel_id=1, source_target_pairs={{0,1},{1,0},{2,3},{3,2},{4,5},{5,4},{6,7},{7,6},{8,9},{9,8},{10,11... | collective-permute-start | bytes 1966088 | tf_op jit(solution)/shard_map/ppermute | solution.py:318
  22.7 13.8 %copy-start.6 = (bf16[1040,128]{1,0:T(8,128)(2,1)}, bf16[1040,128]{1,0:T(8,128)(2,1)S(1)}, u32[]{:S(2)}) copy-start(bf16[1040,128]{1,0:T(8,128)(2,1)S(1)} %collective-permute-done.5) | copy-start | bytes 798724
  22.7 11.4 %collective-permute-start.9 = (bf16[160,2048]{1,0:T(8,128)(2,1)S(1)}, bf16[160,2048]{1,0:T(8,128)(2,1)}, u32[]{:S(2)}, u32[]{:S(2)}) collective-permute-start(bf16[160,2048]{1,0:T(8,128)(2,1)S(1)} %collective-permute-done.1.refs_2_), channel_id=1, source_target_pairs={{0,1},{1,0},{2,3},{3,2},{4,5},{5,4},{6,7},{7,6},{8,9},{9,8},{10,11... | collective-permute-start | bytes 1966088 | tf_op jit(solution)/shard_map/ppermute | solution.py:318
  25.6 8.5 %collective-permute-start.6 = (bf16[1040,128]{1,0:T(8,128)(2,1)S(1)}, bf16[1040,128]{1,0:T(8,128)(2,1)S(1)}, u32[]{:S(2)}, u32[]{:S(2)}) collective-permute-start(bf16[1040,128]{1,0:T(8,128)(2,1)S(1)} %collective-permute-done.4), channel_id=1, source_target_pairs={{0,8},{1,9},{2,10},{3,11},{4,12},{5,13},{6,14},{7,15},{8,0},{9,1},... | collective-permute-start | bytes 798728 | tf_op jit(solution)/shard_map/ppermute | solution.py:318
  26.9 8.6 %copy-start.4 = (bf16[80,2048]{1,0:T(8,128)(2,1)}, bf16[80,2048]{1,0:T(8,128)(2,1)S(1)}, u32[]{:S(2)}) copy-start(bf16[80,2048]{1,0:T(8,128)(2,1)S(1)} %collective-permute-done.2.refs_6_) | copy-start | bytes 983044
  26.9 7.2 %collective-permute-start.10 = (bf16[80,2048]{1,0:T(8,128)(2,1)S(1)}, bf16[80,2048]{1,0:T(8,128)(2,1)S(1)}, u32[]{:S(2)}, u32[]{:S(2)}) collective-permute-start(bf16[80,2048]{1,0:T(8,128)(2,1)S(1)} %collective-permute-done.2.refs_6_), channel_id=1, source_target_pairs={{0,1},{1,0},{2,3},{3,2},{4,5},{5,4},{6,7},{7,6},{8,9},{9,8},{10,11... | collective-permute-start | bytes 983048 | tf_op jit(solution)/shard_map/ppermute | solution.py:318
  28.1 7.3 %copy-start.5 = (bf16[80,2048]{1,0:T(8,128)(2,1)}, bf16[80,2048]{1,0:T(8,128)(2,1)S(1)}, u32[]{:S(2)}) copy-start(bf16[80,2048]{1,0:T(8,128)(2,1)S(1)} %collective-permute-done.3.refs_7_) | copy-start | bytes 983044
  28.1 6.0 %collective-permute-start.11 = (bf16[80,2048]{1,0:T(8,128)(2,1)S(1)}, bf16[80,2048]{1,0:T(8,128)(2,1)S(1)}, u32[]{:S(2)}, u32[]{:S(2)}) collective-permute-start(bf16[80,2048]{1,0:T(8,128)(2,1)S(1)} %collective-permute-done.3.refs_7_), channel_id=1, source_target_pairs={{0,1},{1,0},{2,3},{3,2},{4,5},{5,4},{6,7},{7,6},{8,9},{9,8},{10,11... | collective-permute-start | bytes 983048 | tf_op jit(solution)/shard_map/ppermute | solution.py:318
  34.1 2.4 %copy-start.3 = (bf16[1040,128]{1,0:T(8,128)(2,1)}, bf16[1040,128]{1,0:T(8,128)(2,1)S(1)}, u32[]{:S(2)}) copy-start(bf16[1040,128]{1,0:T(8,128)(2,1)S(1)} %collective-permute-done.6) | copy-start | bytes 798724
  34.1 1.3 %copy-start.8 = (bf16[80,2048]{1,0:T(8,128)(2,1)}, bf16[80,2048]{1,0:T(8,128)(2,1)S(1)}, u32[]{:S(2)}) copy-start(bf16[80,2048]{1,0:T(8,128)(2,1)S(1)} %collective-permute-done.10.refs_8_) | copy-start | bytes 983044
  34.1 1.3 %copy-start.9 = (bf16[80,2048]{1,0:T(8,128)(2,1)}, bf16[80,2048]{1,0:T(8,128)(2,1)S(1)}, u32[]{:S(2)}) copy-start(bf16[80,2048]{1,0:T(8,128)(2,1)S(1)} %collective-permute-done.11.refs_9_) | copy-start | bytes 983044
  34.1 24.3 %collective-permute-start.12 = (bf16[160,2048]{1,0:T(8,128)(2,1)}, bf16[160,2048]{1,0:T(8,128)(2,1)}, u32[]{:S(2)}, u32[]{:S(2)}) collective-permute-start(bf16[160,2048]{1,0:T(8,128)(2,1)} %fusion.1), channel_id=1, source_target_pairs={{8,0},{9,1},{10,2},{11,3},{12,4},{13,5},{14,6},{15,7},{16,8},{17,9... | collective-permute-start | bytes 1966088 | tf_op jit(solution)/shard_map/ppermute | solution.py:358
  58.4 3.0 %collective-permute-start.13 = (bf16[160,2048]{1,0:T(8,128)(2,1)}, bf16[160,2048]{1,0:T(8,128)(2,1)S(1)}, u32[]{:S(2)}, u32[]{:S(2)}) collective-permute-start(bf16[160,2048]{1,0:T(8,128)(2,1)} %collective-permute-done.12.refs_0_), channel_id=1, source_target_pairs={{0,1},{1,0},{2,3},{3,2},{4,5},{5,4},{6,7},{7,6},{8,9},{9,8},{10,11... | collective-permute-start | bytes 1966088 | tf_op jit(solution)/shard_map/ppermute | solution.py:318
  61.4 0.9 copy-start.7
  81.3 32.3 %collective-permute-start.16 = (f32[320,128]{1,0:T(8,128)}, f32[320,128]{1,0:T(8,128)S(1)}, u32[]{:S(2)}, u32[]{:S(2)}) collective-permute-start(f32[320,128]{1,0:T(8,128)} %shard_map.49), channel_id=1, source_target_pairs={{0,8},{1,9},{2,10},{3,11},{4,12},{5,13},{6,14},{7,15},{8,0},{9,1},... | collective-permute-start | bytes 491528 | tf_op jit(solution)/shard_map/ppermute | solution.py:318
  101.0 12.6 %collective-permute-start.14 = (f32[320,128]{1,0:T(8,128)}, f32[320,128]{1,0:T(8,128)S(1)}, u32[]{:S(2)}, u32[]{:S(2)}) collective-permute-start(f32[320,128]{1,0:T(8,128)} %get-tuple-element.40), channel_id=1, source_target_pairs={{0,24},{1,25},{2,26},{3,27},{4,28},{5,29},{6,30},{7,31},{8,16},{9,... | collective-permute-start | bytes 491528 | tf_op jit(solution)/shard_map/ppermute | solution.py:318
  103.4 15.9 %collective-permute-start.15 = (f32[320,128]{1,0:T(8,128)}, f32[320,128]{1,0:T(8,128)S(1)}, u32[]{:S(2)}, u32[]{:S(2)}) collective-permute-start(f32[320,128]{1,0:T(8,128)} %get-tuple-element.41), channel_id=1, source_target_pairs={{0,16},{1,17},{2,18},{3,19},{4,20},{5,21},{6,22},{7,23},{8,24},{9,... | collective-permute-start | bytes 491528 | tf_op jit(solution)/shard_map/ppermute | solution.py:318

commit v6 on v5

--- a/solution.py
+++ b/solution.py
@@ -381,12 +381,10 @@
         scale = (gain * lax.rsqrt(power / length + EPSILON)).reshape(-1)
         return matched_stacks(sensor, scale, wide, tables, per_dev, lag_rows)
 
-    far_parts = stacks_of(range(layers // 2, layers))
-    received = [flip(far_parts[q - layers // 2], GROUP * q) for q in range(layers // 2, layers)]
-    near_parts = [stacks_of([q])[0] for q in range(layers // 2)]
-    received = [
-        near_parts[q] if q == 0 else flip(near_parts[q], GROUP * q) for q in range(layers // 2)
-    ] + received
+    (middle,) = stacks_of([2])
+    nearby, farthest = stacks_of([1, 3])
+    (own,) = stacks_of([0])
+    received = [own, flip(nearby, GROUP), flip(middle, 2 * GROUP), flip(farthest, 3 * GROUP)]
     ordered = []
     for slot in range(layers):
         value = received[slot]

time: 122 us -> 116 us (0.951)
  waiting for transfers between devices: 16 us -> 10.4 us
    ppermute x16, waiting for transfers between devices: 16 us -> 10.4 us  [flip(): return lax.ppermute(value, 'sens', [(i, i ^ bits) for i in range(devices)])]
  transfers between devices with their start and end apart: 17 -> 17, of which waited for: 7 -> 6; matrix products, arithmetic and copies ran while one was open for 15% -> 16% of each run, Pallas kernels for 36% -> 38%
where the time goes in v6:
time: 116 us
  Pallas kernels  62.9 us (54%)
  starting transfers between devices  20.5 us (18%)
  other arithmetic  14.9 us (13%)
  waiting for transfers between devices  10.4 us (9%)
  local copies, waits for them, and re-layouts  6.65 us (6%)
    pallas_call x3, Pallas kernels, matched_stacks(): pl.pallas_call(kernel, grid_spec=pltpu.PrefetchScalarGridSpec(num_scalar_...  36.4 us
    ppermute x16, starting transfers between devices, flip(): return lax.ppermute(value, 'sens', [(i, i ^ bits) for i in range(devices)])  19.2 us
    pallas_call x1, Pallas kernels, early_tables(): pl.pallas_call(kernel, grid_spec=pltpu.PrefetchScalarGridSpec(num_scalar_...  17.1 us
    ppermute x16, waiting for transfers between devices, flip(): return lax.ppermute(value, 'sens', [(i, i ^ bits) for i in range(devices)])  10.4 us
    pallas_call x1, Pallas kernels, late_tables(): pl.pallas_call(kernel, grid_spec=pltpu.PrefetchScalarGridSpec(num_scalar_...  9.34 us
    convert_element_type x3, other arithmetic, stacks_of(): chosen[:, :item_rows].astype(jnp.float32)  4.71 us
    select_n x1, other arithmetic, body(): jnp.where(chip == 0, data, jnp.where(chip == 1, near, jnp.where(chip == 2...  2.48 us
  transfers between devices with their start and end apart: 17, of which 6 were waited for; matrix products, arithmetic and copies ran while one was open for 16% of the time, Pallas kernels for 38%

profile of v6, /device:TPU:0, one launch (start us, length us, event | category | flops | bytes accessed | tf_op | source)
XLA Modules:
  0.0 115.7 jit_solution(16365098249952932049)
XLA Ops:
  0.0 2.9 %collective-permute-start = (bf16[160,2048]{1,0:T(8,128)(2,1)}, bf16[160,2048]{1,0:T(8,128)(2,1)S(1)}, u32[]{:S(2)}, u32[]{:S(2)}) collective-permute-start(bf16[160,2048]{1,0:T(8,128)(2,1)} %refs_0_.1), channel_id=1, source_target_pairs={{0,2},{1,3},{2,0},{3,1},{4,6},{5,7},{6,4},{7,5},{8,10},{9,11},{10,... | collective-permute-start | bytes 1966088 | tf_op jit(solution)/shard_map/ppermute | solution.py:318
  2.9 1.5 %collective-permute-start.1 = (bf16[160,2048]{1,0:T(8,128)(2,1)}, bf16[160,2048]{1,0:T(8,128)(2,1)S(1)}, u32[]{:S(2)}, u32[]{:S(2)}) collective-permute-start(bf16[160,2048]{1,0:T(8,128)(2,1)} %refs_0_.1), channel_id=1, source_target_pairs={{0,4},{1,5},{2,6},{3,7},{4,0},{5,1},{6,2},{7,3},{8,12},{9,13},{10,... | collective-permute-start | bytes 1966088 | tf_op jit(solution)/shard_map/ppermute | solution.py:318
  4.5 1.0 reshape.73
  5.5 0.8 rev.3
  6.3 0.7 convert_element_type.30
  7.2 0.7 convert_element_type.32
  8.2 2.6 %collective-permute-start.4 = (bf16[1040,128]{1,0:T(8,128)(2,1)S(1)}, bf16[1040,128]{1,0:T(8,128)(2,1)S(1)}, u32[]{:S(2)}, u32[]{:S(2)}) collective-permute-start(bf16[1040,128]{1,0:T(8,128)(2,1)S(1)} %concatenate.10), channel_id=1, source_target_pairs={{0,16},{1,17},{2,18},{3,19},{4,20},{5,21},{6,22},{7,23},{8,24},{9,... | collective-permute-start | bytes 798728 | tf_op jit(solution)/shard_map/ppermute | solution.py:318
  10.8 1.6 %collective-permute-start.5 = (bf16[1040,128]{1,0:T(8,128)(2,1)S(1)}, bf16[1040,128]{1,0:T(8,128)(2,1)S(1)}, u32[]{:S(2)}, u32[]{:S(2)}) collective-permute-start(bf16[1040,128]{1,0:T(8,128)(2,1)S(1)} %concatenate.10), channel_id=1, source_target_pairs={{0,8},{1,9},{2,10},{3,11},{4,12},{5,13},{6,14},{7,15},{8,0},{9,1},... | collective-permute-start | bytes 798728 | tf_op jit(solution)/shard_map/ppermute | solution.py:318
  12.8 0.8 slice_convert_fusion
  13.6 4.3 %collective-permute-done.refs_1_ = bf16[160,2048]{1,0:T(8,128)(2,1)S(1)} collective-permute-done((bf16[160,2048]{1,0:T(8,128)(2,1)}, bf16[160,2048]{1,0:T(8,128)(2,1)S(1)}, u32[]{:S(2)}, u32[]{:S(2)}) %collective-permute-start) | collective-permute-done | bytes 655392 | tf_op jit(solution)/shard_map/ppermute | solution.py:318
  17.9 1.8 %collective-permute-start.2 = (bf16[80,2048]{1,0:T(8,128)(2,1)S(1)}, bf16[80,2048]{1,0:T(8,128)(2,1)S(1)}, u32[]{:S(2)}, u32[]{:S(2)}) collective-permute-start(bf16[80,2048]{1,0:T(8,128)(2,1)S(1)} %slice.60), channel_id=1, source_target_pairs={{0,4},{1,5},{2,6},{3,7},{4,0},{5,1},{6,2},{7,3},{8,12},{9,13},{10,... | collective-permute-start | bytes 983048 | tf_op jit(solution)/shard_map/ppermute | solution.py:318
  19.8 1.6 %collective-permute-start.3 = (bf16[80,2048]{1,0:T(8,128)(2,1)S(1)}, bf16[80,2048]{1,0:T(8,128)(2,1)S(1)}, u32[]{:S(2)}, u32[]{:S(2)}) collective-permute-start(bf16[80,2048]{1,0:T(8,128)(2,1)S(1)} %slice.61), channel_id=1, source_target_pairs={{0,2},{1,3},{2,0},{3,1},{4,6},{5,7},{6,4},{7,5},{8,10},{9,11},{10,... | collective-permute-start | bytes 983048 | tf_op jit(solution)/shard_map/ppermute | solution.py:318
  21.3 1.2 %collective-permute-done.4 = bf16[1040,128]{1,0:T(8,128)(2,1)S(1)} collective-permute-done((bf16[1040,128]{1,0:T(8,128)(2,1)S(1)}, bf16[1040,128]{1,0:T(8,128)(2,1)S(1)}, u32[]{:S(2)}, u32[]{:S(2)}) %collective-permute-start.4) | collective-permute-done | bytes 266272 | tf_op jit(solution)/shard_map/ppermute | solution.py:318
  25.6 1.1 collective-permute-start.6
  26.9 1.2 %collective-permute-done.3.refs_7_ = bf16[80,2048]{1,0:T(8,128)(2,1)S(1)} collective-permute-done((bf16[80,2048]{1,0:T(8,128)(2,1)S(1)}, bf16[80,2048]{1,0:T(8,128)(2,1)S(1)}, u32[]{:S(2)}, u32[]{:S(2)}) %collective-permute-start.3) | collective-permute-done | bytes 327712 | tf_op jit(solution)/shard_map/ppermute | solution.py:318
  28.1 2.5 %fusion.1 = bf16[160,2048]{1,0:T(8,128)(2,1)} fusion(bf16[160,2048]{1,0:T(8,128)(2,1)} %refs_0_.1, bf16[160,2048]{1,0:T(8,128)(2,1)S(1)} %collective-permute-done.refs_1_, bf16[160,2048]{1,0:T(8,128)(2,1)S(1)} %collective-permute-done.1.refs_2_, bf16[80,2048]{1,0:T(8,128)(2,1)S(1)} %collective-permute-done.3.refs_7_, ...), kind=kLoop, calls=%fused_computation.2 | loop fusion | flops 2293760 | bytes 3276803 | tf_op jit(solution)/shard_map/jit(_where)/select_n | solution.py:348
  30.6 3.4 %collective-permute-done.6 = bf16[1040,128]{1,0:T(8,128)(2,1)S(1)} collective-permute-done((bf16[1040,128]{1,0:T(8,128)(2,1)S(1)}, bf16[1040,128]{1,0:T(8,128)(2,1)S(1)}, u32[]{:S(2)}, u32[]{:S(2)}) %collective-permute-start.6) | collective-permute-done | bytes 266272 | tf_op jit(solution)/shard_map/ppermute | solution.py:318
  34.1 1.3 %collective-permute-start.12 = (bf16[160,2048]{1,0:T(8,128)(2,1)}, bf16[160,2048]{1,0:T(8,128)(2,1)}, u32[]{:S(2)}, u32[]{:S(2)}) collective-permute-start(bf16[160,2048]{1,0:T(8,128)(2,1)} %fusion.1), channel_id=1, source_target_pairs={{8,0},{9,1},{10,2},{11,3},{12,4},{13,5},{14,6},{15,7},{16,8},{17,9... | collective-permute-start | bytes 1966088 | tf_op jit(solution)/shard_map/ppermute | solution.py:358
  37.8 17.1 %shard_map.46 = (bf16[65536,128]{1,0:T(8,128)(2,1)S(1)}, f32[2,26632,128]{2,1,0:T(8,128)S(1)}, bf16[16,320,128]{2,1,0:T(8,128)(2,1)S(1)}) custom-call(s32[10]{0:T(128)} %stack.73.place, bf16[160,2048]{1,0:T(8,128)(2,1)} %refs_0_.1, bf16[160,2048]{1,0:T(8,128)(2,1)} %copy-done, bf16[160,2048]{1,0:T(8,128)(2,1)} %copy-done.1, ...), custom_call_target="tpu_custom_call" | custom-call | tf_op jit(solution)/shard_map/pallas_call | solution.py:198
  55.0 0.7 maximum_convert_fusion
  55.6 2.1 %fusion.2 = f32[2,1024,128]{2,1,0:T(8,128)} fusion(bf16[1,1040,128]{2,1,0:T(8,128)(2,1)} %bitcast.29, bf16[1,1040,128]{2,1,0:T(8,128)(2,1)} %bitcast.26), kind=kLoop, calls=%fused_computation.7 | loop fusion | flops 1048576 | bytes 1581056 | tf_op jit(solution)/shard_map/convert_element_type | solution.py:377
  57.7 0.7 slice_convert_fusion.3
  59.6 1.8 %slice_convert_fusion.1 = f32[1,1024,128]{2,1,0:T(8,128)} fusion(bf16[1,1040,128]{2,1,0:T(8,128)(2,1)} %bitcast.38), kind=kLoop, calls=%fused_computation.9 | loop fusion | flops 131072 | bytes 786432 | tf_op jit(solution)/shard_map/convert_element_type | solution.py:377
  61.4 0.9 copy-done.7
  62.3 9.3 %shard_map.47 = (bf16[65536,128]{1,0:T(8,128)(2,1)S(1)}, f32[2,26632,128]{2,1,0:T(8,128)S(1)}) custom-call(s32[2]{0:T(128)} %pad_add_fusion.place, bf16[16,320,128]{2,1,0:T(8,128)(2,1)S(1)} %get-tuple-element.34.tail_ref, bf16[65536,128]{1,0:T(8,128)(2,1)S(1)} %get-tuple-element.35.w_in, ...), custom_call_target="tpu_custom_call", output_to_operand_aliasing={{0}: (2, {}), {1}: (3, {})} | custom-call | tf_op jit(solution)/shard_map/pallas_call | solution.py:253
  71.6 9.7 %shard_map.49 = f32[320,128]{1,0:T(8,128)} custom-call(s32[512]{0:T(512)} %add_bitcast_fusion.1.sensor, f32[512]{0:T(512)} %mul.118.scale, f32[32,32,128]{2,1,0:T(8,128)} %bitcast.34, bf16[65536,128]{1,0:T(8,128)(2,1)S(1)} %get-tuple-element.38.w_ref, f32[2,26632,128]{2,1,0:T(8,128)S(1)} %get-tuple-element.39.g_ref), custom_call_target="tpu_custom_call" | custom-call | flops 8000000000 | bytes 8000000 | tf_op jit(solution)/shard_map/pallas_call | solution.py:289
  81.3 3.5 %collective-permute-start.15 = (f32[320,128]{1,0:T(8,128)}, f32[320,128]{1,0:T(8,128)S(1)}, u32[]{:S(2)}, u32[]{:S(2)}) collective-permute-start(f32[320,128]{1,0:T(8,128)} %shard_map.49), channel_id=1, source_target_pairs={{0,16},{1,17},{2,18},{3,19},{4,20},{5,21},{6,22},{7,23},{8,24},{9,... | collective-permute-start | bytes 491528 | tf_op jit(solution)/shard_map/ppermute | solution.py:318
  84.8 17.1 %shard_map.48 = (f32[320,128]{1,0:T(8,128)}, f32[320,128]{1,0:T(8,128)}) custom-call(s32[1024]{0:T(1024)} %bitcast.39, f32[1024]{0:T(1024)} %mul.103.scale, f32[64,32,128]{2,1,0:T(8,128)} %bitcast.35, bf16[65536,128]{1,0:T(8,128)(2,1)S(1)} %get-tuple-element.38.w_ref, f32[2,26632,128]{2,1,0:T(8,128)S(1)} %get-tuple-element.39.g_ref), custom_call_target="tpu_custom_call" | custom-call | flops 16000000000 | bytes 16000000 | tf_op jit(solution)/shard_map/pallas_call | solution.py:289
  101.9 1.5 %collective-permute-start.14 = (f32[320,128]{1,0:T(8,128)}, f32[320,128]{1,0:T(8,128)S(1)}, u32[]{:S(2)}, u32[]{:S(2)}) collective-permute-start(f32[320,128]{1,0:T(8,128)} %get-tuple-element.40), channel_id=1, source_target_pairs={{0,24},{1,25},{2,26},{3,27},{4,28},{5,29},{6,30},{7,31},{8,16},{9,... | collective-permute-start | bytes 491528 | tf_op jit(solution)/shard_map/ppermute | solution.py:318
  104.0 9.6 %shard_map.50 = f32[320,128]{1,0:T(8,128)} custom-call(s32[512]{0:T(512)} %add_bitcast_fusion.sensor, f32[512]{0:T(512)} %mul.123.scale, f32[32,32,128]{2,1,0:T(8,128)} %bitcast.33, bf16[65536,128]{1,0:T(8,128)(2,1)S(1)} %get-tuple-element.38.w_ref, f32[2,26632,128]{2,1,0:T(8,128)S(1)} %get-tuple-element.39.g_ref), custom_call_target="tpu_custom_call" | custom-call | flops 8000000000 | bytes 8000000 | tf_op jit(solution)/shard_map/pallas_call | solution.py:289
  113.7 1.0 select_select_fusion.3
  114.8 0.9 pad_maximum_fusion
  (72 shorter events, 8.4 us)
Async XLA Ops:
  0.0 17.9 %collective-permute-start = (bf16[160,2048]{1,0:T(8,128)(2,1)}, bf16[160,2048]{1,0:T(8,128)(2,1)S(1)}, u32[]{:S(2)}, u32[]{:S(2)}) collective-permute-start(bf16[160,2048]{1,0:T(8,128)(2,1)} %refs_0_.1), channel_id=1, source_target_pairs={{0,2},{1,3},{2,0},{3,1},{4,6},{5,7},{6,4},{7,5},{8,10},{9,11},{10,... | collective-permute-start | bytes 1966088 | tf_op jit(solution)/shard_map/ppermute | solution.py:318
  2.9 16.8 %collective-permute-start.1 = (bf16[160,2048]{1,0:T(8,128)(2,1)}, bf16[160,2048]{1,0:T(8,128)(2,1)S(1)}, u32[]{:S(2)}, u32[]{:S(2)}) collective-permute-start(bf16[160,2048]{1,0:T(8,128)(2,1)} %refs_0_.1), channel_id=1, source_target_pairs={{0,4},{1,5},{2,6},{3,7},{4,0},{5,1},{6,2},{7,3},{8,12},{9,13},{10,... | collective-permute-start | bytes 1966088 | tf_op jit(solution)/shard_map/ppermute | solution.py:318
  8.2 14.3 %collective-permute-start.4 = (bf16[1040,128]{1,0:T(8,128)(2,1)S(1)}, bf16[1040,128]{1,0:T(8,128)(2,1)S(1)}, u32[]{:S(2)}, u32[]{:S(2)}) collective-permute-start(bf16[1040,128]{1,0:T(8,128)(2,1)S(1)} %concatenate.10), channel_id=1, source_target_pairs={{0,16},{1,17},{2,18},{3,19},{4,20},{5,21},{6,22},{7,23},{8,24},{9,... | collective-permute-start | bytes 798728 | tf_op jit(solution)/shard_map/ppermute | solution.py:318
  10.8 11.9 %collective-permute-start.5 = (bf16[1040,128]{1,0:T(8,128)(2,1)S(1)}, bf16[1040,128]{1,0:T(8,128)(2,1)S(1)}, u32[]{:S(2)}, u32[]{:S(2)}) collective-permute-start(bf16[1040,128]{1,0:T(8,128)(2,1)S(1)} %concatenate.10), channel_id=1, source_target_pairs={{0,8},{1,9},{2,10},{3,11},{4,12},{5,13},{6,14},{7,15},{8,0},{9,1},... | collective-permute-start | bytes 798728 | tf_op jit(solution)/shard_map/ppermute | solution.py:318
  12.4 13.2 %collective-permute-start.7 = (bf16[160,2048]{1,0:T(8,128)(2,1)}, bf16[160,2048]{1,0:T(8,128)(2,1)}, u32[]{:S(2)}, u32[]{:S(2)}) collective-permute-start(bf16[160,2048]{1,0:T(8,128)(2,1)} %refs_0_.1), channel_id=1, source_target_pairs={{0,1},{1,0},{2,3},{3,2},{4,5},{5,4},{6,7},{7,6},{8,9},{9,8},{10,11... | collective-permute-start | bytes 1966088 | tf_op jit(solution)/shard_map/ppermute | solution.py:318
  17.9 19.9 %copy-start = (bf16[160,2048]{1,0:T(8,128)(2,1)}, bf16[160,2048]{1,0:T(8,128)(2,1)S(1)}, u32[]{:S(2)}) copy-start(bf16[160,2048]{1,0:T(8,128)(2,1)S(1)} %collective-permute-done.refs_1_) | copy-start | bytes 1966084
  17.9 9.0 %collective-permute-start.2 = (bf16[80,2048]{1,0:T(8,128)(2,1)S(1)}, bf16[80,2048]{1,0:T(8,128)(2,1)S(1)}, u32[]{:S(2)}, u32[]{:S(2)}) collective-permute-start(bf16[80,2048]{1,0:T(8,128)(2,1)S(1)} %slice.60), channel_id=1, source_target_pairs={{0,4},{1,5},{2,6},{3,7},{4,0},{5,1},{6,2},{7,3},{8,12},{9,13},{10,... | collective-permute-start | bytes 983048 | tf_op jit(solution)/shard_map/ppermute | solution.py:318
  19.7 18.1 %copy-start.1 = (bf16[160,2048]{1,0:T(8,128)(2,1)}, bf16[160,2048]{1,0:T(8,128)(2,1)S(1)}, u32[]{:S(2)}) copy-start(bf16[160,2048]{1,0:T(8,128)(2,1)S(1)} %collective-permute-done.1.refs_2_) | copy-start | bytes 1966084
  19.8 8.4 %collective-permute-start.3 = (bf16[80,2048]{1,0:T(8,128)(2,1)S(1)}, bf16[80,2048]{1,0:T(8,128)(2,1)S(1)}, u32[]{:S(2)}, u32[]{:S(2)}) collective-permute-start(bf16[80,2048]{1,0:T(8,128)(2,1)S(1)} %slice.61), channel_id=1, source_target_pairs={{0,2},{1,3},{2,0},{3,1},{4,6},{5,7},{6,4},{7,5},{8,10},{9,11},{10,... | collective-permute-start | bytes 983048 | tf_op jit(solution)/shard_map/ppermute | solution.py:318
  22.5 14.0 %copy-start.6 = (bf16[1040,128]{1,0:T(8,128)(2,1)}, bf16[1040,128]{1,0:T(8,128)(2,1)S(1)}, u32[]{:S(2)}) copy-start(bf16[1040,128]{1,0:T(8,128)(2,1)S(1)} %collective-permute-done.4) | copy-start | bytes 798724
  22.5 11.6 %collective-permute-start.8 = (bf16[160,2048]{1,0:T(8,128)(2,1)S(1)}, bf16[160,2048]{1,0:T(8,128)(2,1)}, u32[]{:S(2)}, u32[]{:S(2)}) collective-permute-start(bf16[160,2048]{1,0:T(8,128)(2,1)S(1)} %collective-permute-done.refs_1_), channel_id=1, source_target_pairs={{0,1},{1,0},{2,3},{3,2},{4,5},{5,4},{6,7},{7,6},{8,9},{9,8},{10,11... | collective-permute-start | bytes 1966088 | tf_op jit(solution)/shard_map/ppermute | solution.py:318
  22.7 13.8 %copy-start.2 = (bf16[1040,128]{1,0:T(8,128)(2,1)}, bf16[1040,128]{1,0:T(8,128)(2,1)S(1)}, u32[]{:S(2)}) copy-start(bf16[1040,128]{1,0:T(8,128)(2,1)S(1)} %collective-permute-done.5) | copy-start | bytes 798724
  22.7 11.4 %collective-permute-start.9 = (bf16[160,2048]{1,0:T(8,128)(2,1)S(1)}, bf16[160,2048]{1,0:T(8,128)(2,1)}, u32[]{:S(2)}, u32[]{:S(2)}) collective-permute-start(bf16[160,2048]{1,0:T(8,128)(2,1)S(1)} %collective-permute-done.1.refs_2_), channel_id=1, source_target_pairs={{0,1},{1,0},{2,3},{3,2},{4,5},{5,4},{6,7},{7,6},{8,9},{9,8},{10,11... | collective-permute-start | bytes 1966088 | tf_op jit(solution)/shard_map/ppermute | solution.py:318
  25.6 8.5 %collective-permute-start.6 = (bf16[1040,128]{1,0:T(8,128)(2,1)S(1)}, bf16[1040,128]{1,0:T(8,128)(2,1)S(1)}, u32[]{:S(2)}, u32[]{:S(2)}) collective-permute-start(bf16[1040,128]{1,0:T(8,128)(2,1)S(1)} %collective-permute-done.4), channel_id=1, source_target_pairs={{0,8},{1,9},{2,10},{3,11},{4,12},{5,13},{6,14},{7,15},{8,0},{9,1},... | collective-permute-start | bytes 798728 | tf_op jit(solution)/shard_map/ppermute | solution.py:318
  26.9 8.6 %copy-start.4 = (bf16[80,2048]{1,0:T(8,128)(2,1)}, bf16[80,2048]{1,0:T(8,128)(2,1)S(1)}, u32[]{:S(2)}) copy-start(bf16[80,2048]{1,0:T(8,128)(2,1)S(1)} %collective-permute-done.2.refs_6_) | copy-start | bytes 983044
  26.9 7.2 %collective-permute-start.10 = (bf16[80,2048]{1,0:T(8,128)(2,1)S(1)}, bf16[80,2048]{1,0:T(8,128)(2,1)S(1)}, u32[]{:S(2)}, u32[]{:S(2)}) collective-permute-start(bf16[80,2048]{1,0:T(8,128)(2,1)S(1)} %collective-permute-done.2.refs_6_), channel_id=1, source_target_pairs={{0,1},{1,0},{2,3},{3,2},{4,5},{5,4},{6,7},{7,6},{8,9},{9,8},{10,11... | collective-permute-start | bytes 983048 | tf_op jit(solution)/shard_map/ppermute | solution.py:318
  28.1 7.3 %copy-start.5 = (bf16[80,2048]{1,0:T(8,128)(2,1)}, bf16[80,2048]{1,0:T(8,128)(2,1)S(1)}, u32[]{:S(2)}) copy-start(bf16[80,2048]{1,0:T(8,128)(2,1)S(1)} %collective-permute-done.3.refs_7_) | copy-start | bytes 983044
  28.1 6.0 %collective-permute-start.11 = (bf16[80,2048]{1,0:T(8,128)(2,1)S(1)}, bf16[80,2048]{1,0:T(8,128)(2,1)S(1)}, u32[]{:S(2)}, u32[]{:S(2)}) collective-permute-start(bf16[80,2048]{1,0:T(8,128)(2,1)S(1)} %collective-permute-done.3.refs_7_), channel_id=1, source_target_pairs={{0,1},{1,0},{2,3},{3,2},{4,5},{5,4},{6,7},{7,6},{8,9},{9,8},{10,11... | collective-permute-start | bytes 983048 | tf_op jit(solution)/shard_map/ppermute | solution.py:318
  34.1 2.4 %copy-start.3 = (bf16[1040,128]{1,0:T(8,128)(2,1)}, bf16[1040,128]{1,0:T(8,128)(2,1)S(1)}, u32[]{:S(2)}) copy-start(bf16[1040,128]{1,0:T(8,128)(2,1)S(1)} %collective-permute-done.6) | copy-start | bytes 798724
  34.1 1.3 %copy-start.8 = (bf16[80,2048]{1,0:T(8,128)(2,1)}, bf16[80,2048]{1,0:T(8,128)(2,1)S(1)}, u32[]{:S(2)}) copy-start(bf16[80,2048]{1,0:T(8,128)(2,1)S(1)} %collective-permute-done.10.refs_8_) | copy-start | bytes 983044
  34.1 1.3 %copy-start.9 = (bf16[80,2048]{1,0:T(8,128)(2,1)}, bf16[80,2048]{1,0:T(8,128)(2,1)S(1)}, u32[]{:S(2)}) copy-start(bf16[80,2048]{1,0:T(8,128)(2,1)S(1)} %collective-permute-done.11.refs_9_) | copy-start | bytes 983044
  34.1 24.3 %collective-permute-start.12 = (bf16[160,2048]{1,0:T(8,128)(2,1)}, bf16[160,2048]{1,0:T(8,128)(2,1)}, u32[]{:S(2)}, u32[]{:S(2)}) collective-permute-start(bf16[160,2048]{1,0:T(8,128)(2,1)} %fusion.1), channel_id=1, source_target_pairs={{8,0},{9,1},{10,2},{11,3},{12,4},{13,5},{14,6},{15,7},{16,8},{17,9... | collective-permute-start | bytes 1966088 | tf_op jit(solution)/shard_map/ppermute | solution.py:358
  58.4 3.0 %collective-permute-start.13 = (bf16[160,2048]{1,0:T(8,128)(2,1)}, bf16[160,2048]{1,0:T(8,128)(2,1)S(1)}, u32[]{:S(2)}, u32[]{:S(2)}) collective-permute-start(bf16[160,2048]{1,0:T(8,128)(2,1)} %collective-permute-done.12.refs_0_), channel_id=1, source_target_pairs={{0,1},{1,0},{2,3},{3,2},{4,5},{5,4},{6,7},{7,6},{8,9},{9,8},{10,11... | collective-permute-start | bytes 1966088 | tf_op jit(solution)/shard_map/ppermute | solution.py:318
  61.4 0.9 copy-start.7
  81.3 32.4 %collective-permute-start.15 = (f32[320,128]{1,0:T(8,128)}, f32[320,128]{1,0:T(8,128)S(1)}, u32[]{:S(2)}, u32[]{:S(2)}) collective-permute-start(f32[320,128]{1,0:T(8,128)} %shard_map.49), channel_id=1, source_target_pairs={{0,16},{1,17},{2,18},{3,19},{4,20},{5,21},{6,22},{7,23},{8,24},{9,... | collective-permute-start | bytes 491528 | tf_op jit(solution)/shard_map/ppermute | solution.py:318
  101.9 11.8 %collective-permute-start.14 = (f32[320,128]{1,0:T(8,128)}, f32[320,128]{1,0:T(8,128)S(1)}, u32[]{:S(2)}, u32[]{:S(2)}) collective-permute-start(f32[320,128]{1,0:T(8,128)} %get-tuple-element.40), channel_id=1, source_target_pairs={{0,24},{1,25},{2,26},{3,27},{4,28},{5,29},{6,30},{7,31},{8,16},{9,... | collective-permute-start | bytes 491528 | tf_op jit(solution)/shard_map/ppermute | solution.py:318
  103.4 10.2 %collective-permute-start.16 = (f32[320,128]{1,0:T(8,128)}, f32[320,128]{1,0:T(8,128)S(1)}, u32[]{:S(2)}, u32[]{:S(2)}) collective-permute-start(f32[320,128]{1,0:T(8,128)} %get-tuple-element.42), channel_id=1, source_target_pairs={{0,8},{1,9},{2,10},{3,11},{4,12},{5,13},{6,14},{7,15},{8,0},{9,1},... | collective-permute-start | bytes 491528 | tf_op jit(solution)/shard_map/ppermute | solution.py:318
